TPU v7x, 32 devices: a whole 2x2x4 slice. The times are simulated.
32 devices in a mesh: vol: 2 (over x), row: 16 (over z, y, core).
Axes of the slice: x: 2, y: 2, z: 4, core: 2. Of those that a mesh axis runs over, the one named last changes fastest.
Arguments:
- volume: float32 [6, 2048, 2048], P('vol', 'row'), parts along dimension 0, may hold values from 0.25 to 2
- psf_spectra: bfloat16 [2, 3, 2048, 2048], P(None, None, 'row'), may hold values from -3.5 to 3.5
- background: float32 [2048, 2048], P('row'), may hold values from 1 to 4
- measured: float32 [4096, 2048], P(('vol', 'row')), parts along dimension 0, may hold values from 0.5 to 4
Outputs:
- new_volume: float32 [6, 2048, 2048], P('vol', 'row'), parts along dimension 0
- projection: float32 [4096, 2048], P(('vol', 'row')), parts along dimension 0
There are 2 independent parts, one for each index of `vol`. A program takes and returns all parts, laid end to end along the dimension named above; an argument that names none is the same for every part. Nothing has to cross between parts.
All inputs are finite; a program needn't handle non-finite values.
Results may differ from a plain program's by a relative error of at most 0.0003.
Values sent between devices are 32-bit elements; how exact they have to be, the bound alone decides.
No kernel may reach another device: no remote copies, remote signals or barrier semaphores. Data moves between devices by JAX's collectives and lax.ppermute only.
A program may use at most 128 MiB of HBM per device.

v0:
```python
import math

import jax
import jax.numpy as jnp
from jax import lax
from jax.sharding import PartitionSpec as P

FLOOR = 0.5
HIGHEST = lax.Precision.HIGHEST


def phase_pair(first_extent, second_extent, modulus, direction):
    first_idx = jnp.arange(first_extent, dtype=jnp.int32)
    second_idx = jnp.arange(second_extent, dtype=jnp.int32)
    phases = first_idx[:, None] * second_idx[None, :] % modulus
    angles = phases.astype(jnp.float32) * (2.0 * math.pi / modulus)
    return (jnp.cos(angles), direction * jnp.sin(angles))


def contract(pattern, fields, coeffs, real_only):
    real_part, imag_part = fields
    coeff_real, coeff_imag = coeffs

    def product(operand, table_side):
        return jnp.einsum(pattern, operand, table_side, precision=HIGHEST)

    if imag_part is None:
        return (product(real_part, coeff_real), product(real_part, coeff_imag))
    out_real = product(real_part, coeff_real) - product(imag_part, coeff_imag)
    if real_only:
        return (out_real, None)
    return (out_real, product(real_part, coeff_imag) + product(imag_part, coeff_real))


def rotate(fields, factors):
    real_part, imag_part = fields
    factor_real, factor_imag = factors
    return (
        real_part * factor_real - imag_part * factor_imag,
        real_part * factor_imag + imag_part * factor_real,
    )


def leading_pass(fields, groups, direction):
    batch_size, row_count, length = fields[0].shape
    inner_count = length // groups
    shaped = tuple(
        (
            None if member is None else member.reshape(batch_size, row_count, inner_count, groups)
            for member in fields
        )
    )
    sectioned = contract(
        "bqnm,nk->bqkm", shaped, phase_pair(inner_count, inner_count, inner_count, direction), False
    )
    sectioned = rotate(sectioned, phase_pair(inner_count, groups, length, direction))
    sectioned = contract(
        "bqkm,mp->bpkq", sectioned, phase_pair(groups, groups, groups, direction), False
    )
    return tuple(
        (member.reshape(batch_size, groups, inner_count * row_count) for member in sectioned)
    )


def trailing_pass(fields, row_count, direction, real_only):
    batch_size, groups, merged = fields[0].shape
    inner_count = merged // row_count
    length = groups * row_count
    shaped = tuple(
        (member.reshape(batch_size, groups, inner_count, row_count) for member in fields)
    )
    sectioned = contract(
        "bskq,st->bktq", shaped, phase_pair(groups, groups, groups, direction), False
    )
    sectioned = rotate(sectioned, phase_pair(groups, row_count, length, direction))
    sectioned = contract(
        "bktq,qu->bkut",
        sectioned,
        phase_pair(row_count, row_count, row_count, direction),
        real_only,
    )
    return tuple(
        (
            None if member is None else member.reshape(batch_size, inner_count, length)
            for member in sectioned
        )
    )


def shards(volume, psf_spectra, background, measured):
    groups = lax.axis_size("row")
    row_count = volume.shape[1]
    length = volume.shape[2]
    inverse_scale = 1.0 / (length * length)
    response_real = psf_spectra[0].astype(jnp.float32)
    response_imag = psf_spectra[1].astype(jnp.float32)

    def inverse_rows(halves):
        return trailing_pass(halves, row_count, 1.0, True)[0]

    outgoing = leading_pass((volume, None), groups, -1.0)
    spec_real, spec_imag = trailing_pass(
        (
            lax.all_to_all(outgoing[0], "row", split_axis=1, concat_axis=1, tiled=True),
            lax.all_to_all(outgoing[1], "row", split_axis=1, concat_axis=1, tiled=True),
        ),
        row_count,
        -1.0,
        False,
    )
    prod_real = spec_real * response_real - spec_imag * response_imag
    prod_imag = spec_real * response_imag + spec_imag * response_real
    summed_spec = (
        jnp.sum(prod_real, axis=0, keepdims=True),
        jnp.sum(prod_imag, axis=0, keepdims=True),
    )
    outgoing = leading_pass(summed_spec, groups, 1.0)
    arrived = lax.all_to_all(outgoing, "row", split_axis=1, concat_axis=1, tiled=True)
    projection = inverse_rows(arrived)[0] * inverse_scale
    quotient = measured / jnp.maximum(projection + background, FLOOR)
    outgoing = leading_pass((quotient[None], None), groups, -1.0)
    arrived = lax.all_to_all(outgoing, "row", split_axis=1, concat_axis=1, tiled=True)
    ratio_real, ratio_imag = trailing_pass(arrived, row_count, -1.0, False)
    corr_real = ratio_real * response_real + ratio_imag * response_imag
    corr_imag = ratio_imag * response_real - ratio_real * response_imag
    outgoing = leading_pass((corr_real, corr_imag), groups, 1.0)
    correction = (
        inverse_rows(
            (
                lax.all_to_all(outgoing[0], "row", split_axis=1, concat_axis=1, tiled=True),
                lax.all_to_all(outgoing[1], "row", split_axis=1, concat_axis=1, tiled=True),
            )
        )
        * inverse_scale
    )
    return (volume * correction, projection)


def solution(mesh):
    in_specs = (
        P("vol", "row", None),
        P(None, None, "row", None),
        P("row", None),
        P(("vol", "row"), None),
    )
    out_specs = (P("vol", "row", None), P(("vol", "row"), None))
    return jax.shard_map(shards, mesh=mesh, in_specs=in_specs, out_specs=out_specs, check_vma=False)
```

profile of v0, /device:TPU:15, one launch (start us, length us, event | category | flops | bytes accessed | tf_op | source)
XLA Modules:
  0.0 714.2 jit_solution(3518631060980232818)
XLA Ops:
  5.8 5.0 fusion.103
  10.8 6.0 add_bitcast_fusion.5
  19.5 3.8 copy.122
  26.3 4.7 add_bitcast_fusion.4
  34.5 5.9 reshape.307
  40.4 7.2 %all-to-all-start.1 = ((f32[3,16,16384]{2,0,1:T(4,128)}), f32[3,16,16384]{2,0,1:T(4,128)}, u32[]{:S(2)}, u32[]{:S(2)}) async-start(f32[3,16,16384]{2,0,1:T(4,128)} %reshape.307), calls=%async_computation.1 | async-start | bytes 8388608 | tf_op jit(solution)/shard_map/all_to_all | solution.py:105
  50.6 4.6 subtract_bitcast_fusion.4
  60.8 79.2 %all-to-all-done.1 = f32[3,16,16384]{2,0,1:T(4,128)} async-done(((f32[3,16,16384]{2,0,1:T(4,128)}), f32[3,16,16384]{2,0,1:T(4,128)}, u32[]{:S(2)}, u32[]{:S(2)}) %all-to-all-start.1) | async-done | bytes 3145760 | tf_op jit(solution)/shard_map/all_to_all | solution.py:105
  139.9 5.1 all-to-all-start
  155.6 5.0 reshape.308
  160.5 5.9 fusion.18
  166.4 5.9 fusion.16
  172.3 65.0 %all-to-all-done = f32[3,16,16384]{2,0,1:T(4,128)} async-done(((f32[3,16,16384]{2,0,1:T(4,128)}), f32[3,16,16384]{2,0,1:T(4,128)}, u32[]{:S(2)}, u32[]{:S(2)}) %all-to-all-start) | async-done | bytes 3145760 | tf_op jit(solution)/shard_map/all_to_all | solution.py:104
  237.3 5.4 reshape.306
  242.7 6.5 fusion.32
  249.2 5.1 subtract_bitcast_fusion.3
  254.3 3.9 fusion.26
  258.3 3.9 fusion.24
  262.2 4.0 fusion.44
  266.2 9.3 %fusion.3 = (f32[128,128,16]{0,1,2:T(8,128)S(1)}, f32[128,128,16]{0,1,2:T(8,128)S(1)}) fusion(f32[128,3,128,16]{2,0,3,1:T(8,128)S(1)} %fusion.44, f32[3,128,128,16]{1,3,2,0:T(8,128)S(1)} %copy-done.14, f32[3,128,128,16]{1,3,2,0:T(8,128)S(1)} %copy-done.15, f32[128,3,128,16]{2,0,3,1:T(8,128)S(1)} %fusion.24, f32[3,128,16,128]{3,2,1,0:T(8,128)S(1)} %get-tuple-element.12), kind=kOutput, calls=%fused_computation.6 | convolution fusion | flops 1214758912 | bytes 17825792 | tf_op jit(solution)/shard_map/bktq,qu->bkut/dot_general | solution.py:25
  285.7 4.8 all-to-all-start.2
  294.0 21.3 %all-to-all-done.2 = f32[1,16,16384]{2,0,1:T(1,128)S(1)} async-done(((f32[1,16,16384]{2,0,1:T(1,128)}), f32[1,16,16384]{2,0,1:T(1,128)S(1)}, u32[]{:S(2)}, u32[]{:S(2)}) %all-to-all-start.2) | async-done | bytes 1048608 | tf_op jit(solution)/shard_map/all_to_all | solution.py:118
  315.3 5.0 all-to-all-start.3
  328.2 16.8 %all-to-all-done.3 = f32[1,16,16384]{2,0,1:T(1,128)S(1)} async-done(((f32[1,16,16384]{2,0,1:T(1,128)}), f32[1,16,16384]{2,0,1:T(1,128)S(1)}, u32[]{:S(2)}, u32[]{:S(2)}) %all-to-all-start.3) | async-done | bytes 1048608 | tf_op jit(solution)/shard_map/all_to_all | solution.py:118
  365.7 4.8 all-to-all-start.4
  374.0 21.4 %all-to-all-done.4 = f32[1,16,16384]{2,0,1:T(1,128)S(1)} async-done(((f32[1,16,16384]{2,0,1:T(1,128)}), f32[1,16,16384]{2,0,1:T(1,128)S(1)}, u32[]{:S(2)}, u32[]{:S(2)}) %all-to-all-start.4) | async-done | bytes 1048608 | tf_op jit(solution)/shard_map/all_to_all | solution.py:122
  395.4 5.2 all-to-all-start.5
  404.6 20.5 %all-to-all-done.5 = f32[1,16,16384]{2,0,1:T(1,128)S(1)} async-done(((f32[1,16,16384]{2,0,1:T(1,128)}), f32[1,16,16384]{2,0,1:T(1,128)S(1)}, u32[]{:S(2)}, u32[]{:S(2)}) %all-to-all-start.5) | async-done | bytes 1048608 | tf_op jit(solution)/shard_map/all_to_all | solution.py:122
  442.6 4.7 fusion.91
  447.3 4.6 fusion.114
  454.6 5.3 convolution_add_fusion
  459.9 6.4 add_bitcast_fusion.2
  475.4 4.7 add_bitcast_fusion.1
  480.1 3.9 copy.227
  484.0 5.9 reshape.311
  489.9 4.8 all-to-all-start.7
  497.7 4.6 subtract_bitcast_fusion.1
  507.9 79.4 %all-to-all-done.7 = f32[3,16,16384]{2,0,1:T(4,128)} async-done(((f32[3,16,16384]{2,0,1:T(4,128)}), f32[3,16,16384]{2,0,1:T(4,128)}, u32[]{:S(2)}, u32[]{:S(2)}) %all-to-all-start.7) | async-done | bytes 3145760 | tf_op jit(solution)/shard_map/all_to_all | solution.py:131
  587.2 5.1 all-to-all-start.6
  593.7 5.0 reshape.312
  598.6 5.9 fusion.10
  604.5 5.9 fusion.8
  610.3 74.3 %all-to-all-done.6 = f32[3,16,16384]{2,0,1:T(4,128)} async-done(((f32[3,16,16384]{2,0,1:T(4,128)}), f32[3,16,16384]{2,0,1:T(4,128)}, u32[]{:S(2)}, u32[]{:S(2)}) %all-to-all-start.6) | async-done | bytes 3145760 | tf_op jit(solution)/shard_map/all_to_all | solution.py:130
  684.6 5.2 reshape.310
  689.8 6.3 fusion.38
  696.1 4.9 subtract_bitcast_fusion
  701.0 4.1 fusion.4
  705.1 4.1 multiply_bitcast_fusion
  (115 shorter events, 126.3 us)
Async XLA Ops:
  3.1 2.7 copy-start
  5.8 5.0 copy-start.2
  23.3 2.9 copy-start.3
  40.4 99.5 %all-to-all-start.1 = ((f32[3,16,16384]{2,0,1:T(4,128)}), f32[3,16,16384]{2,0,1:T(4,128)}, u32[]{:S(2)}, u32[]{:S(2)}) async-start(f32[3,16,16384]{2,0,1:T(4,128)} %reshape.307), calls=%async_computation.1 | async-start | bytes 8388608 | tf_op jit(solution)/shard_map/all_to_all | solution.py:105
  47.6 2.9 copy-start.4
  139.9 97.4 %all-to-all-start = ((f32[3,16,16384]{2,0,1:T(4,128)}), f32[3,16,16384]{2,0,1:T(4,128)}, u32[]{:S(2)}, u32[]{:S(2)}) async-start(f32[3,16,16384]{2,0,1:T(4,128)} %reshape.305), calls=%async_computation | async-start | bytes 8388608 | tf_op jit(solution)/shard_map/all_to_all | solution.py:104
  149.3 4.0 copy-start.7
  153.3 2.2 copy-start.9
  242.7 6.5 copy-start.12
  262.2 4.0 copy-start.14
  262.2 4.0 copy-start.15
  285.7 29.6 %all-to-all-start.2 = ((f32[1,16,16384]{2,0,1:T(1,128)}), f32[1,16,16384]{2,0,1:T(1,128)S(1)}, u32[]{:S(2)}, u32[]{:S(2)}) async-start(f32[1,16,16384]{2,0,1:T(1,128)} %bitcast.372), calls=%async_computation.2 | async-start | bytes 2097152 | tf_op jit(solution)/shard_map/all_to_all | solution.py:118
  294.0 28.8 %copy-start.20 = (f32[128,2048]{1,0:T(8,128)S(1)}, f32[128,2048]{1,0:T(8,128)}, u32[]{:S(2)}) copy-start(f32[128,2048]{1,0:T(8,128)} %param.7) | copy-start | bytes 3145732
  315.3 29.7 %all-to-all-start.3 = ((f32[1,16,16384]{2,0,1:T(1,128)}), f32[1,16,16384]{2,0,1:T(1,128)S(1)}, u32[]{:S(2)}, u32[]{:S(2)}) async-start(f32[1,16,16384]{2,0,1:T(1,128)} %bitcast.370), calls=%async_computation.3 | async-start | bytes 2097152 | tf_op jit(solution)/shard_map/all_to_all | solution.py:118
  350.9 3.1 copy-start.18
  350.9 3.1 copy-start.19
  353.0 1.0 copy-start.16
  365.7 29.7 %all-to-all-start.4 = ((f32[1,16,16384]{2,0,1:T(1,128)}), f32[1,16,16384]{2,0,1:T(1,128)S(1)}, u32[]{:S(2)}, u32[]{:S(2)}) async-start(f32[1,16,16384]{2,0,1:T(1,128)} %bitcast.373), calls=%async_computation.4 | async-start | bytes 2097152 | tf_op jit(solution)/shard_map/all_to_all | solution.py:122
  395.4 29.7 %all-to-all-start.5 = ((f32[1,16,16384]{2,0,1:T(1,128)}), f32[1,16,16384]{2,0,1:T(1,128)S(1)}, u32[]{:S(2)}, u32[]{:S(2)}) async-start(f32[1,16,16384]{2,0,1:T(1,128)} %bitcast.371), calls=%async_computation.5 | async-start | bytes 2097152 | tf_op jit(solution)/shard_map/all_to_all | solution.py:122
  434.5 2.3 copy-start.8
  434.5 2.3 copy-start.10
  454.6 5.3 copy-start.13
  472.5 2.9 copy-start.5
  489.9 97.3 %all-to-all-start.7 = ((f32[3,16,16384]{2,0,1:T(4,128)}), f32[3,16,16384]{2,0,1:T(4,128)}, u32[]{:S(2)}, u32[]{:S(2)}) async-start(f32[3,16,16384]{2,0,1:T(4,128)} %reshape.311), calls=%async_computation.7 | async-start | bytes 8388608 | tf_op jit(solution)/shard_map/all_to_all | solution.py:131
  494.8 2.9 copy-start.6
  507.8 84.5 %copy-start.17 = (f32[1,128,128,16]{1,3,2,0:T(8,128)S(1)}, f32[1,128,128,16]{1,3,2,0:T(8,128)}, u32[]{:S(2)}) copy-start(f32[1,128,128,16]{1,3,2,0:T(8,128)} %copy-done.16) | copy-start | bytes 3145732
  587.2 97.4 %all-to-all-start.6 = ((f32[3,16,16384]{2,0,1:T(4,128)}), f32[3,16,16384]{2,0,1:T(4,128)}, u32[]{:S(2)}, u32[]{:S(2)}) async-start(f32[3,16,16384]{2,0,1:T(4,128)} %reshape.309), calls=%async_computation.6 | async-start | bytes 8388608 | tf_op jit(solution)/shard_map/all_to_all | solution.py:130
  689.8 6.3 copy-start.11
  709.2 1.9 copy-start.1
where the time goes:
time: 721 us; the launch traced here: 714 us
  waiting for transfers between devices  378 us (52%)
  matrix products  183 us (25%)
  local copies, waits for them, and re-layouts  101 us (14%)
  starting transfers between devices  42 us (6%)
  other arithmetic  8.39 us (1%)
    dot_general x56, matrix products, product(): return jnp.einsum(pattern, operand, table_side, precision=HIGHEST)  183 us
    all_to_all x2, waiting for transfers between devices, shards(): lax.all_to_all(outgoing[1], 'row', split_axis=1, concat_axis=1, tiled=True)  159 us
    all_to_all x2, waiting for transfers between devices, shards(): lax.all_to_all(outgoing[0], 'row', split_axis=1, concat_axis=1, tiled=True)  139 us
    all_to_all x4, waiting for transfers between devices, shards(): lax.all_to_all(outgoing, 'row', split_axis=1, concat_axis=1, tiled=True)  79.9 us
    reshape x8, local copies, waits for them, and re-layouts, leading_pass(): member.reshape(batch_size, groups, inner_count * row_count)  30.4 us
    reshape x4, local copies, waits for them, and re-layouts, trailing_pass(): member.reshape(batch_size, groups, inner_count, row_count)  20.5 us
    all_to_all x4, starting transfers between devices, shards(): lax.all_to_all(outgoing, 'row', split_axis=1, concat_axis=1, tiled=True)  19.8 us
  transfers between devices with their start and end apart: 8, of which 8 were waited for; matrix products, arithmetic and copies ran while one was open for 13% of the time, Pallas kernels for 0%

commit v1 on v0

v1 whole, which is shorter than its diff:
```python
import math

import jax
import jax.numpy as jnp
import numpy as np
from jax import lax
from jax.experimental import pallas as pl
from jax.experimental.pallas import tpu as pltpu
from jax.sharding import PartitionSpec as P

FLOOR = 0.5
HIGHEST = lax.Precision.HIGHEST
LANES = 128
SUB = 8


def phase_pair(first_extent, second_extent, modulus, direction):
    first_idx = jnp.arange(first_extent, dtype=jnp.int32)
    second_idx = jnp.arange(second_extent, dtype=jnp.int32)
    phases = first_idx[:, None] * second_idx[None, :] % modulus
    angles = phases.astype(jnp.float32) * (2.0 * math.pi / modulus)
    return (jnp.cos(angles), direction * jnp.sin(angles))


def contract(pattern, fields, coeffs, real_only):
    real_part, imag_part = fields
    coeff_real, coeff_imag = coeffs

    def product(operand, table_side):
        return jnp.einsum(pattern, operand, table_side, precision=HIGHEST)

    if imag_part is None:
        return (product(real_part, coeff_real), product(real_part, coeff_imag))
    out_real = product(real_part, coeff_real) - product(imag_part, coeff_imag)
    if real_only:
        return (out_real, None)
    return (out_real, product(real_part, coeff_imag) + product(imag_part, coeff_real))


def rotate(fields, factors):
    real_part, imag_part = fields
    factor_real, factor_imag = factors
    return (
        real_part * factor_real - imag_part * factor_imag,
        real_part * factor_imag + imag_part * factor_real,
    )


def leading_pass(fields, groups, direction):
    batch_size, row_count, length = fields[0].shape
    inner_count = length // groups
    shaped = tuple(
        None if member is None else member.reshape(batch_size, row_count, inner_count, groups)
        for member in fields
    )
    sectioned = contract(
        "bqnm,nk->bqkm", shaped, phase_pair(inner_count, inner_count, inner_count, direction), False
    )
    sectioned = rotate(sectioned, phase_pair(inner_count, groups, length, direction))
    sectioned = contract(
        "bqkm,mp->bpkq", sectioned, phase_pair(groups, groups, groups, direction), False
    )
    return tuple(member.reshape(batch_size, groups, inner_count * row_count) for member in sectioned)


def trailing_pass(fields, row_count, direction, real_only):
    batch_size, groups, merged = fields[0].shape
    inner_count = merged // row_count
    length = groups * row_count
    shaped = tuple(member.reshape(batch_size, groups, inner_count, row_count) for member in fields)
    sectioned = contract(
        "bskq,st->bktq", shaped, phase_pair(groups, groups, groups, direction), False
    )
    sectioned = rotate(sectioned, phase_pair(groups, row_count, length, direction))
    sectioned = contract(
        "bktq,qu->bkut", sectioned, phase_pair(row_count, row_count, row_count, direction), real_only
    )
    return tuple(
        None if member is None else member.reshape(batch_size, inner_count, length)
        for member in sectioned
    )


def generic_shards(volume, psf_spectra, background, measured):
    groups = lax.axis_size("row")
    row_count = volume.shape[1]
    length = volume.shape[2]
    inverse_scale = 1.0 / (length * length)
    response_real = psf_spectra[0].astype(jnp.float32)
    response_imag = psf_spectra[1].astype(jnp.float32)

    def swap(field):
        return lax.all_to_all(field, "row", split_axis=1, concat_axis=1, tiled=True)

    outgoing = leading_pass((volume, None), groups, -1.0)
    spec_real, spec_imag = trailing_pass(
        (swap(outgoing[0]), swap(outgoing[1])), row_count, -1.0, False
    )
    prod_real = spec_real * response_real - spec_imag * response_imag
    prod_imag = spec_real * response_imag + spec_imag * response_real
    summed = (jnp.sum(prod_real, axis=0, keepdims=True), jnp.sum(prod_imag, axis=0, keepdims=True))
    outgoing = leading_pass(summed, groups, 1.0)
    arrived = (swap(outgoing[0]), swap(outgoing[1]))
    projection = trailing_pass(arrived, row_count, 1.0, True)[0][0] * inverse_scale
    quotient = measured / jnp.maximum(projection + background, FLOOR)
    outgoing = leading_pass((quotient[None], None), groups, -1.0)
    arrived = (swap(outgoing[0]), swap(outgoing[1]))
    ratio_real, ratio_imag = trailing_pass(arrived, row_count, -1.0, False)
    corr_real = ratio_real * response_real + ratio_imag * response_imag
    corr_imag = ratio_imag * response_real - ratio_real * response_imag
    outgoing = leading_pass((corr_real, corr_imag), groups, 1.0)
    arrived = (swap(outgoing[0]), swap(outgoing[1]))
    correction = trailing_pass(arrived, row_count, 1.0, True)[0] * inverse_scale
    return (volume * correction, projection)


def times(z, angle):
    re, im = z
    c, s = math.cos(angle), math.sin(angle)
    if abs(s) < 1e-12:
        return z if c > 0 else (-re, None if im is None else -im)
    if abs(c) < 1e-12:
        if im is None:
            return (None, re if s > 0 else -re)
        return (-im, re) if s > 0 else (im, -re)
    if im is None:
        return (re * c, re * s)
    if abs(abs(c) - abs(s)) < 1e-12:
        sc, ss = math.copysign(1.0, c), math.copysign(1.0, s)
        a = re if sc > 0 else -re
        b = im if sc > 0 else -im
        r, i = (a - im, b + re) if ss > 0 else (a + im, b - re)
        return (r * abs(c), i * abs(c))
    return (re * c - im * s, re * s + im * c)


def plus(a, b):
    if a is None:
        return b
    return a if b is None else a + b


def minus(a, b):
    if b is None:
        return a
    return -b if a is None else a - b


def cadd(a, b):
    return (plus(a[0], b[0]), plus(a[1], b[1]))


def csub(a, b):
    return (minus(a[0], b[0]), minus(a[1], b[1]))


def conj(a):
    return (a[0], None if a[1] is None else -a[1])


def cfft(xs, sign):
    n = len(xs)
    if n == 1:
        return list(xs)
    even, odd = cfft(xs[0::2], sign), cfft(xs[1::2], sign)
    turned = [times(odd[t], sign * 2.0 * math.pi * t / n) for t in range(n // 2)]
    return [cadd(even[t], turned[t]) for t in range(n // 2)] + [
        csub(even[t], turned[t]) for t in range(n // 2)
    ]


def rfft(xs):
    n = len(xs)
    if n == 2:
        return [(xs[0] + xs[1], None), (xs[0] - xs[1], None)]
    even, odd = rfft(xs[0::2]), rfft(xs[1::2])
    out = [None] * (n // 2 + 1)
    for t in range(n // 4 + 1):
        turned = times(odd[t], -2.0 * math.pi * t / n)
        out[t] = cadd(even[t], turned)
        if t < n // 4:
            out[n // 2 - t] = conj(csub(even[t], turned))
    return out


def c2r(zs):
    n = 2 * (len(zs) - 1)
    if n == 2:
        return [zs[0][0] + zs[1][0], zs[0][0] - zs[1][0]]
    q = n // 4
    even, odd = [], []
    for t in range(q):
        mirror = conj(zs[n // 2 - t])
        even.append(cadd(zs[t], mirror))
        odd.append(times(csub(zs[t], mirror), 2.0 * math.pi * t / n))
    even.append((zs[q][0] * 2.0, None))
    odd.append((zs[q][1] * -2.0, None))
    a, b = c2r(even), c2r(odd)
    return [half[i] for i in range(n // 2) for half in (a, b)]


def split_table(table):
    high = table.astype(jnp.bfloat16)
    low = (table - high.astype(np.float64)).astype(jnp.bfloat16)
    return np.stack([high, low])


def make_tables(groups, lanes):
    length = groups * lanes
    per = lanes // groups
    pos = np.arange(lanes)
    w_y = np.zeros((groups, 2, SUB, 2, lanes))
    w_0 = np.zeros((groups, 2, SUB, 2, lanes))
    half = SUB // 2
    for p in range(groups):
        for r in range(SUB):
            ang = 2.0 * np.pi * ((per * p + r) * pos % lanes) / lanes
            w_y[p, 0, r] = np.cos(ang), np.sin(ang)
            w_y[p, 1, r] = -np.sin(ang), np.cos(ang)
            if r < half:
                unit = per * p + r
                if r == 0 and p >= groups // 2:
                    unit = per * p + per // 2
                ang = 2.0 * np.pi * (groups * unit * pos % length) / length
                w_0[p, 0, r, 0] = np.cos(ang)
                w_0[p, 1, r, 0] = -np.sin(ang)
                if r == 0 and p == 0:
                    w_0[p, 1, r, 0] = (-1.0) ** pos
            else:
                ang = (groups * (per * p + r - half) + groups // 2) * pos % length
                ang = 2.0 * np.pi * ang / length
                w_0[p, 0, r, 1] = np.cos(ang)
                w_0[p, 1, r, 1] = -np.sin(ang)
    rows = groups * 2 * SUB
    ang = 2.0 * np.pi * (pos[:, None] * pos[None, :] % lanes) / lanes
    w_x = np.block([[np.cos(ang), -np.sin(ang)], [np.sin(ang), np.cos(ang)]])
    ang = 2.0 * np.pi * (np.arange(groups)[:, None] * pos[None, :] % length) / length
    turn = np.stack([np.cos(ang), -np.sin(ang)], axis=1).astype(np.float32)
    return (
        split_table(w_y.reshape(rows, 2 * lanes)),
        split_table(w_0.reshape(rows, 2 * lanes)),
        split_table(w_x),
        split_table(w_x.T),
        turn,
    )


def kept_rows(groups, lanes):
    per = lanes // groups
    half = SUB // 2
    own = [groups * w for w in range(half)] + [groups * w + groups // 2 for w in range(half)]
    for tile in range(1, groups // 2):
        own += [groups * w + tile for w in range(per)]
    return own


NN = (((1,), (0,)), ((), ()))
NT = (((1,), (1,)), ((), ()))


def halves(x):
    high = x.astype(jnp.bfloat16)
    return high, (x - high.astype(jnp.float32)).astype(jnp.bfloat16)


def mm(a, b, dims):
    return lax.dot_general(a, b, dims, preferred_element_type=jnp.float32)


def data_table(x, table):
    high, low = halves(x)
    return mm(high, table[0], NN) + (mm(low, table[0], NN) + mm(high, table[1], NN))


def table_data(table, x):
    high, low = halves(x)
    return mm(table[0], high, NT) + (mm(table[0], low, NT) + mm(table[1], high, NT))


def y_forward(read, emit, z, w_y, w_0, turn, groups, rows, lanes):
    def chunk(i, carry):
        out = rfft([read(i, a) for a in range(groups)])
        here = pl.ds(pl.multiple_of(i * SUB, SUB), SUB)
        z[0, here, :lanes] = out[0][0]
        z[0, here, lanes:] = out[groups // 2][0]
        for t in range(1, groups // 2):
            re, im = out[t]
            c, s = turn[t, 0:1, :], turn[t, 1:2, :]
            z[t, here, :lanes] = re * c - im * s
            z[t, here, lanes:] = re * s + im * c
        return carry

    lax.fori_loop(0, rows // SUB, chunk, 0)
    for t in range(groups // 2):
        emit(t, table_data(w_0 if t == 0 else w_y, z[t]))


def y_inverse(fetch, write, z, w_y, w_0, turn, groups, rows, lanes):
    for t in range(groups // 2):
        z[t] = data_table(fetch(t).T, w_0 if t == 0 else w_y)

    def chunk(i, carry):
        here = pl.ds(pl.multiple_of(i * SUB, SUB), SUB)
        zs = [(z[0, here, :lanes] * 2.0, None)]
        for t in range(1, groups // 2):
            re, im = z[t, here, :lanes], z[t, here, lanes:]
            c, s = turn[t, 0:1, :], turn[t, 1:2, :]
            zs.append((re * c + im * s, im * c - re * s))
        zs.append((z[0, here, lanes:] * 2.0, None))
        write(i, here, c2r(zs))
        return carry

    lax.fori_loop(0, rows // SUB, chunk, 0)


def x_radix(tile, z, base, turn, groups, lanes, step):
    for t, (re, im) in enumerate(cfft(tile, -1.0)):
        here = pl.ds(pl.multiple_of(base + t * step, SUB), SUB)
        if t == 0:
            z[here, :lanes] = re
            z[here, lanes:] = im
        else:
            c, s = turn[t, 0:1, :], turn[t, 1:2, :]
            z[here, :lanes] = re * c - im * s
            z[here, lanes:] = re * s + im * c


def x_unradix(z, base, turn, groups, lanes, step):
    zs = []
    for t in range(groups):
        here = pl.ds(pl.multiple_of(base + t * step, SUB), SUB)
        re, im = z[here, :lanes], z[here, lanes:]
        if t:
            c, s = turn[t, 0:1, :], turn[t, 1:2, :]
            re, im = re * c + im * s, im * c - re * s
        zs.append((re, im))
    return cfft(zs, 1.0)


def fast_shards(volume, psf_spectra, background, measured):
    groups = lax.axis_size("row")
    parts = lax.axis_size("vol")
    depth, rows, length = volume.shape
    lanes = LANES
    tiles = groups // 2
    kept = tiles * SUB
    pair = 2 * SUB
    f32 = jnp.float32
    place = lax.axis_index("row")
    part = lax.axis_index("vol")
    w_y, w_0, w_x, w_xi, turn = (jnp.asarray(t) for t in make_tables(groups, lanes))
    own_rows = kept_rows(groups, rows)

    whole = lambda *shape: pl.BlockSpec(shape, lambda *_: (0,) * len(shape))
    y_specs = [whole(*w_y.shape), whole(*w_0.shape), whole(*turn.shape)]
    x_specs = [whole(*w_x.shape), whole(*w_xi.shape), whole(*turn.shape)]
    y_scratch = pltpu.VMEM((tiles, rows, 2 * lanes), f32)
    send_shape = (groups, tiles, 2, SUB, lanes)

    def many(n):
        return (groups, n, tiles, 2, SUB, lanes)

    low = place < groups // 2
    mid = rows // 2
    pick_send = np.zeros((kept, rows), np.float32)
    pick_own = np.zeros((kept, rows), np.float32)
    for r, k in enumerate(own_rows):
        pick_send[r, (rows - k) if k else mid] = 1.0
        pick_own[r, k] = 1.0
    pick_high = pick_own.copy()
    pick_high[0] = 0.0
    pick_high[0, mid] = 1.0

    def pick_kernel(where_ref, sel_ref, own_l_ref, own_h_ref, psf_ref, send_ref, own_ref):
        sel = jnp.where(where_ref[0] == 1, own_l_ref[...], own_h_ref[...])
        for c in range(2):
            own_ref[c, 0] = mm(sel, psf_ref[c, 0], NN)

        @pl.when(where_ref[1] == 0)
        def _():
            send_ref[0] = mm(sel_ref[...], psf_ref[0, 0], NN)

        @pl.when(where_ref[1] != 0)
        def _():
            send_ref[0] = mm(sel_ref[...], psf_ref[1, 0], NN)

    flags = jnp.stack([low.astype(jnp.int32), part.astype(jnp.int32), (place == 0).astype(jnp.int32)])
    smem = pl.BlockSpec(memory_space=pltpu.SMEM)
    bf = jnp.bfloat16
    send, own = pl.pallas_call(
        pick_kernel,
        grid=(depth,),
        in_specs=[smem, whole(kept, rows), whole(kept, rows), whole(kept, rows),
                  pl.BlockSpec((2, 1, rows, length), lambda d: (0, d, 0, 0))],
        out_specs=[pl.BlockSpec((1, kept, length), lambda d: (d, 0, 0)),
                   pl.BlockSpec((2, 1, kept, length), lambda d: (0, d, 0, 0))],
        out_shape=[jax.ShapeDtypeStruct((depth, kept, length), f32),
                   jax.ShapeDtypeStruct((2, depth, kept, length), f32)],
        name="pick",
    )(flags, jnp.asarray(pick_send, bf), jnp.asarray(pick_own, bf), jnp.asarray(pick_high, bf), psf_spectra)
    flip = [(p, groups - 1 - p) for p in range(groups)]
    mine = lax.ppermute(send, "row", flip)
    other = lax.ppermute(mine, "vol", [(0, 1), (1, 0)])
    edge = psf_spectra[:, :, 0, :].astype(f32).reshape(2 * depth, length)
    edge = jnp.pad(edge, ((0, pair - 2 * depth), (0, 0)))
    edge = lax.ppermute(edge, "row", [(groups - p, p) for p in range(1, groups // 2)] + [(groups // 2, 0)])

    scale = 0.5 / (length * length)
    many_t = 2
    width = many_t * lanes

    def mix_kernel(where_ref, own_ref, mine_ref, other_ref, edge_ref, a_ref, b_ref, o_s, p_s, e_s):
        step = pl.program_id(0)

        @pl.when(step == 0)
        def _():
            zero = where_ref[2] == 1
            is_low = where_ref[0] == 1
            first = lax.broadcasted_iota(jnp.int32, (SUB, length), 0) == 0
            for c in range(2):
                for d in range(depth):
                    base = (c * depth + d) * kept
                    mine_here = where_ref[1] == c
                    o_s[base:base + kept, :] = own_ref[c, d].astype(bf)
                    p = jnp.where(mine_here, mine_ref[d], other_ref[d])
                    row = c * depth + d
                    swap = jnp.where(zero, own_ref[c, d, 0:1, :], edge_ref[row:row + 1, :])
                    head = jnp.where(jnp.logical_and(first, is_low), swap, p[:SUB])
                    p_s[base:base + kept, :] = jnp.concatenate([head, p[SUB:]], 0).astype(bf)
            e_s[...] = edge_ref[...].astype(bf)

        freq = lax.broadcasted_iota(jnp.int32, (length, width), 0)
        col = lax.broadcasted_iota(jnp.int32, (length, width), 1)
        target = (col % lanes) * groups + step * many_t + col // lanes
        hot = jnp.where(freq == target, 1.0, 0.0).astype(bf)
        hot_rev = jnp.where(freq == (length - target) % length, 1.0, 0.0).astype(bf)
        plain = mm(o_s[...], hot, NN)
        mirror = mm(p_s[...], hot_rev, NN)
        e_plain = mm(e_s[...], hot, NN)
        e_mirror = mm(e_s[...], hot_rev, NN)
        zero = jnp.where(where_ref[2] == 1, 1.0, 0.0).astype(f32)
        first = lax.broadcasted_iota(jnp.int32, (SUB, width), 0) == 0
        for c in range(2):
            sign = 1.0 if c == 0 else -1.0
            for d in range(depth):
                row = c * depth + d
                base = row * kept
                h = (plain[base:base + kept] + sign * mirror[base:base + kept]) * scale
                e = (e_plain[row:row + 1] + sign * e_mirror[row:row + 1]) * scale
                a0 = h[:SUB] * (1.0 - 0.75 * zero) + (0.25 * zero) * e
                b0 = (h[:SUB] - e) * (0.25 * zero)
                a_ref[c, d, :SUB, :] = jnp.where(first, a0, h[:SUB])
                a_ref[c, d, SUB:, :] = h[SUB:]
                b_ref[c, d, :SUB, :] = jnp.where(first, b0, 0.0)
                b_ref[c, d, SUB:, :] = jnp.zeros((SUB, width), f32)

    planes = 2 * depth * kept
    a_all, b_all = pl.pallas_call(
        mix_kernel,
        grid=(groups // many_t,),
        in_specs=[smem, whole(2, depth, kept, length), whole(depth, kept, length),
                  whole(depth, kept, length), whole(pair, length)],
        out_specs=[pl.BlockSpec((2, depth, kept, width), lambda i: (0, 0, 0, i)),
                   pl.BlockSpec((2, depth, pair, width), lambda i: (0, 0, 0, i))],
        out_shape=[jax.ShapeDtypeStruct((2, depth, kept, length), f32),
                   jax.ShapeDtypeStruct((2, depth, pair, length), f32)],
        scratch_shapes=[pltpu.VMEM((planes, length), bf), pltpu.VMEM((planes, length), bf),
                        pltpu.VMEM((pair, length), bf)],
        name="mix",
    )(flags, own, mine, other, edge)

    def forward_kernel(wy_ref, w0_ref, turn_ref, v_ref, o_ref, z):
        def read(i, a):
            return v_ref[0, pl.ds(pl.multiple_of(i * SUB, SUB), SUB), a * lanes:(a + 1) * lanes]

        def emit(t, out):
            o_ref[:, 0, t] = out.reshape(groups, 2, SUB, rows)

        y_forward(read, emit, z, wy_ref, w0_ref, turn_ref, groups, rows, lanes)

    outgoing = pl.pallas_call(
        forward_kernel,
        grid=(depth,),
        in_specs=y_specs + [pl.BlockSpec((1, rows, length), lambda d: (d, 0, 0))],
        out_specs=pl.BlockSpec((groups, 1, tiles, 2, SUB, lanes), lambda d: (0, d, 0, 0, 0, 0)),
        out_shape=jax.ShapeDtypeStruct(many(depth), f32),
        scratch_shapes=[y_scratch],
        name="forward_y",
    )(w_y, w_0, turn, volume)

    def swap(field):
        return lax.all_to_all(field, "row", split_axis=0, concat_axis=0, tiled=True)

    arrived = swap(outgoing)

    block = groups * pair
    x_scratch = lambda n: pltpu.VMEM((n * block, 2 * lanes), f32)

    def source(s_ref, d, h, flipped=False):
        out = []
        for s in range(groups):
            re, im = s_ref[s, d, h, 0], s_ref[s, d, h, 1]
            out.append((re, -im if flipped else im))
        return out

    def project_kernel(wx_ref, wxi_ref, turn_ref, s_ref, a_ref, b_ref, o_ref, z, t_s, zc):
        def gather(flipped):
            def one(i, carry):
                d, h = i // 2, i % 2
                x_radix(source(s_ref, d, h, flipped), z, d * block + h * SUB, turn_ref, groups, lanes, pair)
                return carry
            lax.fori_loop(0, 2 * depth, one, 0)
            for d in range(depth):
                zc[d * block:(d + 1) * block, :] = data_table(z[d * block:(d + 1) * block, :], wx_ref)

        def multiply(k_ref, fresh):
            for t in range(groups):
                here = slice(t * pair, (t + 1) * pair)
                cols = slice(t * lanes, (t + 1) * lanes)
                re, im = (None, None) if fresh else (t_s[here, :lanes], t_s[here, lanes:])
                for d in range(depth):
                    at = slice(d * block + t * pair, d * block + (t + 1) * pair)
                    zr, zi = zc[at, :lanes], zc[at, lanes:]
                    kr, ki = k_ref[0, d, :, cols], k_ref[1, d, :, cols]
                    re = plus(re, zr * kr - zi * ki)
                    im = plus(im, zr * ki + zi * kr)
                t_s[here, :lanes] = re
                t_s[here, lanes:] = im

        gather(False)
        multiply(a_ref, True)

        @pl.when(pl.program_id(0) == 0)
        def _():
            gather(True)
            multiply(b_ref, False)

        zc[:block, :] = data_table(t_s[...], wxi_ref)

        def back(h, carry):
            for s, (re, im) in enumerate(x_unradix(zc, h * SUB, turn_ref, groups, lanes, pair)):
                o_ref[s, h, 0] = re
                o_ref[s, h, 1] = im
            return carry
        lax.fori_loop(0, 2, back, 0)

    k_specs = [pl.BlockSpec((2, depth, pair, length), lambda j: (0, 0, j, 0)),
               whole(2, depth, pair, length)]
    one_spec = pl.BlockSpec((groups, 2, 2, SUB, lanes), lambda j: (0, j, 0, 0, 0))
    all_spec = pl.BlockSpec((groups, depth, 2, 2, SUB, lanes), lambda j: (0, 0, j, 0, 0, 0))
    outgoing = pl.pallas_call(
        project_kernel,
        grid=(tiles // 2,),
        in_specs=x_specs + [all_spec] + k_specs,
        out_specs=one_spec,
        out_shape=jax.ShapeDtypeStruct(send_shape, f32),
        scratch_shapes=[x_scratch(depth), x_scratch(1), x_scratch(depth)],
        name="project_x",
    )(w_x, w_xi, turn, arrived, a_all, b_all)
    arrived = swap(outgoing)

    def ratio_kernel(wy_ref, w0_ref, turn_ref, g_ref, bg_ref, me_ref, p_ref, o_ref, z, q_s):
        def fetch(t):
            return g_ref[:, t].reshape(groups * 2 * SUB, rows)

        def write(i, here, outs):
            for a, value in enumerate(outs):
                cols = slice(a * lanes, (a + 1) * lanes)
                p_ref[here, cols] = value
                q_s[here, cols] = me_ref[here, cols] / jnp.maximum(value + bg_ref[here, cols], FLOOR)

        y_inverse(fetch, write, z, wy_ref, w0_ref, turn_ref, groups, rows, lanes)

        def read(i, a):
            return q_s[pl.ds(pl.multiple_of(i * SUB, SUB), SUB), a * lanes:(a + 1) * lanes]

        def emit(t, out):
            o_ref[:, t] = out.reshape(groups, 2, SUB, rows)

        y_forward(read, emit, z, wy_ref, w0_ref, turn_ref, groups, rows, lanes)

    projection, outgoing = pl.pallas_call(
        ratio_kernel,
        out_shape=[jax.ShapeDtypeStruct((rows, length), f32), jax.ShapeDtypeStruct(send_shape, f32)],
        scratch_shapes=[y_scratch, pltpu.VMEM((rows, length), f32)],
        name="ratio",
    )(w_y, w_0, turn, arrived, background, measured)
    arrived = swap(outgoing)

    def correct_kernel(wx_ref, wxi_ref, turn_ref, s_ref, a_ref, b_ref, o_ref, z, zq, zc, c_s):
        def gather(flipped, out):
            def one(h, carry):
                tile = []
                for s in range(groups):
                    re, im = s_ref[s, h, 0], s_ref[s, h, 1]
                    tile.append((re, -im if flipped else im))
                x_radix(tile, z, h * SUB, turn_ref, groups, lanes, pair)
                return carry
            lax.fori_loop(0, 2, one, 0)
            out[...] = data_table(z[...], wx_ref)

        def multiply(k_ref, src, fresh):
            for t in range(groups):
                here = slice(t * pair, (t + 1) * pair)
                cols = slice(t * lanes, (t + 1) * lanes)
                zr, zi = src[here, :lanes], src[here, lanes:]
                for d in range(depth):
                    at = slice(d * block + t * pair, d * block + (t + 1) * pair)
                    kr, ki = k_ref[0, d, :, cols], k_ref[1, d, :, cols]
                    re, im = zr * kr + zi * ki, zi * kr - zr * ki
                    if not fresh:
                        re, im = re + c_s[at, :lanes], im + c_s[at, lanes:]
                    c_s[at, :lanes] = re
                    c_s[at, lanes:] = im

        gather(False, zq)
        multiply(a_ref, zq, True)

        @pl.when(pl.program_id(0) == 0)
        def _():
            gather(True, zq)
            multiply(b_ref, zq, False)

        for d in range(depth):
            zc[d * block:(d + 1) * block, :] = data_table(c_s[d * block:(d + 1) * block, :], wxi_ref)

        def back(i, carry):
            d, h = i // 2, i % 2
            out = x_unradix(zc, d * block + h * SUB, turn_ref, groups, lanes, pair)
            for s, (re, im) in enumerate(out):
                o_ref[s, d, h, 0] = re
                o_ref[s, d, h, 1] = im
            return carry
        lax.fori_loop(0, 2 * depth, back, 0)

    outgoing = pl.pallas_call(
        correct_kernel,
        grid=(tiles // 2,),
        in_specs=x_specs + [one_spec] + k_specs,
        out_specs=all_spec,
        out_shape=jax.ShapeDtypeStruct(many(depth), f32),
        scratch_shapes=[x_scratch(1), x_scratch(1), x_scratch(depth), x_scratch(depth)],
        name="correct_x",
    )(w_x, w_xi, turn, arrived, a_all, b_all)
    arrived = swap(outgoing)

    def final_kernel(wy_ref, w0_ref, turn_ref, g_ref, v_ref, o_ref, z):
        def fetch(t):
            return g_ref[:, 0, t].reshape(groups * 2 * SUB, rows)

        def write(i, here, outs):
            for a, value in enumerate(outs):
                cols = slice(a * lanes, (a + 1) * lanes)
                o_ref[0, here, cols] = v_ref[0, here, cols] * value

        y_inverse(fetch, write, z, wy_ref, w0_ref, turn_ref, groups, rows, lanes)

    new_volume = pl.pallas_call(
        final_kernel,
        grid=(depth,),
        in_specs=y_specs + [
            pl.BlockSpec((groups, 1, tiles, 2, SUB, lanes), lambda d: (0, d, 0, 0, 0, 0)),
            pl.BlockSpec((1, rows, length), lambda d: (d, 0, 0))],
        out_specs=pl.BlockSpec((1, rows, length), lambda d: (d, 0, 0)),
        out_shape=jax.ShapeDtypeStruct((depth, rows, length), f32),
        scratch_shapes=[y_scratch],
        name="final_y",
    )(w_y, w_0, turn, arrived, volume)
    return new_volume, projection


def solution(mesh):
    groups, parts = mesh.shape["row"], mesh.shape["vol"]

    def shards(volume, psf_spectra, background, measured):
        rows = volume.shape[1]
        fits = parts == 2 and rows == LANES and rows == SUB * groups
        body = fast_shards if fits else generic_shards
        return body(volume, psf_spectra, background, measured)

    in_specs = (
        P("vol", "row", None),
        P(None, None, "row", None),
        P("row", None),
        P(("vol", "row"), None),
    )
    out_specs = (P("vol", "row", None), P(("vol", "row"), None))
    return jax.shard_map(shards, mesh=mesh, in_specs=in_specs, out_specs=out_specs, check_vma=False)
```

time: 721 us -> 372 us (0.52)
  waiting for transfers between devices: 378 us -> 165 us
  matrix products: 183 us -> 0 us
  blocking collectives: 0 us -> 136 us
  local copies, waits for them, and re-layouts: 101 us -> 2.76 us
  Pallas kernels: 0 us -> 56.1 us
  starting transfers between devices: 42 us -> 9.53 us
  other arithmetic: 8.39 us -> 0.68 us
    all_to_all x8 -> x1, waiting for transfers between devices: 378 us -> 0.01 us  [swap(): return lax.all_to_all(field, 'row', split_axis=0, concat_axis=0, tiled=True)]
    dot_general x56 -> x0, matrix products: 183 us -> none  [product(): return jnp.einsum(pattern, operand, table_side, precision=HIGHEST)]
    ppermute x0 -> x3, waiting for transfers between devices: none -> 165 us  [the longest x1 131 us: fast_shards(): mine = lax.ppermute(send, 'row', flip)]
    all_to_all x0 -> x3, blocking collectives: none -> 136 us  [swap(): return lax.all_to_all(field, 'row', split_axis=0, concat_axis=0, tiled=True)]
    pallas_call x0 -> x7, Pallas kernels: none -> 56.1 us  [the longest x1 15 us: fast_shards(): pl.pallas_call(mix_kernel, grid=(groups // many_t,), in_specs=[smem, whol...]
    reshape x13 -> x0, local copies, waits for them, and re-layouts: 53.6 us -> none  [the longest x8 30.4 us: leading_pass(): member.reshape(batch_size, groups, inner_count * row_count)]
    all_to_all x8 -> x1, starting transfers between devices: 42 us -> 6.52 us  [swap(): return lax.all_to_all(field, 'row', split_axis=0, concat_axis=0, tiled=True)]
    add x5 -> x0, local copies, waits for them, and re-layouts: 12.6 us -> none  [the longest x2 7.4 us: rotate(): real_part * factor_imag + imag_part * factor_real]
  transfers between devices with their start and end apart: 8 -> 4, of which waited for: 8 -> 3; matrix products, arithmetic and copies ran while one was open for 13% -> 0% of each run, Pallas kernels for 0% -> 6%
where the time goes in v1:
time: 372 us; the launch traced here: 370 us
  waiting for transfers between devices  165 us (44%)
  blocking collectives  136 us (37%)
  Pallas kernels  56.1 us (15%)
  starting transfers between devices  9.53 us (3%)
    all_to_all x3, blocking collectives, swap(): return lax.all_to_all(field, 'row', split_axis=0, concat_axis=0, tiled=True)  136 us
    ppermute x1, waiting for transfers between devices, fast_shards(): mine = lax.ppermute(send, 'row', flip)  131 us
    ppermute x1, waiting for transfers between devices, fast_shards(): other = lax.ppermute(mine, 'vol', [(0, 1), (1, 0)])  28.2 us
    pallas_call x1, Pallas kernels, fast_shards(): pl.pallas_call(mix_kernel, grid=(groups // many_t,), in_specs=[smem, whol...  15 us
    pallas_call x1, Pallas kernels, fast_shards(): pl.pallas_call(project_kernel, grid=(tiles // 2,), in_specs=x_specs + [al...  8.44 us
    pallas_call x1, Pallas kernels, fast_shards(): pl.pallas_call(correct_kernel, grid=(tiles // 2,), in_specs=x_specs + [on...  8.11 us
  transfers between devices with their start and end apart: 4, of which 3 were waited for; matrix products, arithmetic and copies ran while one was open for 0% of the time, Pallas kernels for 6%

profile of v1, /device:TPU:15, one launch (start us, length us, event | category | flops | bytes accessed | tf_op | source)
XLA Modules:
  0.0 370.2 jit_solution(5490222426013345419)
XLA Ops:
  0.6 6.6 %forward_y.1 = f32[16,3,8,2,8,128]{5,4,3,2,1,0:T(8,128)} custom-call(bf16[2,256,256]{2,1,0:T(8,128)(2,1)} %constant.32.clone.wy_ref, bf16[2,256,256]{2,1,0:T(8,128)(2,1)} %constant.33.clone.w0_ref, f32[16,2,128]{2,1,0:T(2,128)} %constant.36.clone.turn_ref, f32[3,128,2048]{2,1,0:T(8,128)} %v_ref.3), custom_call_target="tpu_custom_call" | custom-call | tf_op jit(solution)/shard_map/forward_y/pallas_call | solution.py:481
  7.3 6.5 %all-to-all-start = ((f32[16,3,8,2,8,128]{5,4,3,2,1,0:T(8,128)}), f32[16,3,8,2,8,128]{5,4,3,2,1,0:T(8,128)S(1)}, u32[]{:S(2)}, u32[]{:S(2)}) async-start(f32[16,3,8,2,8,128]{5,4,3,2,1,0:T(8,128)} %forward_y.1), calls=%async_computation | async-start | bytes 6291456 | tf_op jit(solution)/shard_map/all_to_all | solution.py:492
  13.8 0.7 pad_add_fusion.where_ref
  14.5 5.5 %pick.1 = (f32[3,64,2048]{2,1,0:T(8,128)}, f32[2,3,64,2048]{3,2,1,0:T(8,128)}) custom-call(s32[3]{0:T(128)} %pad_add_fusion.where_ref, bf16[64,128]{1,0:T(8,128)(2,1)} %constant.37.clone.sel_ref, bf16[64,128]{1,0:T(8,128)(2,1)} %constant.38.clone.own_l_ref, bf16[64,128]{1,0:T(8,128)(2,1)} %constant.39.clone.own_h_ref, bf16[2,3,128,2048]{3,2,1,0:T(8,128)(2,1)} %psf_ref.1), custom_call_target="tpu_custom_call" | custom-call | tf_op jit(solution)/shard_map/pick/pallas_call | solution.py:390
  19.9 1.5 collective-permute-start
  21.4 131.2 %collective-permute-done.mine_ref = f32[3,64,2048]{2,1,0:T(8,128)} collective-permute-done((f32[3,64,2048]{2,1,0:T(8,128)}, f32[3,64,2048]{2,1,0:T(8,128)}, u32[]{:S(2)}, u32[]{:S(2)}) %collective-permute-start) | collective-permute-done | bytes 1572896 | tf_op jit(solution)/shard_map/ppermute | solution.py:402
  152.6 0.3 collective-permute-start.1
  152.9 1.1 slice_reduce_fusion
  154.0 1.3 collective-permute-start.2
  155.3 5.3 %collective-permute-done.2.edge_ref = f32[16,2048]{1,0:T(8,128)S(1)} collective-permute-done((f32[16,2048]{1,0:T(8,128)S(1)}, f32[16,2048]{1,0:T(8,128)S(1)}, u32[]{:S(2)}, u32[]{:S(2)}) %collective-permute-start.2) | collective-permute-done | bytes 131104 | tf_op jit(solution)/shard_map/ppermute | solution.py:406
  160.6 0.0 copy-start.1
  160.6 28.2 %collective-permute-done.1.other_ref = f32[3,64,2048]{2,1,0:T(8,128)} collective-permute-done((f32[3,64,2048]{2,1,0:T(8,128)}, f32[3,64,2048]{2,1,0:T(8,128)}, u32[]{:S(2)}, u32[]{:S(2)}) %collective-permute-start.1) | collective-permute-done | bytes 1572896 | tf_op jit(solution)/shard_map/ppermute | solution.py:403
  188.8 0.0 copy-done.1
  188.8 15.0 %mix.1 = (f32[2,3,64,2048]{3,2,1,0:T(8,128)}, f32[2,3,16,2048]{3,2,1,0:T(8,128)}) custom-call(s32[3]{0:T(128)} %pad_add_fusion.where_ref, f32[2,3,64,2048]{3,2,1,0:T(8,128)} %get-tuple-element.8.own_ref, f32[3,64,2048]{2,1,0:T(8,128)} %collective-permute-done.mine_ref, f32[3,64,2048]{2,1,0:T(8,128)} %collective-permute-done.1.other_ref, f32[16,2048]{1,0:T(8,128)} %copy-done.1), custom_call_target="tpu_custom_call" | custom-call | tf_op jit(solution)/shard_map/mix/pallas_call | solution.py:458
  203.8 0.0 all-to-all-done.s_ref
  203.8 0.0 copy-start
  203.8 1.7 copy-done
  205.5 8.4 %project_x.1 = f32[16,8,2,8,128]{4,3,2,1,0:T(8,128)} custom-call(bf16[2,256,256]{2,1,0:T(8,128)(2,1)} %constant.34.clone.wx_ref, bf16[2,256,256]{2,1,0:T(8,128)(2,1)} %constant.35.clone.wxi_ref, f32[16,2,128]{2,1,0:T(2,128)} %constant.36.clone.turn_ref, f32[16,3,8,2,8,128]{5,4,3,2,1,0:T(8,128)} %copy-done, f32[2,3,64,2048]{3,2,1,0:T(8,128)} %get-tuple-element.10.a_ref, ...), custom_call_target="tpu_custom_call" | custom-call | tf_op jit(solution)/shard_map/project_x/pallas_call | solution.py:551
  213.9 31.1 %all_to_all.20.g_ref = f32[16,8,2,8,128]{4,3,2,1,0:T(8,128)} all-to-all(f32[16,8,2,8,128]{4,3,2,1,0:T(8,128)} %project_x.1), channel_id=1, replica_groups=mesh['vol'=2,'row'=16] {'row'}, dimensions={0} | all-to-all | bytes 2097152 | tf_op jit(solution)/shard_map/all_to_all | solution.py:492
  245.0 5.6 %ratio.1 = (f32[128,2048]{1,0:T(8,128)}, f32[16,8,2,8,128]{4,3,2,1,0:T(8,128)}) custom-call(bf16[2,256,256]{2,1,0:T(8,128)(2,1)} %constant.32.clone.wy_ref, bf16[2,256,256]{2,1,0:T(8,128)(2,1)} %constant.33.clone.w0_ref, f32[16,2,128]{2,1,0:T(2,128)} %constant.36.clone.turn_ref, f32[16,8,2,8,128]{4,3,2,1,0:T(8,128)} %all_to_all.20.g_ref, ...), custom_call_target="tpu_custom_call" | custom-call | tf_op jit(solution)/shard_map/ratio/pallas_call | solution.py:582
  250.6 30.0 %all_to_all.21.s_ref = f32[16,8,2,8,128]{4,3,2,1,0:T(8,128)} all-to-all(f32[16,8,2,8,128]{4,3,2,1,0:T(8,128)} %get-tuple-element.12), channel_id=1, replica_groups=mesh['vol'=2,'row'=16] {'row'}, dimensions={0} | all-to-all | bytes 2097152 | tf_op jit(solution)/shard_map/all_to_all | solution.py:492
  280.6 8.1 %correct_x.1 = f32[16,3,8,2,8,128]{5,4,3,2,1,0:T(8,128)} custom-call(bf16[2,256,256]{2,1,0:T(8,128)(2,1)} %constant.34.clone.wx_ref, bf16[2,256,256]{2,1,0:T(8,128)(2,1)} %constant.35.clone.wxi_ref, f32[16,2,128]{2,1,0:T(2,128)} %constant.36.clone.turn_ref, f32[16,8,2,8,128]{4,3,2,1,0:T(8,128)} %all_to_all.21.s_ref, ...), custom_call_target="tpu_custom_call" | custom-call | tf_op jit(solution)/shard_map/correct_x/pallas_call | solution.py:636
  288.7 74.8 %all_to_all.22.g_ref = f32[16,3,8,2,8,128]{5,4,3,2,1,0:T(8,128)} all-to-all(f32[16,3,8,2,8,128]{5,4,3,2,1,0:T(8,128)} %correct_x.1), channel_id=1, replica_groups=mesh['vol'=2,'row'=16] {'row'}, dimensions={0} | all-to-all | bytes 6291456 | tf_op jit(solution)/shard_map/all_to_all | solution.py:492
  363.5 6.7 %final_y.1 = f32[3,128,2048]{2,1,0:T(8,128)} custom-call(bf16[2,256,256]{2,1,0:T(8,128)(2,1)} %constant.32.clone.wy_ref, bf16[2,256,256]{2,1,0:T(8,128)(2,1)} %constant.33.clone.w0_ref, f32[16,2,128]{2,1,0:T(2,128)} %constant.36.clone.turn_ref, f32[16,3,8,2,8,128]{5,4,3,2,1,0:T(8,128)} %all_to_all.22.g_ref, f32[3,128,2048]{2,1,0:T(8,128)} %v_ref.3), custom_call_target="tpu_custom_call" | custom-call | tf_op jit(solution)/shard_map/final_y/pallas_call | solution.py:658
  (2 shorter events, 0.0 us)
Async XLA Ops:
  7.3 196.5 %all-to-all-start = ((f32[16,3,8,2,8,128]{5,4,3,2,1,0:T(8,128)}), f32[16,3,8,2,8,128]{5,4,3,2,1,0:T(8,128)S(1)}, u32[]{:S(2)}, u32[]{:S(2)}) async-start(f32[16,3,8,2,8,128]{5,4,3,2,1,0:T(8,128)} %forward_y.1), calls=%async_computation | async-start | bytes 6291456 | tf_op jit(solution)/shard_map/all_to_all | solution.py:492
  19.9 132.7 %collective-permute-start = (f32[3,64,2048]{2,1,0:T(8,128)}, f32[3,64,2048]{2,1,0:T(8,128)}, u32[]{:S(2)}, u32[]{:S(2)}) collective-permute-start(f32[3,64,2048]{2,1,0:T(8,128)} %get-tuple-element.9), channel_id=1, source_target_pairs={{0,15},{1,14},{2,13},{3,12},{4,11},{5,10},{6,9},{7,8},{8,7},{9,6},... | collective-permute-start | bytes 4718600 | tf_op jit(solution)/shard_map/ppermute | solution.py:402
  152.6 36.2 %collective-permute-start.1 = (f32[3,64,2048]{2,1,0:T(8,128)}, f32[3,64,2048]{2,1,0:T(8,128)}, u32[]{:S(2)}, u32[]{:S(2)}) collective-permute-start(f32[3,64,2048]{2,1,0:T(8,128)} %collective-permute-done.mine_ref), channel_id=1, source_target_pairs={{0,16},{16,0},{1,17},{17,1},{2,18},{18,2},{3,19},{19,3},{4,20},{20... | collective-permute-start | bytes 4718600 | tf_op jit(solution)/shard_map/ppermute | solution.py:403
  154.0 6.6 %collective-permute-start.2 = (f32[16,2048]{1,0:T(8,128)S(1)}, f32[16,2048]{1,0:T(8,128)S(1)}, u32[]{:S(2)}, u32[]{:S(2)}) collective-permute-start(f32[16,2048]{1,0:T(8,128)S(1)} %pad_convert_fusion), channel_id=1, source_target_pairs={{15,1},{14,2},{13,3},{12,4},{11,5},{10,6},{9,7},{8,0},{31,17},{30,... | collective-permute-start | bytes 393224 | tf_op jit(solution)/shard_map/ppermute | solution.py:406
  160.6 28.2 %copy-start.1 = (f32[16,2048]{1,0:T(8,128)}, f32[16,2048]{1,0:T(8,128)S(1)}, u32[]{:S(2)}) copy-start(f32[16,2048]{1,0:T(8,128)S(1)} %collective-permute-done.2.edge_ref) | copy-start | bytes 393220
  203.8 1.7 copy-start

commit v2 on v1

--- a/solution.py
+++ b/solution.py
@@ -7,6 +7,7 @@
 from jax.experimental import pallas as pl
 from jax.experimental.pallas import tpu as pltpu
 from jax.sharding import PartitionSpec as P
+
 
 FLOOR = 0.5
 HIGHEST = lax.Precision.HIGHEST
@@ -313,7 +314,7 @@
     lax.fori_loop(0, rows // SUB, chunk, 0)
 
 
-def x_radix(tile, z, base, turn, groups, lanes, step):
+def x_radix(tile, z, base, turn, lanes, step):
     for t, (re, im) in enumerate(cfft(tile, -1.0)):
         here = pl.ds(pl.multiple_of(base + t * step, SUB), SUB)
         if t == 0:
@@ -339,7 +340,6 @@
 
 def fast_shards(volume, psf_spectra, background, measured):
     groups = lax.axis_size("row")
-    parts = lax.axis_size("vol")
     depth, rows, length = volume.shape
     lanes = LANES
     tiles = groups // 2
@@ -371,60 +371,63 @@
     pick_high[0] = 0.0
     pick_high[0, mid] = 1.0
 
-    def pick_kernel(where_ref, sel_ref, own_l_ref, own_h_ref, psf_ref, send_ref, own_ref):
-        sel = jnp.where(where_ref[0] == 1, own_l_ref[...], own_h_ref[...])
-        for c in range(2):
-            own_ref[c, 0] = mm(sel, psf_ref[c, 0], NN)
-
-        @pl.when(where_ref[1] == 0)
-        def _():
-            send_ref[0] = mm(sel_ref[...], psf_ref[0, 0], NN)
-
-        @pl.when(where_ref[1] != 0)
-        def _():
-            send_ref[0] = mm(sel_ref[...], psf_ref[1, 0], NN)
+    def pick_kernel(part_ref, sel_ref, psf_ref, send_ref):
+        send_ref[...] = mm(sel_ref[...], psf_ref[0, 0], NN)
 
     flags = jnp.stack([low.astype(jnp.int32), part.astype(jnp.int32), (place == 0).astype(jnp.int32)])
     smem = pl.BlockSpec(memory_space=pltpu.SMEM)
     bf = jnp.bfloat16
-    send, own = pl.pallas_call(
-        pick_kernel,
-        grid=(depth,),
-        in_specs=[smem, whole(kept, rows), whole(kept, rows), whole(kept, rows),
-                  pl.BlockSpec((2, 1, rows, length), lambda d: (0, d, 0, 0))],
-        out_specs=[pl.BlockSpec((1, kept, length), lambda d: (d, 0, 0)),
-                   pl.BlockSpec((2, 1, kept, length), lambda d: (0, d, 0, 0))],
-        out_shape=[jax.ShapeDtypeStruct((depth, kept, length), f32),
-                   jax.ShapeDtypeStruct((2, depth, kept, length), f32)],
-        name="pick",
-    )(flags, jnp.asarray(pick_send, bf), jnp.asarray(pick_own, bf), jnp.asarray(pick_high, bf), psf_spectra)
+    sel_send = jnp.asarray(pick_send, bf)
     flip = [(p, groups - 1 - p) for p in range(groups)]
-    mine = lax.ppermute(send, "row", flip)
-    other = lax.ppermute(mine, "vol", [(0, 1), (1, 0)])
+    sends, mine, other = [], [], []
+    for d in range(depth):
+        send = pl.pallas_call(
+            pick_kernel,
+            grid_spec=pltpu.PrefetchScalarGridSpec(
+                num_scalar_prefetch=1,
+                grid=(1,),
+                in_specs=[whole(kept, rows),
+                          pl.BlockSpec((1, 1, rows, length), lambda i, where, d=d: (where[1], d, 0, 0))],
+                out_specs=whole(kept, length),
+            ),
+            out_shape=jax.ShapeDtypeStruct((kept, length), f32),
+            name="pick",
+        )(flags, sel_send, psf_spectra)
+        sends.append(send)
     edge = psf_spectra[:, :, 0, :].astype(f32).reshape(2 * depth, length)
     edge = jnp.pad(edge, ((0, pair - 2 * depth), (0, 0)))
-    edge = lax.ppermute(edge, "row", [(groups - p, p) for p in range(1, groups // 2)] + [(groups // 2, 0)])
+    edge, early, *sends = lax.optimization_barrier((edge, volume, *sends))
+    ends = [(groups - p, p) for p in range(1, groups // 2)] + [(groups // 2, 0)]
+    edge = lax.ppermute(edge, "row", ends)
+    for d in range(depth):
+        mine.append(lax.ppermute(sends[d], "row", flip))
+    for d in range(depth):
+        other.append(lax.ppermute(mine[d], "vol", [(0, 1), (1, 0)]))
 
     scale = 0.5 / (length * length)
     many_t = 2
     width = many_t * lanes
 
-    def mix_kernel(where_ref, own_ref, mine_ref, other_ref, edge_ref, a_ref, b_ref, o_s, p_s, e_s):
+    def mix_kernel(where_ref, own_l_ref, own_h_ref, psf_ref, edge_ref, *rest):
+        mine_refs, other_refs = rest[:depth], rest[depth:2 * depth]
+        a_ref, b_ref, o_s, p_s, e_s = rest[2 * depth:]
         step = pl.program_id(0)
 
         @pl.when(step == 0)
         def _():
             zero = where_ref[2] == 1
             is_low = where_ref[0] == 1
+            sel = jnp.where(is_low, own_l_ref[...], own_h_ref[...]).astype(bf)
             first = lax.broadcasted_iota(jnp.int32, (SUB, length), 0) == 0
             for c in range(2):
+                mine_here = where_ref[1] == c
                 for d in range(depth):
-                    base = (c * depth + d) * kept
-                    mine_here = where_ref[1] == c
-                    o_s[base:base + kept, :] = own_ref[c, d].astype(bf)
-                    p = jnp.where(mine_here, mine_ref[d], other_ref[d])
                     row = c * depth + d
-                    swap = jnp.where(zero, own_ref[c, d, 0:1, :], edge_ref[row:row + 1, :])
+                    base = row * kept
+                    kept_own = mm(sel, psf_ref[c, d], NN)
+                    o_s[base:base + kept, :] = kept_own.astype(bf)
+                    p = jnp.where(mine_here, mine_refs[d][...], other_refs[d][...])
+                    swap = jnp.where(zero, kept_own[0:1, :], edge_ref[row:row + 1, :])
                     head = jnp.where(jnp.logical_and(first, is_low), swap, p[:SUB])
                     p_s[base:base + kept, :] = jnp.concatenate([head, p[SUB:]], 0).astype(bf)
             e_s[...] = edge_ref[...].astype(bf)
@@ -458,8 +461,8 @@
     a_all, b_all = pl.pallas_call(
         mix_kernel,
         grid=(groups // many_t,),
-        in_specs=[smem, whole(2, depth, kept, length), whole(depth, kept, length),
-                  whole(depth, kept, length), whole(pair, length)],
+        in_specs=[smem, whole(kept, rows), whole(kept, rows), whole(2, depth, rows, length),
+                  whole(pair, length)] + [whole(kept, length)] * (2 * depth),
         out_specs=[pl.BlockSpec((2, depth, kept, width), lambda i: (0, 0, 0, i)),
                    pl.BlockSpec((2, depth, pair, width), lambda i: (0, 0, 0, i))],
         out_shape=[jax.ShapeDtypeStruct((2, depth, kept, length), f32),
@@ -467,7 +470,7 @@
         scratch_shapes=[pltpu.VMEM((planes, length), bf), pltpu.VMEM((planes, length), bf),
                         pltpu.VMEM((pair, length), bf)],
         name="mix",
-    )(flags, own, mine, other, edge)
+    )(flags, jnp.asarray(pick_own), jnp.asarray(pick_high), psf_spectra, edge, *mine, *other)
 
     def forward_kernel(wy_ref, w0_ref, turn_ref, v_ref, o_ref, z):
         def read(i, a):
@@ -486,11 +489,12 @@
         out_shape=jax.ShapeDtypeStruct(many(depth), f32),
         scratch_shapes=[y_scratch],
         name="forward_y",
-    )(w_y, w_0, turn, volume)
+    )(w_y, w_0, turn, early)
 
     def swap(field):
         return lax.all_to_all(field, "row", split_axis=0, concat_axis=0, tiled=True)
 
+    outgoing, _ = lax.optimization_barrier((outgoing, mine[depth // 2]))
     arrived = swap(outgoing)
 
     block = groups * pair
@@ -507,8 +511,9 @@
         def gather(flipped):
             def one(i, carry):
                 d, h = i // 2, i % 2
-                x_radix(source(s_ref, d, h, flipped), z, d * block + h * SUB, turn_ref, groups, lanes, pair)
+                x_radix(source(s_ref, d, h, flipped), z, d * block + h * SUB, turn_ref, lanes, pair)
                 return carry
+
             lax.fori_loop(0, 2 * depth, one, 0)
             for d in range(depth):
                 zc[d * block:(d + 1) * block, :] = data_table(z[d * block:(d + 1) * block, :], wx_ref)
@@ -542,6 +547,7 @@
                 o_ref[s, h, 0] = re
                 o_ref[s, h, 1] = im
             return carry
+
         lax.fori_loop(0, 2, back, 0)
 
     k_specs = [pl.BlockSpec((2, depth, pair, length), lambda j: (0, 0, j, 0)),
@@ -594,8 +600,9 @@
                 for s in range(groups):
                     re, im = s_ref[s, h, 0], s_ref[s, h, 1]
                     tile.append((re, -im if flipped else im))
-                x_radix(tile, z, h * SUB, turn_ref, groups, lanes, pair)
+                x_radix(tile, z, h * SUB, turn_ref, lanes, pair)
                 return carry
+
             lax.fori_loop(0, 2, one, 0)
             out[...] = data_table(z[...], wx_ref)
 
@@ -631,6 +638,7 @@
                 o_ref[s, d, h, 0] = re
                 o_ref[s, d, h, 1] = im
             return carry
+
         lax.fori_loop(0, 2 * depth, back, 0)
 
     outgoing = pl.pallas_call(

time: 372 us -> 359 us (0.965)
  waiting for transfers between devices: 165 us -> 143 us
    ppermute x3 -> x7, waiting for transfers between devices: 165 us -> 143 us  [the longest x3 131 us: fast_shards(): mine.append(lax.ppermute(sends[d], 'row', flip))]
    pallas_call x1 -> x3, Pallas kernels: 5.47 us -> 8.2 us  [fast_shards(): pl.pallas_call(pick_kernel, grid_spec=pltpu.PrefetchScalarGridSpec(num_sc...]
  transfers between devices with their start and end apart: 4 -> 8, of which waited for: 3 -> 5; matrix products, arithmetic and copies ran while one was open for 0% -> 0% of each run, Pallas kernels for 6% -> 6%
where the time goes in v2:
time: 359 us; the launch traced here: 357 us
  waiting for transfers between devices  143 us (40%)
  blocking collectives  136 us (38%)
  Pallas kernels  59.5 us (17%)
  starting transfers between devices  11.8 us (3%)
  local copies, waits for them, and re-layouts  5.98 us (2%)
    all_to_all x3, blocking collectives, swap(): return lax.all_to_all(field, 'row', split_axis=0, concat_axis=0, tiled=True)  136 us
    ppermute x3, waiting for transfers between devices, fast_shards(): mine.append(lax.ppermute(sends[d], 'row', flip))  131 us
    pallas_call x1, Pallas kernels, fast_shards(): pl.pallas_call(mix_kernel, grid=(groups // many_t,), in_specs=[smem, whol...  15.8 us
    pallas_call x1, Pallas kernels, fast_shards(): pl.pallas_call(project_kernel, grid=(tiles // 2,), in_specs=x_specs + [al...  8.44 us
    pallas_call x3, Pallas kernels, fast_shards(): pl.pallas_call(pick_kernel, grid_spec=pltpu.PrefetchScalarGridSpec(num_sc...  8.2 us
    pallas_call x1, Pallas kernels, fast_shards(): pl.pallas_call(correct_kernel, grid=(tiles // 2,), in_specs=x_specs + [on...  8.11 us
  transfers between devices with their start and end apart: 8, of which 5 were waited for; matrix products, arithmetic and copies ran while one was open for 0% of the time, Pallas kernels for 6%

profile of v2, /device:TPU:15, one launch (start us, length us, event | category | flops | bytes accessed | tf_op | source)
XLA Modules:
  0.0 357.1 jit_solution(10626836347306917537)
XLA Ops:
  0.6 1.1 slice_reduce_fusion
  1.7 0.6 pad_add_fusion.part_ref.where_ref
  2.3 2.7 pick.3
  5.0 2.7 pick.5
  7.8 2.7 pick.4
  10.6 1.9 collective-permute-start
  12.4 6.6 %forward_y.1 = f32[16,3,8,2,8,128]{5,4,3,2,1,0:T(8,128)} custom-call(bf16[2,256,256]{2,1,0:T(8,128)(2,1)} %constant.32.clone.wy_ref, bf16[2,256,256]{2,1,0:T(8,128)(2,1)} %constant.33.clone.w0_ref, f32[16,2,128]{2,1,0:T(2,128)} %constant.36.clone.turn_ref, f32[3,128,2048]{2,1,0:T(8,128)} %v_ref.2), custom_call_target="tpu_custom_call" | custom-call | tf_op jit(solution)/shard_map/forward_y/pallas_call | solution.py:484
  19.0 18.4 %collective-permute-done.rest_1_ = f32[64,2048]{1,0:T(8,128)S(1)} collective-permute-done((f32[64,2048]{1,0:T(8,128)}, f32[64,2048]{1,0:T(8,128)S(1)}, u32[]{:S(2)}, u32[]{:S(2)}) %collective-permute-start) | collective-permute-done | bytes 524320 | tf_op jit(solution)/shard_map/ppermute | solution.py:403
  37.5 0.0 copy-start.1
  37.5 0.8 copy-done.1
  38.3 5.2 %all-to-all-start = ((f32[16,3,8,2,8,128]{5,4,3,2,1,0:T(8,128)}), f32[16,3,8,2,8,128]{5,4,3,2,1,0:T(8,128)S(1)}, u32[]{:S(2)}, u32[]{:S(2)}) async-start(f32[16,3,8,2,8,128]{5,4,3,2,1,0:T(8,128)} %forward_y.1), calls=%async_computation | async-start | bytes 6291456 | tf_op jit(solution)/shard_map/all_to_all | solution.py:495
  43.5 1.5 collective-permute-start.2
  45.0 1.2 collective-permute-start.3
  46.1 0.3 collective-permute-start.5
  46.4 103.0 %collective-permute-done.2.rest_0_ = f32[64,2048]{1,0:T(8,128)S(1)} collective-permute-done((f32[64,2048]{1,0:T(8,128)}, f32[64,2048]{1,0:T(8,128)S(1)}, u32[]{:S(2)}, u32[]{:S(2)}) %collective-permute-start.2) | collective-permute-done | bytes 524320 | tf_op jit(solution)/shard_map/ppermute | solution.py:403
  149.4 0.0 copy-start.2
  149.4 0.8 copy-done.2
  150.1 0.3 collective-permute-start.4
  150.4 9.3 %collective-permute-done.3.rest_2_ = f32[64,2048]{1,0:T(8,128)S(1)} collective-permute-done((f32[64,2048]{1,0:T(8,128)}, f32[64,2048]{1,0:T(8,128)S(1)}, u32[]{:S(2)}, u32[]{:S(2)}) %collective-permute-start.3) | collective-permute-done | bytes 524320 | tf_op jit(solution)/shard_map/ppermute | solution.py:403
  159.7 0.0 copy-start.3
  159.7 0.3 collective-permute-start.6
  160.0 1.3 collective-permute-start.1
  161.3 5.3 %collective-permute-done.1.edge_ref = f32[16,2048]{1,0:T(8,128)S(1)} collective-permute-done((f32[16,2048]{1,0:T(8,128)S(1)}, f32[16,2048]{1,0:T(8,128)S(1)}, u32[]{:S(2)}, u32[]{:S(2)}) %collective-permute-start.1) | collective-permute-done | bytes 131104 | tf_op jit(solution)/shard_map/ppermute | solution.py:401
  166.6 0.0 copy-start.6
  166.6 0.0 collective-permute-done.5.rest_4_
  166.6 0.0 copy-start.4
  166.6 0.0 collective-permute-done.4.rest_3_
  166.6 0.0 copy-done.3
  166.6 0.8 copy-done.4
  167.4 0.0 copy-start.5
  167.4 0.8 copy-done.5
  168.2 6.6 %collective-permute-done.6.rest_5_ = f32[64,2048]{1,0:T(8,128)} collective-permute-done((f32[64,2048]{1,0:T(8,128)S(1)}, f32[64,2048]{1,0:T(8,128)}, u32[]{:S(2)}, u32[]{:S(2)}) %collective-permute-start.6) | collective-permute-done | bytes 524320 | tf_op jit(solution)/shard_map/ppermute | solution.py:405
  174.8 0.0 copy-done.6
  174.8 15.8 %mix.1 = (f32[2,3,64,2048]{3,2,1,0:T(8,128)}, f32[2,3,16,2048]{3,2,1,0:T(8,128)}) custom-call(s32[3]{0:T(128)} %pad_add_fusion.part_ref.where_ref, f32[64,128]{1,0:T(8,128)} %constant.38.clone.own_l_ref, f32[64,128]{1,0:T(8,128)} %constant.39.clone.own_h_ref, bf16[2,3,128,2048]{3,2,1,0:T(8,128)(2,1)} %psf_ref.7, f32[16,2048]{1,0:T(8,128)} %copy-done.6, ...), custom_call_target="tpu_custom_call" | custom-call | tf_op jit(solution)/shard_map/mix/pallas_call | solution.py:461
  190.6 0.0 all-to-all-done.s_ref
  190.6 0.0 copy-start
  190.6 1.7 copy-done
  192.3 8.4 %project_x.1 = f32[16,8,2,8,128]{4,3,2,1,0:T(8,128)} custom-call(bf16[2,256,256]{2,1,0:T(8,128)(2,1)} %constant.34.clone.wx_ref, bf16[2,256,256]{2,1,0:T(8,128)(2,1)} %constant.35.clone.wxi_ref, f32[16,2,128]{2,1,0:T(2,128)} %constant.36.clone.turn_ref, f32[16,3,8,2,8,128]{5,4,3,2,1,0:T(8,128)} %copy-done, f32[2,3,64,2048]{3,2,1,0:T(8,128)} %get-tuple-element.18.a_ref, ...), custom_call_target="tpu_custom_call" | custom-call | tf_op jit(solution)/shard_map/project_x/pallas_call | solution.py:557
  200.7 30.5 %all_to_all.20.g_ref = f32[16,8,2,8,128]{4,3,2,1,0:T(8,128)} all-to-all(f32[16,8,2,8,128]{4,3,2,1,0:T(8,128)} %project_x.1), channel_id=1, replica_groups=mesh['vol'=2,'row'=16] {'row'}, dimensions={0} | all-to-all | bytes 2097152 | tf_op jit(solution)/shard_map/all_to_all | solution.py:495
  231.2 5.6 %ratio.1 = (f32[128,2048]{1,0:T(8,128)}, f32[16,8,2,8,128]{4,3,2,1,0:T(8,128)}) custom-call(bf16[2,256,256]{2,1,0:T(8,128)(2,1)} %constant.32.clone.wy_ref, bf16[2,256,256]{2,1,0:T(8,128)(2,1)} %constant.33.clone.w0_ref, f32[16,2,128]{2,1,0:T(2,128)} %constant.36.clone.turn_ref, f32[16,8,2,8,128]{4,3,2,1,0:T(8,128)} %all_to_all.20.g_ref, ...), custom_call_target="tpu_custom_call" | custom-call | tf_op jit(solution)/shard_map/ratio/pallas_call | solution.py:588
  236.9 30.6 %all_to_all.21.s_ref = f32[16,8,2,8,128]{4,3,2,1,0:T(8,128)} all-to-all(f32[16,8,2,8,128]{4,3,2,1,0:T(8,128)} %get-tuple-element.20), channel_id=1, replica_groups=mesh['vol'=2,'row'=16] {'row'}, dimensions={0} | all-to-all | bytes 2097152 | tf_op jit(solution)/shard_map/all_to_all | solution.py:495
  267.5 8.1 %correct_x.1 = f32[16,3,8,2,8,128]{5,4,3,2,1,0:T(8,128)} custom-call(bf16[2,256,256]{2,1,0:T(8,128)(2,1)} %constant.34.clone.wx_ref, bf16[2,256,256]{2,1,0:T(8,128)(2,1)} %constant.35.clone.wxi_ref, f32[16,2,128]{2,1,0:T(2,128)} %constant.36.clone.turn_ref, f32[16,8,2,8,128]{4,3,2,1,0:T(8,128)} %all_to_all.21.s_ref, ...), custom_call_target="tpu_custom_call" | custom-call | tf_op jit(solution)/shard_map/correct_x/pallas_call | solution.py:644
  275.6 74.8 %all_to_all.22.g_ref = f32[16,3,8,2,8,128]{5,4,3,2,1,0:T(8,128)} all-to-all(f32[16,3,8,2,8,128]{5,4,3,2,1,0:T(8,128)} %correct_x.1), channel_id=1, replica_groups=mesh['vol'=2,'row'=16] {'row'}, dimensions={0} | all-to-all | bytes 6291456 | tf_op jit(solution)/shard_map/all_to_all | solution.py:495
  350.4 6.7 %final_y.1 = f32[3,128,2048]{2,1,0:T(8,128)} custom-call(bf16[2,256,256]{2,1,0:T(8,128)(2,1)} %constant.32.clone.wy_ref, bf16[2,256,256]{2,1,0:T(8,128)(2,1)} %constant.33.clone.w0_ref, f32[16,2,128]{2,1,0:T(2,128)} %constant.36.clone.turn_ref, f32[16,3,8,2,8,128]{5,4,3,2,1,0:T(8,128)} %all_to_all.22.g_ref, f32[3,128,2048]{2,1,0:T(8,128)} %v_ref.2), custom_call_target="tpu_custom_call" | custom-call | tf_op jit(solution)/shard_map/final_y/pallas_call | solution.py:666
  (2 shorter events, 0.0 us)
Async XLA Ops:
  10.6 26.9 %collective-permute-start = (f32[64,2048]{1,0:T(8,128)}, f32[64,2048]{1,0:T(8,128)S(1)}, u32[]{:S(2)}, u32[]{:S(2)}) collective-permute-start(f32[64,2048]{1,0:T(8,128)} %pick.4), channel_id=1, source_target_pairs={{0,15},{1,14},{2,13},{3,12},{4,11},{5,10},{6,9},{7,8},{8,7},{9,6},... | collective-permute-start | bytes 1572872 | tf_op jit(solution)/shard_map/ppermute | solution.py:403
  37.5 0.8 copy-start.1
  38.3 152.4 %all-to-all-start = ((f32[16,3,8,2,8,128]{5,4,3,2,1,0:T(8,128)}), f32[16,3,8,2,8,128]{5,4,3,2,1,0:T(8,128)S(1)}, u32[]{:S(2)}, u32[]{:S(2)}) async-start(f32[16,3,8,2,8,128]{5,4,3,2,1,0:T(8,128)} %forward_y.1), calls=%async_computation | async-start | bytes 6291456 | tf_op jit(solution)/shard_map/all_to_all | solution.py:495
  43.5 105.9 %collective-permute-start.2 = (f32[64,2048]{1,0:T(8,128)}, f32[64,2048]{1,0:T(8,128)S(1)}, u32[]{:S(2)}, u32[]{:S(2)}) collective-permute-start(f32[64,2048]{1,0:T(8,128)} %pick.3), channel_id=1, source_target_pairs={{0,15},{1,14},{2,13},{3,12},{4,11},{5,10},{6,9},{7,8},{8,7},{9,6},... | collective-permute-start | bytes 1572872 | tf_op jit(solution)/shard_map/ppermute | solution.py:403
  45.0 114.8 %collective-permute-start.3 = (f32[64,2048]{1,0:T(8,128)}, f32[64,2048]{1,0:T(8,128)S(1)}, u32[]{:S(2)}, u32[]{:S(2)}) collective-permute-start(f32[64,2048]{1,0:T(8,128)} %pick.5), channel_id=1, source_target_pairs={{0,15},{1,14},{2,13},{3,12},{4,11},{5,10},{6,9},{7,8},{8,7},{9,6},... | collective-permute-start | bytes 1572872 | tf_op jit(solution)/shard_map/ppermute | solution.py:403
  46.1 120.5 %collective-permute-start.5 = (f32[64,2048]{1,0:T(8,128)}, f32[64,2048]{1,0:T(8,128)S(1)}, u32[]{:S(2)}, u32[]{:S(2)}) collective-permute-start(f32[64,2048]{1,0:T(8,128)} %copy-done.1), channel_id=1, source_target_pairs={{0,16},{16,0},{1,17},{17,1},{2,18},{18,2},{3,19},{19,3},{4,20},{20... | collective-permute-start | bytes 1572872 | tf_op jit(solution)/shard_map/ppermute | solution.py:405
  149.4 0.8 copy-start.2
  150.1 16.4 %collective-permute-start.4 = (f32[64,2048]{1,0:T(8,128)S(1)}, f32[64,2048]{1,0:T(8,128)S(1)}, u32[]{:S(2)}, u32[]{:S(2)}) collective-permute-start(f32[64,2048]{1,0:T(8,128)S(1)} %collective-permute-done.2.rest_0_), channel_id=1, source_target_pairs={{0,16},{16,0},{1,17},{17,1},{2,18},{18,2},{3,19},{19,3},{4,20},{20... | collective-permute-start | bytes 1572872 | tf_op jit(solution)/shard_map/ppermute | solution.py:405
  159.7 6.9 %copy-start.3 = (f32[64,2048]{1,0:T(8,128)}, f32[64,2048]{1,0:T(8,128)S(1)}, u32[]{:S(2)}) copy-start(f32[64,2048]{1,0:T(8,128)S(1)} %collective-permute-done.3.rest_2_) | copy-start | bytes 1572868
  159.7 15.1 %collective-permute-start.6 = (f32[64,2048]{1,0:T(8,128)S(1)}, f32[64,2048]{1,0:T(8,128)}, u32[]{:S(2)}, u32[]{:S(2)}) collective-permute-start(f32[64,2048]{1,0:T(8,128)S(1)} %collective-permute-done.3.rest_2_), channel_id=1, source_target_pairs={{0,16},{16,0},{1,17},{17,1},{2,18},{18,2},{3,19},{19,3},{4,20},{20... | collective-permute-start | bytes 1572872 | tf_op jit(solution)/shard_map/ppermute | solution.py:405
  160.0 6.6 %collective-permute-start.1 = (f32[16,2048]{1,0:T(8,128)S(1)}, f32[16,2048]{1,0:T(8,128)S(1)}, u32[]{:S(2)}, u32[]{:S(2)}) collective-permute-start(f32[16,2048]{1,0:T(8,128)S(1)} %pad_convert_fusion), channel_id=1, source_target_pairs={{15,1},{14,2},{13,3},{12,4},{11,5},{10,6},{9,7},{8,0},{31,17},{30,... | collective-permute-start | bytes 393224 | tf_op jit(solution)/shard_map/ppermute | solution.py:401
  166.6 8.3 %copy-start.6 = (f32[16,2048]{1,0:T(8,128)}, f32[16,2048]{1,0:T(8,128)S(1)}, u32[]{:S(2)}) copy-start(f32[16,2048]{1,0:T(8,128)S(1)} %collective-permute-done.1.edge_ref) | copy-start | bytes 393220
  166.6 0.8 copy-start.4
  167.4 0.8 copy-start.5
  190.6 1.7 copy-start

commit v3 on v2

--- a/solution.py
+++ b/solution.py
@@ -352,8 +352,19 @@
     own_rows = kept_rows(groups, rows)
 
     whole = lambda *shape: pl.BlockSpec(shape, lambda *_: (0,) * len(shape))
-    y_specs = [whole(*w_y.shape), whole(*w_0.shape), whole(*turn.shape)]
-    x_specs = [whole(*w_x.shape), whole(*w_xi.shape), whole(*turn.shape)]
+    near = pl.BlockSpec(memory_space=pltpu.VMEM)
+
+    def keep(x):
+        return pltpu.with_memory_space_constraint(x, pltpu.VMEM)
+
+    def far(x):
+        return pltpu.with_memory_space_constraint(x, pltpu.HBM)
+
+    y_tables, x_tables = (w_y, w_0, turn), (w_x, w_xi, turn)
+    y_near = tuple(keep(t) for t in y_tables)
+    x_near = tuple(keep(t) for t in x_tables)
+    y_specs = [whole(*t.shape) for t in y_tables]
+    x_specs = [whole(*t.shape) for t in x_tables]
     y_scratch = pltpu.VMEM((tiles, rows, 2 * lanes), f32)
     send_shape = (groups, tiles, 2, SUB, lanes)
 
@@ -387,20 +398,19 @@
                 num_scalar_prefetch=1,
                 grid=(1,),
                 in_specs=[whole(kept, rows),
-                          pl.BlockSpec((1, 1, rows, length), lambda i, where, d=d: (where[1], d, 0, 0))],
+                          pl.BlockSpec((1, 1, rows, length), lambda i, where, d=d: (where[0], d, 0, 0))],
                 out_specs=whole(kept, length),
             ),
             out_shape=jax.ShapeDtypeStruct((kept, length), f32),
             name="pick",
-        )(flags, sel_send, psf_spectra)
+        )(part.astype(jnp.int32).reshape(1), sel_send, psf_spectra)
         sends.append(send)
-    edge = psf_spectra[:, :, 0, :].astype(f32).reshape(2 * depth, length)
+        mine.append(lax.ppermute(send, "row", flip))
+    late, early, _ = lax.optimization_barrier((psf_spectra, volume, sends[-1]))
+    edge = late[:, :, 0, :].astype(f32).reshape(2 * depth, length)
     edge = jnp.pad(edge, ((0, pair - 2 * depth), (0, 0)))
-    edge, early, *sends = lax.optimization_barrier((edge, volume, *sends))
     ends = [(groups - p, p) for p in range(1, groups // 2)] + [(groups // 2, 0)]
     edge = lax.ppermute(edge, "row", ends)
-    for d in range(depth):
-        mine.append(lax.ppermute(sends[d], "row", flip))
     for d in range(depth):
         other.append(lax.ppermute(mine[d], "vol", [(0, 1), (1, 0)]))
 
@@ -442,6 +452,7 @@
         e_plain = mm(e_s[...], hot, NN)
         e_mirror = mm(e_s[...], hot_rev, NN)
         zero = jnp.where(where_ref[2] == 1, 1.0, 0.0).astype(f32)
+        b_ref[...] = jnp.zeros((2, SUB, width), f32)
         first = lax.broadcasted_iota(jnp.int32, (SUB, width), 0) == 0
         for c in range(2):
             sign = 1.0 if c == 0 else -1.0
@@ -454,8 +465,7 @@
                 b0 = (h[:SUB] - e) * (0.25 * zero)
                 a_ref[c, d, :SUB, :] = jnp.where(first, a0, h[:SUB])
                 a_ref[c, d, SUB:, :] = h[SUB:]
-                b_ref[c, d, :SUB, :] = jnp.where(first, b0, 0.0)
-                b_ref[c, d, SUB:, :] = jnp.zeros((SUB, width), f32)
+                b_ref[c, d:d + 1, :] = b0[0:1, :]
 
     planes = 2 * depth * kept
     a_all, b_all = pl.pallas_call(
@@ -464,9 +474,9 @@
         in_specs=[smem, whole(kept, rows), whole(kept, rows), whole(2, depth, rows, length),
                   whole(pair, length)] + [whole(kept, length)] * (2 * depth),
         out_specs=[pl.BlockSpec((2, depth, kept, width), lambda i: (0, 0, 0, i)),
-                   pl.BlockSpec((2, depth, pair, width), lambda i: (0, 0, 0, i))],
+                   pl.BlockSpec((2, SUB, width), lambda i: (0, 0, i))],
         out_shape=[jax.ShapeDtypeStruct((2, depth, kept, length), f32),
-                   jax.ShapeDtypeStruct((2, depth, pair, length), f32)],
+                   jax.ShapeDtypeStruct((2, SUB, length), f32)],
         scratch_shapes=[pltpu.VMEM((planes, length), bf), pltpu.VMEM((planes, length), bf),
                         pltpu.VMEM((pair, length), bf)],
         name="mix",
@@ -489,80 +499,85 @@
         out_shape=jax.ShapeDtypeStruct(many(depth), f32),
         scratch_shapes=[y_scratch],
         name="forward_y",
-    )(w_y, w_0, turn, early)
+    )(*y_tables, early)
 
     def swap(field):
         return lax.all_to_all(field, "row", split_axis=0, concat_axis=0, tiled=True)
 
-    outgoing, _ = lax.optimization_barrier((outgoing, mine[depth // 2]))
+    outgoing, _ = lax.optimization_barrier((outgoing, mine[0]))
     arrived = swap(outgoing)
 
     block = groups * pair
     x_scratch = lambda n: pltpu.VMEM((n * block, 2 * lanes), f32)
 
-    def source(s_ref, d, h, flipped=False):
-        out = []
-        for s in range(groups):
-            re, im = s_ref[s, d, h, 0], s_ref[s, d, h, 1]
-            out.append((re, -im if flipped else im))
-        return out
+    small = groups * SUB
+    lead = lambda: lax.broadcasted_iota(jnp.int32, (SUB, lanes), 0)
 
     def project_kernel(wx_ref, wxi_ref, turn_ref, s_ref, a_ref, b_ref, o_ref, z, t_s, zc):
-        def gather(flipped):
-            def one(i, carry):
-                d, h = i // 2, i % 2
-                x_radix(source(s_ref, d, h, flipped), z, d * block + h * SUB, turn_ref, lanes, pair)
-                return carry
-
-            lax.fori_loop(0, 2 * depth, one, 0)
+        def one(i, carry):
+            d, h = i // 2, i % 2
+            j = pl.program_id(0) * 2 + h
+            tile = [(s_ref[s, d, j, 0], s_ref[s, d, j, 1]) for s in range(groups)]
+            x_radix(tile, z, d * block + h * SUB, turn_ref, lanes, pair)
+            return carry
+
+        lax.fori_loop(0, 2 * depth, one, 0)
+        for d in range(depth):
+            zc[d * block:(d + 1) * block, :] = data_table(z[d * block:(d + 1) * block, :], wx_ref)
+        for t in range(groups):
+            here = slice(t * pair, (t + 1) * pair)
+            cols = slice(t * lanes, (t + 1) * lanes)
+            re = im = None
             for d in range(depth):
-                zc[d * block:(d + 1) * block, :] = data_table(z[d * block:(d + 1) * block, :], wx_ref)
-
-        def multiply(k_ref, fresh):
-            for t in range(groups):
-                here = slice(t * pair, (t + 1) * pair)
-                cols = slice(t * lanes, (t + 1) * lanes)
-                re, im = (None, None) if fresh else (t_s[here, :lanes], t_s[here, lanes:])
-                for d in range(depth):
-                    at = slice(d * block + t * pair, d * block + (t + 1) * pair)
-                    zr, zi = zc[at, :lanes], zc[at, lanes:]
-                    kr, ki = k_ref[0, d, :, cols], k_ref[1, d, :, cols]
-                    re = plus(re, zr * kr - zi * ki)
-                    im = plus(im, zr * ki + zi * kr)
-                t_s[here, :lanes] = re
-                t_s[here, lanes:] = im
-
-        gather(False)
-        multiply(a_ref, True)
+                at = slice(d * block + t * pair, d * block + (t + 1) * pair)
+                zr, zi = zc[at, :lanes], zc[at, lanes:]
+                kr, ki = a_ref[0, d, :, cols], a_ref[1, d, :, cols]
+                re = plus(re, zr * kr - zi * ki)
+                im = plus(im, zr * ki + zi * kr)
+            t_s[here, :lanes] = re
+            t_s[here, lanes:] = im
 
         @pl.when(pl.program_id(0) == 0)
         def _():
-            gather(True)
-            multiply(b_ref, False)
+            def row(s, c):
+                out = s_ref[s, 0, 0, c, 0:1, :]
+                for d in range(1, depth):
+                    out = jnp.where(lead() == d, s_ref[s, d, 0, c, 0:1, :], out)
+                return jnp.broadcast_to(out, (SUB, lanes))
+
+            x_radix([(row(s, 0), -row(s, 1)) for s in range(groups)], z, 0, turn_ref, lanes, SUB)
+            zc[:small, :] = data_table(z[:small, :], wx_ref)
+            for t in range(groups):
+                at = slice(t * SUB, (t + 1) * SUB)
+                cols = slice(t * lanes, (t + 1) * lanes)
+                zr, zi = zc[at, :lanes], zc[at, lanes:]
+                kr, ki = b_ref[0, :, cols], b_ref[1, :, cols]
+                top = slice(t * pair, t * pair + 1)
+                t_s[top, :lanes] += jnp.sum(zr * kr - zi * ki, axis=0, keepdims=True)
+                t_s[top, lanes:] += jnp.sum(zr * ki + zi * kr, axis=0, keepdims=True)
 
         zc[:block, :] = data_table(t_s[...], wxi_ref)
 
         def back(h, carry):
+            j = pl.program_id(0) * 2 + h
             for s, (re, im) in enumerate(x_unradix(zc, h * SUB, turn_ref, groups, lanes, pair)):
-                o_ref[s, h, 0] = re
-                o_ref[s, h, 1] = im
+                o_ref[s, j, 0] = re
+                o_ref[s, j, 1] = im
             return carry
 
         lax.fori_loop(0, 2, back, 0)
 
-    k_specs = [pl.BlockSpec((2, depth, pair, length), lambda j: (0, 0, j, 0)),
-               whole(2, depth, pair, length)]
-    one_spec = pl.BlockSpec((groups, 2, 2, SUB, lanes), lambda j: (0, j, 0, 0, 0))
-    all_spec = pl.BlockSpec((groups, depth, 2, 2, SUB, lanes), lambda j: (0, 0, j, 0, 0, 0))
+    k_specs = [pl.BlockSpec((2, depth, pair, length), lambda j: (0, 0, j, 0)), whole(2, SUB, length)]
     outgoing = pl.pallas_call(
         project_kernel,
         grid=(tiles // 2,),
-        in_specs=x_specs + [all_spec] + k_specs,
-        out_specs=one_spec,
-        out_shape=jax.ShapeDtypeStruct(send_shape, f32),
+        in_specs=x_specs + [near] + k_specs,
+        out_specs=near,
+        out_shape=pltpu.VMEM(send_shape, f32),
         scratch_shapes=[x_scratch(depth), x_scratch(1), x_scratch(depth)],
+        compiler_params=pltpu.CompilerParams(vmem_limit_bytes=24 << 20),
         name="project_x",
-    )(w_x, w_xi, turn, arrived, a_all, b_all)
+    )(*(far(t) for t in x_tables), keep(arrived), far(a_all), far(b_all))
     arrived = swap(outgoing)
 
     def ratio_kernel(wy_ref, w0_ref, turn_ref, g_ref, bg_ref, me_ref, p_ref, o_ref, z, q_s):
@@ -587,56 +602,62 @@
 
     projection, outgoing = pl.pallas_call(
         ratio_kernel,
-        out_shape=[jax.ShapeDtypeStruct((rows, length), f32), jax.ShapeDtypeStruct(send_shape, f32)],
+        in_specs=[near] * 3 + [near] * 3,
+        out_specs=[whole(rows, length), near],
+        out_shape=[jax.ShapeDtypeStruct((rows, length), f32), pltpu.VMEM(send_shape, f32)],
         scratch_shapes=[y_scratch, pltpu.VMEM((rows, length), f32)],
+        compiler_params=pltpu.CompilerParams(vmem_limit_bytes=16 << 20),
         name="ratio",
-    )(w_y, w_0, turn, arrived, background, measured)
+    )(*y_near, keep(arrived), keep(background), keep(measured))
     arrived = swap(outgoing)
 
     def correct_kernel(wx_ref, wxi_ref, turn_ref, s_ref, a_ref, b_ref, o_ref, z, zq, zc, c_s):
-        def gather(flipped, out):
-            def one(h, carry):
-                tile = []
-                for s in range(groups):
-                    re, im = s_ref[s, h, 0], s_ref[s, h, 1]
-                    tile.append((re, -im if flipped else im))
-                x_radix(tile, z, h * SUB, turn_ref, lanes, pair)
-                return carry
-
-            lax.fori_loop(0, 2, one, 0)
-            out[...] = data_table(z[...], wx_ref)
-
-        def multiply(k_ref, src, fresh):
-            for t in range(groups):
-                here = slice(t * pair, (t + 1) * pair)
-                cols = slice(t * lanes, (t + 1) * lanes)
-                zr, zi = src[here, :lanes], src[here, lanes:]
-                for d in range(depth):
-                    at = slice(d * block + t * pair, d * block + (t + 1) * pair)
-                    kr, ki = k_ref[0, d, :, cols], k_ref[1, d, :, cols]
-                    re, im = zr * kr + zi * ki, zi * kr - zr * ki
-                    if not fresh:
-                        re, im = re + c_s[at, :lanes], im + c_s[at, lanes:]
-                    c_s[at, :lanes] = re
-                    c_s[at, lanes:] = im
-
-        gather(False, zq)
-        multiply(a_ref, zq, True)
+        mine_rows = pl.ds(pl.multiple_of(pl.program_id(0) * pair, pair), pair)
+
+        def one(h, carry):
+            j = pl.program_id(0) * 2 + h
+            tile = [(s_ref[s, j, 0], s_ref[s, j, 1]) for s in range(groups)]
+            x_radix(tile, z, h * SUB, turn_ref, lanes, pair)
+            return carry
+
+        lax.fori_loop(0, 2, one, 0)
+        zq[...] = data_table(z[...], wx_ref)
+        for t in range(groups):
+            here = slice(t * pair, (t + 1) * pair)
+            cols = slice(t * lanes, (t + 1) * lanes)
+            zr, zi = zq[here, :lanes], zq[here, lanes:]
+            for d in range(depth):
+                at = slice(d * block + t * pair, d * block + (t + 1) * pair)
+                kr, ki = a_ref[0, d, mine_rows, cols], a_ref[1, d, mine_rows, cols]
+                c_s[at, :lanes] = zr * kr + zi * ki
+                c_s[at, lanes:] = zi * kr - zr * ki
 
         @pl.when(pl.program_id(0) == 0)
         def _():
-            gather(True, zq)
-            multiply(b_ref, zq, False)
+            tile = [(s_ref[s, 0, 0], -s_ref[s, 0, 1]) for s in range(groups)]
+            x_radix(tile, z, 0, turn_ref, lanes, SUB)
+            zq[:small, :] = data_table(z[:small, :], wx_ref)
+            for t in range(groups):
+                at = slice(t * SUB, t * SUB + 1)
+                cols = slice(t * lanes, (t + 1) * lanes)
+                zr, zi = zq[at, :lanes], zq[at, lanes:]
+                kr, ki = b_ref[0, :, cols], b_ref[1, :, cols]
+                re, im = zr * kr + zi * ki, zi * kr - zr * ki
+                for d in range(depth):
+                    top = slice(d * block + t * pair, d * block + t * pair + 1)
+                    c_s[top, :lanes] += re[d:d + 1, :]
+                    c_s[top, lanes:] += im[d:d + 1, :]
 
         for d in range(depth):
             zc[d * block:(d + 1) * block, :] = data_table(c_s[d * block:(d + 1) * block, :], wxi_ref)
 
         def back(i, carry):
             d, h = i // 2, i % 2
+            j = pl.program_id(0) * 2 + h
             out = x_unradix(zc, d * block + h * SUB, turn_ref, groups, lanes, pair)
             for s, (re, im) in enumerate(out):
-                o_ref[s, d, h, 0] = re
-                o_ref[s, d, h, 1] = im
+                o_ref[s, d, j, 0] = re
+                o_ref[s, d, j, 1] = im
             return carry
 
         lax.fori_loop(0, 2 * depth, back, 0)
@@ -644,36 +665,36 @@
     outgoing = pl.pallas_call(
         correct_kernel,
         grid=(tiles // 2,),
-        in_specs=x_specs + [one_spec] + k_specs,
-        out_specs=all_spec,
-        out_shape=jax.ShapeDtypeStruct(many(depth), f32),
+        in_specs=[near] * 6,
+        out_specs=near,
+        out_shape=pltpu.VMEM(many(depth), f32),
         scratch_shapes=[x_scratch(1), x_scratch(1), x_scratch(depth), x_scratch(depth)],
+        compiler_params=pltpu.CompilerParams(vmem_limit_bytes=24 << 20),
         name="correct_x",
-    )(w_x, w_xi, turn, arrived, a_all, b_all)
+    )(*x_near, keep(arrived), keep(a_all), keep(b_all))
     arrived = swap(outgoing)
 
     def final_kernel(wy_ref, w0_ref, turn_ref, g_ref, v_ref, o_ref, z):
         def fetch(t):
-            return g_ref[:, 0, t].reshape(groups * 2 * SUB, rows)
+            return g_ref[:, pl.program_id(0), t].reshape(groups * 2 * SUB, rows)
 
         def write(i, here, outs):
             for a, value in enumerate(outs):
                 cols = slice(a * lanes, (a + 1) * lanes)
-                o_ref[0, here, cols] = v_ref[0, here, cols] * value
+                o_ref[0, here, cols] = v_ref[pl.program_id(0), here, cols] * value
 
         y_inverse(fetch, write, z, wy_ref, w0_ref, turn_ref, groups, rows, lanes)
 
     new_volume = pl.pallas_call(
         final_kernel,
         grid=(depth,),
-        in_specs=y_specs + [
-            pl.BlockSpec((groups, 1, tiles, 2, SUB, lanes), lambda d: (0, d, 0, 0, 0, 0)),
-            pl.BlockSpec((1, rows, length), lambda d: (d, 0, 0))],
+        in_specs=[near] * 3 + [near, near],
         out_specs=pl.BlockSpec((1, rows, length), lambda d: (d, 0, 0)),
         out_shape=jax.ShapeDtypeStruct((depth, rows, length), f32),
         scratch_shapes=[y_scratch],
+        compiler_params=pltpu.CompilerParams(vmem_limit_bytes=16 << 20),
         name="final_y",
-    )(w_y, w_0, turn, arrived, volume)
+    )(*y_near, keep(arrived), keep(volume))
     return new_volume, projection
 
 

time: 359 us -> 338 us (0.942)
  Pallas kernels: 59.5 us -> 47.9 us
  local copies, waits for them, and re-layouts: 5.98 us -> 1.95 us
  waiting for transfers between devices: 143 us -> 139 us
    pallas_call x4, Pallas kernels: 28.9 us -> 19.4 us  [the longest x1 6.6 us: fast_shards(): pl.pallas_call(project_kernel, grid=(tiles // 2,), in_specs=x_specs + [ne...]
    unnamed x14 -> x24, local copies, waits for them, and re-layouts: 4.88 us -> 0.86 us
  transfers between devices with their start and end apart: 8 -> 8, of which waited for: 5 -> 5; matrix products, arithmetic and copies ran while one was open for 0% -> 1% of each run, Pallas kernels for 6% -> 8%
where the time goes in v3:
time: 338 us; the launch traced here: 336 us
  waiting for transfers between devices  139 us (41%)
  blocking collectives  134 us (40%)
  Pallas kernels  47.9 us (14%)
  starting transfers between devices  11.7 us (3%)
    all_to_all x3, blocking collectives, swap(): return lax.all_to_all(field, 'row', split_axis=0, concat_axis=0, tiled=True)  134 us
    ppermute x3, waiting for transfers between devices, fast_shards(): mine.append(lax.ppermute(send, 'row', flip))  127 us
    pallas_call x1, Pallas kernels, fast_shards(): pl.pallas_call(mix_kernel, grid=(groups // many_t,), in_specs=[smem, whol...  15.7 us
    ppermute x3, waiting for transfers between devices, fast_shards(): other.append(lax.ppermute(mine[d], 'vol', [(0, 1), (1, 0)]))  6.84 us
  transfers between devices with their start and end apart: 8, of which 5 were waited for; matrix products, arithmetic and copies ran while one was open for 1% of the time, Pallas kernels for 8%

profile of v3, /device:TPU:15, one launch (start us, length us, event | category | flops | bytes accessed | tf_op | source)
XLA Modules:
  0.0 336.4 jit_solution(2808041512484720474)
XLA Ops:
  0.6 2.1 pick.4
  2.7 1.8 collective-permute-start
  4.5 2.1 pick.3
  6.6 6.6 %forward_y.1 = f32[16,3,8,2,8,128]{5,4,3,2,1,0:T(8,128)} custom-call(bf16[2,256,256]{2,1,0:T(8,128)(2,1)} %constant.32.clone.wy_ref, bf16[2,256,256]{2,1,0:T(8,128)(2,1)} %constant.33.clone.w0_ref, f32[16,2,128]{2,1,0:T(2,128)} %constant.36.clone.turn_ref, f32[3,128,2048]{2,1,0:T(8,128)} %v_ref.2), custom_call_target="tpu_custom_call" | custom-call | tf_op jit(solution)/shard_map/forward_y/pallas_call | solution.py:494
  13.2 16.3 %collective-permute-done.rest_0_ = f32[64,2048]{1,0:T(8,128)S(1)} collective-permute-done((f32[64,2048]{1,0:T(8,128)}, f32[64,2048]{1,0:T(8,128)S(1)}, u32[]{:S(2)}, u32[]{:S(2)}) %collective-permute-start) | collective-permute-done | bytes 524320 | tf_op jit(solution)/shard_map/ppermute | solution.py:408
  29.5 0.8 copy-done.10
  30.3 5.2 %all-to-all-start = ((f32[16,3,8,2,8,128]{5,4,3,2,1,0:T(8,128)}), f32[16,3,8,2,8,128]{5,4,3,2,1,0:T(8,128)S(1)}, u32[]{:S(2)}, u32[]{:S(2)}) async-start(f32[16,3,8,2,8,128]{5,4,3,2,1,0:T(8,128)} %forward_y.1), calls=%async_computation | async-start | bytes 6291456 | tf_op jit(solution)/shard_map/all_to_all | solution.py:505
  35.6 2.1 pick.5
  37.6 1.5 collective-permute-start.2
  39.1 1.2 collective-permute-start.3
  40.3 0.3 collective-permute-start.4
  40.5 101.0 %collective-permute-done.2.rest_1_ = f32[64,2048]{1,0:T(8,128)} collective-permute-done((f32[64,2048]{1,0:T(8,128)}, f32[64,2048]{1,0:T(8,128)}, u32[]{:S(2)}, u32[]{:S(2)}) %collective-permute-start.2) | collective-permute-done | bytes 524320 | tf_op jit(solution)/shard_map/ppermute | solution.py:408
  141.5 0.3 collective-permute-start.5
  141.8 10.1 %collective-permute-done.3.rest_2_ = f32[64,2048]{1,0:T(8,128)} collective-permute-done((f32[64,2048]{1,0:T(8,128)}, f32[64,2048]{1,0:T(8,128)}, u32[]{:S(2)}, u32[]{:S(2)}) %collective-permute-start.3) | collective-permute-done | bytes 524320 | tf_op jit(solution)/shard_map/ppermute | solution.py:408
  151.9 0.3 collective-permute-start.6
  152.2 1.1 slice_reduce_fusion
  153.3 1.3 collective-permute-start.1
  154.6 0.7 pad_add_fusion.where_ref
  155.3 4.6 %collective-permute-done.1.edge_ref = f32[16,2048]{1,0:T(8,128)S(1)} collective-permute-done((f32[16,2048]{1,0:T(8,128)S(1)}, f32[16,2048]{1,0:T(8,128)S(1)}, u32[]{:S(2)}, u32[]{:S(2)}) %collective-permute-start.1) | collective-permute-done | bytes 131104 | tf_op jit(solution)/shard_map/ppermute | solution.py:413
  159.9 0.0 collective-permute-done.4.rest_3_
  159.9 0.0 collective-permute-done.5.rest_4_
  159.9 6.8 %collective-permute-done.6.rest_5_ = f32[64,2048]{1,0:T(8,128)} collective-permute-done((f32[64,2048]{1,0:T(8,128)}, f32[64,2048]{1,0:T(8,128)}, u32[]{:S(2)}, u32[]{:S(2)}) %collective-permute-start.6) | collective-permute-done | bytes 524320 | tf_op jit(solution)/shard_map/ppermute | solution.py:415
  166.7 0.0 copy-done.11
  166.7 15.7 %mix.1 = (f32[2,3,64,2048]{3,2,1,0:T(8,128)}, f32[2,8,2048]{2,1,0:T(8,128)}) custom-call(s32[3]{0:T(128)} %pad_add_fusion.where_ref, f32[64,128]{1,0:T(8,128)} %constant.38.clone.own_l_ref, f32[64,128]{1,0:T(8,128)} %constant.39.clone.own_h_ref, bf16[2,3,128,2048]{3,2,1,0:T(8,128)(2,1)} %psf_ref.7, f32[16,2048]{1,0:T(8,128)} %copy-done.11, ...), custom_call_target="tpu_custom_call" | custom-call | tf_op jit(solution)/shard_map/mix/pallas_call | solution.py:471
  182.5 0.0 all-to-all-done.s_ref
  182.5 0.0 copy-start.2
  182.5 0.0 copy-start.3
  182.5 0.0 copy-start.4
  182.5 0.0 copy-start.5
  182.5 0.0 copy-start.9
  182.5 6.6 %project_x.1 = f32[16,8,2,8,128]{4,3,2,1,0:T(8,128)S(1)} custom-call(bf16[2,256,256]{2,1,0:T(8,128)(2,1)} %constant.34.clone.wx_ref, bf16[2,256,256]{2,1,0:T(8,128)(2,1)} %constant.35.clone.wxi_ref, f32[16,2,128]{2,1,0:T(2,128)} %constant.36.clone.turn_ref, f32[16,3,8,2,8,128]{5,4,3,2,1,0:T(8,128)S(1)} %all-to-all-done.s_ref, ...), custom_call_target="tpu_custom_call" | custom-call | tf_op jit(solution)/shard_map/project_x/pallas_call | solution.py:571
  189.1 30.2 %all_to_all.20.g_ref = f32[16,8,2,8,128]{4,3,2,1,0:T(8,128)S(1)} all-to-all(f32[16,8,2,8,128]{4,3,2,1,0:T(8,128)S(1)} %project_x.1), channel_id=1, replica_groups=mesh['vol'=2,'row'=16] {'row'}, dimensions={0} | all-to-all | bytes 2097152 | tf_op jit(solution)/shard_map/all_to_all | solution.py:505
  219.4 0.0 copy-done.2
  219.4 0.0 copy-done.3
  219.4 0.0 copy-done.4
  219.4 0.0 copy-done.5
  219.4 0.0 copy-done.9
  219.4 0.0 copy-start.1
  219.4 0.0 copy-start.6
  219.4 0.0 copy-start.7
  219.4 0.0 copy-start.8
  219.4 3.4 %ratio.1 = (f32[128,2048]{1,0:T(8,128)}, f32[16,8,2,8,128]{4,3,2,1,0:T(8,128)S(1)}) custom-call(bf16[2,256,256]{2,1,0:T(8,128)(2,1)S(1)} %copy-done.3, bf16[2,256,256]{2,1,0:T(8,128)(2,1)S(1)} %copy-done.2, f32[16,2,128]{2,1,0:T(2,128)S(1)} %copy-done.9, f32[16,8,2,8,128]{4,3,2,1,0:T(8,128)S(1)} %all_to_all.20.g_ref, f32[128,2048]{1,0:T(8,128)S(1)} %copy-done.4, ...), custom_call_target="tpu_custom_call" | custom-call | tf_op jit(solution)/shard_map/ratio/pallas_call | solution.py:603
  222.8 29.5 %all_to_all.21.s_ref = f32[16,8,2,8,128]{4,3,2,1,0:T(8,128)S(1)} all-to-all(f32[16,8,2,8,128]{4,3,2,1,0:T(8,128)S(1)} %get-tuple-element.14), channel_id=1, replica_groups=mesh['vol'=2,'row'=16] {'row'}, dimensions={0} | all-to-all | bytes 2097152 | tf_op jit(solution)/shard_map/all_to_all | solution.py:505
  252.3 5.1 %correct_x.1 = f32[16,3,8,2,8,128]{5,4,3,2,1,0:T(8,128)S(1)} custom-call(bf16[2,256,256]{2,1,0:T(8,128)(2,1)S(1)} %copy-done.7, bf16[2,256,256]{2,1,0:T(8,128)(2,1)S(1)} %copy-done.6, f32[16,2,128]{2,1,0:T(2,128)S(1)} %copy-done.9, f32[16,8,2,8,128]{4,3,2,1,0:T(8,128)S(1)} %all_to_all.21.s_ref, f32[2,3,64,2048]{3,2,1,0:T(8,128)S(1)} %copy-done.1, ...), custom_call_target="tpu_custom_call" | custom-call | tf_op jit(solution)/shard_map/correct_x/pallas_call | solution.py:665
  257.5 0.0 copy-start
  257.5 74.7 %all_to_all.22.g_ref = f32[16,3,8,2,8,128]{5,4,3,2,1,0:T(8,128)S(1)} all-to-all(f32[16,3,8,2,8,128]{5,4,3,2,1,0:T(8,128)S(1)} %correct_x.1), channel_id=1, replica_groups=mesh['vol'=2,'row'=16] {'row'}, dimensions={0} | all-to-all | bytes 6291456 | tf_op jit(solution)/shard_map/all_to_all | solution.py:505
  332.2 0.0 copy-done
  332.2 4.3 %final_y.1 = f32[3,128,2048]{2,1,0:T(8,128)} custom-call(bf16[2,256,256]{2,1,0:T(8,128)(2,1)S(1)} %copy-done.3, bf16[2,256,256]{2,1,0:T(8,128)(2,1)S(1)} %copy-done.2, f32[16,2,128]{2,1,0:T(2,128)S(1)} %copy-done.9, f32[16,3,8,2,8,128]{5,4,3,2,1,0:T(8,128)S(1)} %all_to_all.22.g_ref, f32[3,128,2048]{2,1,0:T(8,128)S(1)} %copy-done), custom_call_target="tpu_custom_call" | custom-call | tf_op jit(solution)/shard_map/final_y/pallas_call | solution.py:688
  (8 shorter events, 0.0 us)
Async XLA Ops:
  2.7 26.8 %collective-permute-start = (f32[64,2048]{1,0:T(8,128)}, f32[64,2048]{1,0:T(8,128)S(1)}, u32[]{:S(2)}, u32[]{:S(2)}) collective-permute-start(f32[64,2048]{1,0:T(8,128)} %pick.4), channel_id=1, source_target_pairs={{0,15},{1,14},{2,13},{3,12},{4,11},{5,10},{6,9},{7,8},{8,7},{9,6},... | collective-permute-start | bytes 1572872 | tf_op jit(solution)/shard_map/ppermute | solution.py:408
  29.5 0.8 copy-start.10
  30.3 152.1 %all-to-all-start = ((f32[16,3,8,2,8,128]{5,4,3,2,1,0:T(8,128)}), f32[16,3,8,2,8,128]{5,4,3,2,1,0:T(8,128)S(1)}, u32[]{:S(2)}, u32[]{:S(2)}) async-start(f32[16,3,8,2,8,128]{5,4,3,2,1,0:T(8,128)} %forward_y.1), calls=%async_computation | async-start | bytes 6291456 | tf_op jit(solution)/shard_map/all_to_all | solution.py:505
  37.6 103.9 %collective-permute-start.2 = (f32[64,2048]{1,0:T(8,128)}, f32[64,2048]{1,0:T(8,128)}, u32[]{:S(2)}, u32[]{:S(2)}) collective-permute-start(f32[64,2048]{1,0:T(8,128)} %pick.5), channel_id=1, source_target_pairs={{0,15},{1,14},{2,13},{3,12},{4,11},{5,10},{6,9},{7,8},{8,7},{9,6},... | collective-permute-start | bytes 1572872 | tf_op jit(solution)/shard_map/ppermute | solution.py:408
  39.1 112.8 %collective-permute-start.3 = (f32[64,2048]{1,0:T(8,128)}, f32[64,2048]{1,0:T(8,128)}, u32[]{:S(2)}, u32[]{:S(2)}) collective-permute-start(f32[64,2048]{1,0:T(8,128)} %pick.3), channel_id=1, source_target_pairs={{0,15},{1,14},{2,13},{3,12},{4,11},{5,10},{6,9},{7,8},{8,7},{9,6},... | collective-permute-start | bytes 1572872 | tf_op jit(solution)/shard_map/ppermute | solution.py:408
  40.3 119.6 %collective-permute-start.4 = (f32[64,2048]{1,0:T(8,128)}, f32[64,2048]{1,0:T(8,128)}, u32[]{:S(2)}, u32[]{:S(2)}) collective-permute-start(f32[64,2048]{1,0:T(8,128)} %copy-done.10), channel_id=1, source_target_pairs={{0,16},{16,0},{1,17},{17,1},{2,18},{18,2},{3,19},{19,3},{4,20},{20... | collective-permute-start | bytes 1572872 | tf_op jit(solution)/shard_map/ppermute | solution.py:415
  141.5 18.4 %collective-permute-start.5 = (f32[64,2048]{1,0:T(8,128)}, f32[64,2048]{1,0:T(8,128)}, u32[]{:S(2)}, u32[]{:S(2)}) collective-permute-start(f32[64,2048]{1,0:T(8,128)} %collective-permute-done.2.rest_1_), channel_id=1, source_target_pairs={{0,16},{16,0},{1,17},{17,1},{2,18},{18,2},{3,19},{19,3},{4,20},{20... | collective-permute-start | bytes 1572872 | tf_op jit(solution)/shard_map/ppermute | solution.py:415
  151.9 14.8 %collective-permute-start.6 = (f32[64,2048]{1,0:T(8,128)}, f32[64,2048]{1,0:T(8,128)}, u32[]{:S(2)}, u32[]{:S(2)}) collective-permute-start(f32[64,2048]{1,0:T(8,128)} %collective-permute-done.3.rest_2_), channel_id=1, source_target_pairs={{0,16},{16,0},{1,17},{17,1},{2,18},{18,2},{3,19},{19,3},{4,20},{20... | collective-permute-start | bytes 1572872 | tf_op jit(solution)/shard_map/ppermute | solution.py:415
  153.3 6.6 %collective-permute-start.1 = (f32[16,2048]{1,0:T(8,128)S(1)}, f32[16,2048]{1,0:T(8,128)S(1)}, u32[]{:S(2)}, u32[]{:S(2)}) collective-permute-start(f32[16,2048]{1,0:T(8,128)S(1)} %pad_convert_fusion), channel_id=1, source_target_pairs={{15,1},{14,2},{13,3},{12,4},{11,5},{10,6},{9,7},{8,0},{31,17},{30,... | collective-permute-start | bytes 393224 | tf_op jit(solution)/shard_map/ppermute | solution.py:413
  159.9 6.8 %copy-start.11 = (f32[16,2048]{1,0:T(8,128)}, f32[16,2048]{1,0:T(8,128)S(1)}, u32[]{:S(2)}) copy-start(f32[16,2048]{1,0:T(8,128)S(1)} %collective-permute-done.1.edge_ref) | copy-start | bytes 393220
  182.5 36.9 %copy-start.2 = (bf16[2,256,256]{2,1,0:T(8,128)(2,1)S(1)}, bf16[2,256,256]{2,1,0:T(8,128)(2,1)}, u32[]{:S(2)}) copy-start(bf16[2,256,256]{2,1,0:T(8,128)(2,1)} %constant.33.clone.w0_ref) | copy-start | bytes 786436
  182.5 36.9 %copy-start.3 = (bf16[2,256,256]{2,1,0:T(8,128)(2,1)S(1)}, bf16[2,256,256]{2,1,0:T(8,128)(2,1)}, u32[]{:S(2)}) copy-start(bf16[2,256,256]{2,1,0:T(8,128)(2,1)} %constant.32.clone.wy_ref) | copy-start | bytes 786436
  182.5 36.9 %copy-start.4 = (f32[128,2048]{1,0:T(8,128)S(1)}, f32[128,2048]{1,0:T(8,128)}, u32[]{:S(2)}) copy-start(f32[128,2048]{1,0:T(8,128)} %bg_ref.1) | copy-start | bytes 3145732
  182.5 36.9 %copy-start.5 = (f32[128,2048]{1,0:T(8,128)S(1)}, f32[128,2048]{1,0:T(8,128)}, u32[]{:S(2)}) copy-start(f32[128,2048]{1,0:T(8,128)} %me_ref.1) | copy-start | bytes 3145732
  182.5 36.9 %copy-start.9 = (f32[16,2,128]{2,1,0:T(2,128)S(1)}, f32[16,2,128]{2,1,0:T(2,128)}, u32[]{:S(2)}) copy-start(f32[16,2,128]{2,1,0:T(2,128)} %constant.36.clone.turn_ref) | copy-start | bytes 49156
  219.4 32.9 %copy-start.1 = (f32[2,3,64,2048]{3,2,1,0:T(8,128)S(1)}, f32[2,3,64,2048]{3,2,1,0:T(8,128)}, u32[]{:S(2)}) copy-start(f32[2,3,64,2048]{3,2,1,0:T(8,128)} %get-tuple-element.12.a_ref) | copy-start | bytes 9437188
  219.4 32.9 %copy-start.6 = (bf16[2,256,256]{2,1,0:T(8,128)(2,1)S(1)}, bf16[2,256,256]{2,1,0:T(8,128)(2,1)}, u32[]{:S(2)}) copy-start(bf16[2,256,256]{2,1,0:T(8,128)(2,1)} %constant.35.clone.wxi_ref) | copy-start | bytes 786436
  219.4 32.9 %copy-start.7 = (bf16[2,256,256]{2,1,0:T(8,128)(2,1)S(1)}, bf16[2,256,256]{2,1,0:T(8,128)(2,1)}, u32[]{:S(2)}) copy-start(bf16[2,256,256]{2,1,0:T(8,128)(2,1)} %constant.34.clone.wx_ref) | copy-start | bytes 786436
  219.4 32.9 %copy-start.8 = (f32[2,8,2048]{2,1,0:T(8,128)S(1)}, f32[2,8,2048]{2,1,0:T(8,128)}, u32[]{:S(2)}) copy-start(f32[2,8,2048]{2,1,0:T(8,128)} %get-tuple-element.13.b_ref) | copy-start | bytes 393220
  257.5 74.7 %copy-start = (f32[3,128,2048]{2,1,0:T(8,128)S(1)}, f32[3,128,2048]{2,1,0:T(8,128)}, u32[]{:S(2)}) copy-start(f32[3,128,2048]{2,1,0:T(8,128)} %v_ref.2) | copy-start | bytes 9437188

commit v4 on v3

--- a/solution.py
+++ b/solution.py
@@ -237,13 +237,8 @@
     w_x = np.block([[np.cos(ang), -np.sin(ang)], [np.sin(ang), np.cos(ang)]])
     ang = 2.0 * np.pi * (np.arange(groups)[:, None] * pos[None, :] % length) / length
     turn = np.stack([np.cos(ang), -np.sin(ang)], axis=1).astype(np.float32)
-    return (
-        split_table(w_y.reshape(rows, 2 * lanes)),
-        split_table(w_0.reshape(rows, 2 * lanes)),
-        split_table(w_x),
-        split_table(w_x.T),
-        turn,
-    )
+    w_y, w_0 = split_table(w_y.reshape(rows, 2 * lanes)), split_table(w_0.reshape(rows, 2 * lanes))
+    return w_y, w_0, split_table(w_x), split_table(w_x.T), turn
 
 
 def kept_rows(groups, lanes):
@@ -278,17 +273,21 @@
     return mm(table[0], high, NT) + (mm(table[0], low, NT) + mm(table[1], high, NT))
 
 
+def y_store(xs, z, here, turn, groups, lanes):
+    out = rfft(xs)
+    z[0, here, :lanes] = out[0][0]
+    z[0, here, lanes:] = out[groups // 2][0]
+    for t in range(1, groups // 2):
+        re, im = out[t]
+        c, s = turn[t, 0:1, :], turn[t, 1:2, :]
+        z[t, here, :lanes] = re * c - im * s
+        z[t, here, lanes:] = re * s + im * c
+
+
 def y_forward(read, emit, z, w_y, w_0, turn, groups, rows, lanes):
     def chunk(i, carry):
-        out = rfft([read(i, a) for a in range(groups)])
         here = pl.ds(pl.multiple_of(i * SUB, SUB), SUB)
-        z[0, here, :lanes] = out[0][0]
-        z[0, here, lanes:] = out[groups // 2][0]
-        for t in range(1, groups // 2):
-            re, im = out[t]
-            c, s = turn[t, 0:1, :], turn[t, 1:2, :]
-            z[t, here, :lanes] = re * c - im * s
-            z[t, here, lanes:] = re * s + im * c
+        y_store([read(i, a) for a in range(groups)], z, here, turn, groups, lanes)
         return carry
 
     lax.fori_loop(0, rows // SUB, chunk, 0)
@@ -316,7 +315,7 @@
 
 def x_radix(tile, z, base, turn, lanes, step):
     for t, (re, im) in enumerate(cfft(tile, -1.0)):
-        here = pl.ds(pl.multiple_of(base + t * step, SUB), SUB)
+        here = slice(base + t * step, base + t * step + SUB)
         if t == 0:
             z[here, :lanes] = re
             z[here, lanes:] = im
@@ -329,7 +328,7 @@
 def x_unradix(z, base, turn, groups, lanes, step):
     zs = []
     for t in range(groups):
-        here = pl.ds(pl.multiple_of(base + t * step, SUB), SUB)
+        here = slice(base + t * step, base + t * step + SUB)
         re, im = z[here, :lanes], z[here, lanes:]
         if t:
             c, s = turn[t, 0:1, :], turn[t, 1:2, :]
@@ -361,7 +360,7 @@
         return pltpu.with_memory_space_constraint(x, pltpu.HBM)
 
     y_tables, x_tables = (w_y, w_0, turn), (w_x, w_xi, turn)
-    y_near = tuple(keep(t) for t in y_tables)
+    y_near = tuple(keep(t) for t in (w_y, w_0, turn))
     x_near = tuple(keep(t) for t in x_tables)
     y_specs = [whole(*t.shape) for t in y_tables]
     x_specs = [whole(*t.shape) for t in x_tables]
@@ -514,15 +513,11 @@
     lead = lambda: lax.broadcasted_iota(jnp.int32, (SUB, lanes), 0)
 
     def project_kernel(wx_ref, wxi_ref, turn_ref, s_ref, a_ref, b_ref, o_ref, z, t_s, zc):
-        def one(i, carry):
-            d, h = i // 2, i % 2
-            j = pl.program_id(0) * 2 + h
-            tile = [(s_ref[s, d, j, 0], s_ref[s, d, j, 1]) for s in range(groups)]
-            x_radix(tile, z, d * block + h * SUB, turn_ref, lanes, pair)
-            return carry
-
-        lax.fori_loop(0, 2 * depth, one, 0)
         for d in range(depth):
+            for h in range(2):
+                j = pl.program_id(0) * 2 + h
+                tile = [(s_ref[s, d, j, 0], s_ref[s, d, j, 1]) for s in range(groups)]
+                x_radix(tile, z, d * block + h * SUB, turn_ref, lanes, pair)
             zc[d * block:(d + 1) * block, :] = data_table(z[d * block:(d + 1) * block, :], wx_ref)
         for t in range(groups):
             here = slice(t * pair, (t + 1) * pair)
@@ -558,14 +553,11 @@
 
         zc[:block, :] = data_table(t_s[...], wxi_ref)
 
-        def back(h, carry):
+        for h in range(2):
             j = pl.program_id(0) * 2 + h
             for s, (re, im) in enumerate(x_unradix(zc, h * SUB, turn_ref, groups, lanes, pair)):
                 o_ref[s, j, 0] = re
                 o_ref[s, j, 1] = im
-            return carry
-
-        lax.fori_loop(0, 2, back, 0)
 
     k_specs = [pl.BlockSpec((2, depth, pair, length), lambda j: (0, 0, j, 0)), whole(2, SUB, length)]
     outgoing = pl.pallas_call(
@@ -580,32 +572,29 @@
     )(*(far(t) for t in x_tables), keep(arrived), far(a_all), far(b_all))
     arrived = swap(outgoing)
 
-    def ratio_kernel(wy_ref, w0_ref, turn_ref, g_ref, bg_ref, me_ref, p_ref, o_ref, z, q_s):
+    def ratio_kernel(wy_ref, w0_ref, turn_ref, g_ref, bg_ref, me_ref, p_ref, o_ref, z):
         def fetch(t):
             return g_ref[:, t].reshape(groups * 2 * SUB, rows)
 
         def write(i, here, outs):
+            ratio = []
             for a, value in enumerate(outs):
                 cols = slice(a * lanes, (a + 1) * lanes)
                 p_ref[here, cols] = value
-                q_s[here, cols] = me_ref[here, cols] / jnp.maximum(value + bg_ref[here, cols], FLOOR)
+                ratio.append(me_ref[here, cols] / jnp.maximum(value + bg_ref[here, cols], FLOOR))
+            y_store(ratio, z, here, turn_ref, groups, lanes)
 
         y_inverse(fetch, write, z, wy_ref, w0_ref, turn_ref, groups, rows, lanes)
-
-        def read(i, a):
-            return q_s[pl.ds(pl.multiple_of(i * SUB, SUB), SUB), a * lanes:(a + 1) * lanes]
-
-        def emit(t, out):
+        for t in range(tiles):
+            out = table_data(w0_ref if t == 0 else wy_ref, z[t])
             o_ref[:, t] = out.reshape(groups, 2, SUB, rows)
-
-        y_forward(read, emit, z, wy_ref, w0_ref, turn_ref, groups, rows, lanes)
 
     projection, outgoing = pl.pallas_call(
         ratio_kernel,
-        in_specs=[near] * 3 + [near] * 3,
+        in_specs=[near] * 6,
         out_specs=[whole(rows, length), near],
         out_shape=[jax.ShapeDtypeStruct((rows, length), f32), pltpu.VMEM(send_shape, f32)],
-        scratch_shapes=[y_scratch, pltpu.VMEM((rows, length), f32)],
+        scratch_shapes=[y_scratch],
         compiler_params=pltpu.CompilerParams(vmem_limit_bytes=16 << 20),
         name="ratio",
     )(*y_near, keep(arrived), keep(background), keep(measured))
@@ -614,13 +603,10 @@
     def correct_kernel(wx_ref, wxi_ref, turn_ref, s_ref, a_ref, b_ref, o_ref, z, zq, zc, c_s):
         mine_rows = pl.ds(pl.multiple_of(pl.program_id(0) * pair, pair), pair)
 
-        def one(h, carry):
+        for h in range(2):
             j = pl.program_id(0) * 2 + h
             tile = [(s_ref[s, j, 0], s_ref[s, j, 1]) for s in range(groups)]
             x_radix(tile, z, h * SUB, turn_ref, lanes, pair)
-            return carry
-
-        lax.fori_loop(0, 2, one, 0)
         zq[...] = data_table(z[...], wx_ref)
         for t in range(groups):
             here = slice(t * pair, (t + 1) * pair)
@@ -650,17 +636,12 @@
 
         for d in range(depth):
             zc[d * block:(d + 1) * block, :] = data_table(c_s[d * block:(d + 1) * block, :], wxi_ref)
-
-        def back(i, carry):
-            d, h = i // 2, i % 2
-            j = pl.program_id(0) * 2 + h
-            out = x_unradix(zc, d * block + h * SUB, turn_ref, groups, lanes, pair)
-            for s, (re, im) in enumerate(out):
-                o_ref[s, d, j, 0] = re
-                o_ref[s, d, j, 1] = im
-            return carry
-
-        lax.fori_loop(0, 2 * depth, back, 0)
+            for h in range(2):
+                j = pl.program_id(0) * 2 + h
+                out = x_unradix(zc, d * block + h * SUB, turn_ref, groups, lanes, pair)
+                for s, (re, im) in enumerate(out):
+                    o_ref[s, d, j, 0] = re
+                    o_ref[s, d, j, 1] = im
 
     outgoing = pl.pallas_call(
         correct_kernel,

time: 338 us -> 337 us (level)
  no operation moved by 1% of the time
where the time goes in v4:
time: 337 us; the launch traced here: 335 us
  waiting for transfers between devices  139 us (41%)
  blocking collectives  134 us (40%)
  Pallas kernels  46.3 us (14%)
  starting transfers between devices  11.7 us (3%)
    all_to_all x3, blocking collectives, swap(): return lax.all_to_all(field, 'row', split_axis=0, concat_axis=0, tiled=True)  134 us
    ppermute x3, waiting for transfers between devices, fast_shards(): mine.append(lax.ppermute(send, 'row', flip))  127 us
    pallas_call x1, Pallas kernels, fast_shards(): pl.pallas_call(mix_kernel, grid=(groups // many_t,), in_specs=[smem, whol...  15.7 us
    ppermute x3, waiting for transfers between devices, fast_shards(): other.append(lax.ppermute(mine[d], 'vol', [(0, 1), (1, 0)]))  6.84 us
  transfers between devices with their start and end apart: 8, of which 5 were waited for; matrix products, arithmetic and copies ran while one was open for 1% of the time, Pallas kernels for 8%

profile of v4, /device:TPU:15, one launch (start us, length us, event | category | flops | bytes accessed | tf_op | source)
XLA Modules:
  0.0 334.8 jit_solution(10252415568542063178)
XLA Ops:
  0.6 2.1 pick.4
  2.7 1.8 collective-permute-start
  4.5 2.1 pick.3
  6.6 6.6 %forward_y.1 = f32[16,3,8,2,8,128]{5,4,3,2,1,0:T(8,128)} custom-call(bf16[2,256,256]{2,1,0:T(8,128)(2,1)} %constant.32.clone.wy_ref, bf16[2,256,256]{2,1,0:T(8,128)(2,1)} %constant.33.clone.w0_ref, f32[16,2,128]{2,1,0:T(2,128)} %constant.36.clone.turn_ref, f32[3,128,2048]{2,1,0:T(8,128)} %v_ref.2), custom_call_target="tpu_custom_call" | custom-call | tf_op jit(solution)/shard_map/forward_y/pallas_call | solution.py:493
  13.2 16.3 %collective-permute-done.rest_0_ = f32[64,2048]{1,0:T(8,128)S(1)} collective-permute-done((f32[64,2048]{1,0:T(8,128)}, f32[64,2048]{1,0:T(8,128)S(1)}, u32[]{:S(2)}, u32[]{:S(2)}) %collective-permute-start) | collective-permute-done | bytes 524320 | tf_op jit(solution)/shard_map/ppermute | solution.py:407
  29.5 0.8 copy-done.10
  30.3 5.2 %all-to-all-start = ((f32[16,3,8,2,8,128]{5,4,3,2,1,0:T(8,128)}), f32[16,3,8,2,8,128]{5,4,3,2,1,0:T(8,128)S(1)}, u32[]{:S(2)}, u32[]{:S(2)}) async-start(f32[16,3,8,2,8,128]{5,4,3,2,1,0:T(8,128)} %forward_y.1), calls=%async_computation | async-start | bytes 6291456 | tf_op jit(solution)/shard_map/all_to_all | solution.py:504
  35.6 2.1 pick.5
  37.6 1.5 collective-permute-start.2
  39.1 1.2 collective-permute-start.3
  40.3 0.3 collective-permute-start.4
  40.5 101.0 %collective-permute-done.2.rest_1_ = f32[64,2048]{1,0:T(8,128)} collective-permute-done((f32[64,2048]{1,0:T(8,128)}, f32[64,2048]{1,0:T(8,128)}, u32[]{:S(2)}, u32[]{:S(2)}) %collective-permute-start.2) | collective-permute-done | bytes 524320 | tf_op jit(solution)/shard_map/ppermute | solution.py:407
  141.5 0.3 collective-permute-start.5
  141.8 10.1 %collective-permute-done.3.rest_2_ = f32[64,2048]{1,0:T(8,128)} collective-permute-done((f32[64,2048]{1,0:T(8,128)}, f32[64,2048]{1,0:T(8,128)}, u32[]{:S(2)}, u32[]{:S(2)}) %collective-permute-start.3) | collective-permute-done | bytes 524320 | tf_op jit(solution)/shard_map/ppermute | solution.py:407
  151.9 0.3 collective-permute-start.6
  152.2 1.1 slice_reduce_fusion
  153.3 1.3 collective-permute-start.1
  154.6 0.7 pad_add_fusion.where_ref
  155.3 4.6 %collective-permute-done.1.edge_ref = f32[16,2048]{1,0:T(8,128)S(1)} collective-permute-done((f32[16,2048]{1,0:T(8,128)S(1)}, f32[16,2048]{1,0:T(8,128)S(1)}, u32[]{:S(2)}, u32[]{:S(2)}) %collective-permute-start.1) | collective-permute-done | bytes 131104 | tf_op jit(solution)/shard_map/ppermute | solution.py:412
  159.9 0.0 collective-permute-done.4.rest_3_
  159.9 0.0 collective-permute-done.5.rest_4_
  159.9 6.8 %collective-permute-done.6.rest_5_ = f32[64,2048]{1,0:T(8,128)} collective-permute-done((f32[64,2048]{1,0:T(8,128)}, f32[64,2048]{1,0:T(8,128)}, u32[]{:S(2)}, u32[]{:S(2)}) %collective-permute-start.6) | collective-permute-done | bytes 524320 | tf_op jit(solution)/shard_map/ppermute | solution.py:414
  166.7 0.0 copy-done.11
  166.7 15.7 %mix.1 = (f32[2,3,64,2048]{3,2,1,0:T(8,128)}, f32[2,8,2048]{2,1,0:T(8,128)}) custom-call(s32[3]{0:T(128)} %pad_add_fusion.where_ref, f32[64,128]{1,0:T(8,128)} %constant.38.clone.own_l_ref, f32[64,128]{1,0:T(8,128)} %constant.39.clone.own_h_ref, bf16[2,3,128,2048]{3,2,1,0:T(8,128)(2,1)} %psf_ref.7, f32[16,2048]{1,0:T(8,128)} %copy-done.11, ...), custom_call_target="tpu_custom_call" | custom-call | tf_op jit(solution)/shard_map/mix/pallas_call | solution.py:470
  182.5 0.0 all-to-all-done.s_ref
  182.5 0.0 copy-start.2
  182.5 0.0 copy-start.3
  182.5 0.0 copy-start.4
  182.5 0.0 copy-start.5
  182.5 0.0 copy-start.9
  182.5 5.9 %project_x.1 = f32[16,8,2,8,128]{4,3,2,1,0:T(8,128)S(1)} custom-call(bf16[2,256,256]{2,1,0:T(8,128)(2,1)} %constant.34.clone.wx_ref, bf16[2,256,256]{2,1,0:T(8,128)(2,1)} %constant.35.clone.wxi_ref, f32[16,2,128]{2,1,0:T(2,128)} %constant.36.clone.turn_ref, f32[16,3,8,2,8,128]{5,4,3,2,1,0:T(8,128)S(1)} %all-to-all-done.s_ref, ...), custom_call_target="tpu_custom_call" | custom-call | tf_op jit(solution)/shard_map/project_x/pallas_call | solution.py:563
  188.4 30.2 %all_to_all.20.g_ref = f32[16,8,2,8,128]{4,3,2,1,0:T(8,128)S(1)} all-to-all(f32[16,8,2,8,128]{4,3,2,1,0:T(8,128)S(1)} %project_x.1), channel_id=1, replica_groups=mesh['vol'=2,'row'=16] {'row'}, dimensions={0} | all-to-all | bytes 2097152 | tf_op jit(solution)/shard_map/all_to_all | solution.py:504
  218.6 0.0 copy-done.2
  218.6 0.0 copy-done.3
  218.6 0.0 copy-done.4
  218.7 0.0 copy-done.5
  218.7 0.0 copy-done.9
  218.7 0.0 copy-start.1
  218.7 0.0 copy-start.6
  218.7 0.0 copy-start.7
  218.7 0.0 copy-start.8
  218.7 3.3 ratio.1
  222.0 29.5 %all_to_all.21.s_ref = f32[16,8,2,8,128]{4,3,2,1,0:T(8,128)S(1)} all-to-all(f32[16,8,2,8,128]{4,3,2,1,0:T(8,128)S(1)} %get-tuple-element.14), channel_id=1, replica_groups=mesh['vol'=2,'row'=16] {'row'}, dimensions={0} | all-to-all | bytes 2097152 | tf_op jit(solution)/shard_map/all_to_all | solution.py:504
  251.5 0.0 copy-done.1
  251.5 4.3 %correct_x.1 = f32[16,3,8,2,8,128]{5,4,3,2,1,0:T(8,128)S(1)} custom-call(bf16[2,256,256]{2,1,0:T(8,128)(2,1)S(1)} %copy-done.7, bf16[2,256,256]{2,1,0:T(8,128)(2,1)S(1)} %copy-done.6, f32[16,2,128]{2,1,0:T(2,128)S(1)} %copy-done.9, f32[16,8,2,8,128]{4,3,2,1,0:T(8,128)S(1)} %all_to_all.21.s_ref, f32[2,3,64,2048]{3,2,1,0:T(8,128)S(1)} %copy-done.1, ...), custom_call_target="tpu_custom_call" | custom-call | tf_op jit(solution)/shard_map/correct_x/pallas_call | solution.py:646
  255.8 0.0 copy-start
  255.8 74.7 %all_to_all.22.g_ref = f32[16,3,8,2,8,128]{5,4,3,2,1,0:T(8,128)S(1)} all-to-all(f32[16,3,8,2,8,128]{5,4,3,2,1,0:T(8,128)S(1)} %correct_x.1), channel_id=1, replica_groups=mesh['vol'=2,'row'=16] {'row'}, dimensions={0} | all-to-all | bytes 6291456 | tf_op jit(solution)/shard_map/all_to_all | solution.py:504
  330.6 4.3 %final_y.1 = f32[3,128,2048]{2,1,0:T(8,128)} custom-call(bf16[2,256,256]{2,1,0:T(8,128)(2,1)S(1)} %copy-done.3, bf16[2,256,256]{2,1,0:T(8,128)(2,1)S(1)} %copy-done.2, f32[16,2,128]{2,1,0:T(2,128)S(1)} %copy-done.9, f32[16,3,8,2,8,128]{5,4,3,2,1,0:T(8,128)S(1)} %all_to_all.22.g_ref, f32[3,128,2048]{2,1,0:T(8,128)S(1)} %copy-done), custom_call_target="tpu_custom_call" | custom-call | tf_op jit(solution)/shard_map/final_y/pallas_call | solution.py:669
  (8 shorter events, 0.0 us)
Async XLA Ops:
  2.7 26.8 %collective-permute-start = (f32[64,2048]{1,0:T(8,128)}, f32[64,2048]{1,0:T(8,128)S(1)}, u32[]{:S(2)}, u32[]{:S(2)}) collective-permute-start(f32[64,2048]{1,0:T(8,128)} %pick.4), channel_id=1, source_target_pairs={{0,15},{1,14},{2,13},{3,12},{4,11},{5,10},{6,9},{7,8},{8,7},{9,6},... | collective-permute-start | bytes 1572872 | tf_op jit(solution)/shard_map/ppermute | solution.py:407
  29.5 0.8 copy-start.10
  30.3 152.1 %all-to-all-start = ((f32[16,3,8,2,8,128]{5,4,3,2,1,0:T(8,128)}), f32[16,3,8,2,8,128]{5,4,3,2,1,0:T(8,128)S(1)}, u32[]{:S(2)}, u32[]{:S(2)}) async-start(f32[16,3,8,2,8,128]{5,4,3,2,1,0:T(8,128)} %forward_y.1), calls=%async_computation | async-start | bytes 6291456 | tf_op jit(solution)/shard_map/all_to_all | solution.py:504
  37.6 103.9 %collective-permute-start.2 = (f32[64,2048]{1,0:T(8,128)}, f32[64,2048]{1,0:T(8,128)}, u32[]{:S(2)}, u32[]{:S(2)}) collective-permute-start(f32[64,2048]{1,0:T(8,128)} %pick.5), channel_id=1, source_target_pairs={{0,15},{1,14},{2,13},{3,12},{4,11},{5,10},{6,9},{7,8},{8,7},{9,6},... | collective-permute-start | bytes 1572872 | tf_op jit(solution)/shard_map/ppermute | solution.py:407
  39.1 112.8 %collective-permute-start.3 = (f32[64,2048]{1,0:T(8,128)}, f32[64,2048]{1,0:T(8,128)}, u32[]{:S(2)}, u32[]{:S(2)}) collective-permute-start(f32[64,2048]{1,0:T(8,128)} %pick.3), channel_id=1, source_target_pairs={{0,15},{1,14},{2,13},{3,12},{4,11},{5,10},{6,9},{7,8},{8,7},{9,6},... | collective-permute-start | bytes 1572872 | tf_op jit(solution)/shard_map/ppermute | solution.py:407
  40.3 119.6 %collective-permute-start.4 = (f32[64,2048]{1,0:T(8,128)}, f32[64,2048]{1,0:T(8,128)}, u32[]{:S(2)}, u32[]{:S(2)}) collective-permute-start(f32[64,2048]{1,0:T(8,128)} %copy-done.10), channel_id=1, source_target_pairs={{0,16},{16,0},{1,17},{17,1},{2,18},{18,2},{3,19},{19,3},{4,20},{20... | collective-permute-start | bytes 1572872 | tf_op jit(solution)/shard_map/ppermute | solution.py:414
  141.5 18.4 %collective-permute-start.5 = (f32[64,2048]{1,0:T(8,128)}, f32[64,2048]{1,0:T(8,128)}, u32[]{:S(2)}, u32[]{:S(2)}) collective-permute-start(f32[64,2048]{1,0:T(8,128)} %collective-permute-done.2.rest_1_), channel_id=1, source_target_pairs={{0,16},{16,0},{1,17},{17,1},{2,18},{18,2},{3,19},{19,3},{4,20},{20... | collective-permute-start | bytes 1572872 | tf_op jit(solution)/shard_map/ppermute | solution.py:414
  151.9 14.8 %collective-permute-start.6 = (f32[64,2048]{1,0:T(8,128)}, f32[64,2048]{1,0:T(8,128)}, u32[]{:S(2)}, u32[]{:S(2)}) collective-permute-start(f32[64,2048]{1,0:T(8,128)} %collective-permute-done.3.rest_2_), channel_id=1, source_target_pairs={{0,16},{16,0},{1,17},{17,1},{2,18},{18,2},{3,19},{19,3},{4,20},{20... | collective-permute-start | bytes 1572872 | tf_op jit(solution)/shard_map/ppermute | solution.py:414
  153.3 6.6 %collective-permute-start.1 = (f32[16,2048]{1,0:T(8,128)S(1)}, f32[16,2048]{1,0:T(8,128)S(1)}, u32[]{:S(2)}, u32[]{:S(2)}) collective-permute-start(f32[16,2048]{1,0:T(8,128)S(1)} %pad_convert_fusion), channel_id=1, source_target_pairs={{15,1},{14,2},{13,3},{12,4},{11,5},{10,6},{9,7},{8,0},{31,17},{30,... | collective-permute-start | bytes 393224 | tf_op jit(solution)/shard_map/ppermute | solution.py:412
  159.9 6.8 %copy-start.11 = (f32[16,2048]{1,0:T(8,128)}, f32[16,2048]{1,0:T(8,128)S(1)}, u32[]{:S(2)}) copy-start(f32[16,2048]{1,0:T(8,128)S(1)} %collective-permute-done.1.edge_ref) | copy-start | bytes 393220
  182.5 36.2 %copy-start.2 = (bf16[2,256,256]{2,1,0:T(8,128)(2,1)S(1)}, bf16[2,256,256]{2,1,0:T(8,128)(2,1)}, u32[]{:S(2)}) copy-start(bf16[2,256,256]{2,1,0:T(8,128)(2,1)} %constant.33.clone.w0_ref) | copy-start | bytes 786436
  182.5 36.2 %copy-start.3 = (bf16[2,256,256]{2,1,0:T(8,128)(2,1)S(1)}, bf16[2,256,256]{2,1,0:T(8,128)(2,1)}, u32[]{:S(2)}) copy-start(bf16[2,256,256]{2,1,0:T(8,128)(2,1)} %constant.32.clone.wy_ref) | copy-start | bytes 786436
  182.5 36.2 %copy-start.4 = (f32[128,2048]{1,0:T(8,128)S(1)}, f32[128,2048]{1,0:T(8,128)}, u32[]{:S(2)}) copy-start(f32[128,2048]{1,0:T(8,128)} %bg_ref.1) | copy-start | bytes 3145732
  182.5 36.2 %copy-start.5 = (f32[128,2048]{1,0:T(8,128)S(1)}, f32[128,2048]{1,0:T(8,128)}, u32[]{:S(2)}) copy-start(f32[128,2048]{1,0:T(8,128)} %me_ref.1) | copy-start | bytes 3145732
  182.5 36.2 %copy-start.9 = (f32[16,2,128]{2,1,0:T(2,128)S(1)}, f32[16,2,128]{2,1,0:T(2,128)}, u32[]{:S(2)}) copy-start(f32[16,2,128]{2,1,0:T(2,128)} %constant.36.clone.turn_ref) | copy-start | bytes 49156
  218.7 32.8 %copy-start.1 = (f32[2,3,64,2048]{3,2,1,0:T(8,128)S(1)}, f32[2,3,64,2048]{3,2,1,0:T(8,128)}, u32[]{:S(2)}) copy-start(f32[2,3,64,2048]{3,2,1,0:T(8,128)} %get-tuple-element.12.a_ref) | copy-start | bytes 9437188
  218.7 32.8 %copy-start.6 = (bf16[2,256,256]{2,1,0:T(8,128)(2,1)S(1)}, bf16[2,256,256]{2,1,0:T(8,128)(2,1)}, u32[]{:S(2)}) copy-start(bf16[2,256,256]{2,1,0:T(8,128)(2,1)} %constant.35.clone.wxi_ref) | copy-start | bytes 786436
  218.7 32.8 %copy-start.7 = (bf16[2,256,256]{2,1,0:T(8,128)(2,1)S(1)}, bf16[2,256,256]{2,1,0:T(8,128)(2,1)}, u32[]{:S(2)}) copy-start(bf16[2,256,256]{2,1,0:T(8,128)(2,1)} %constant.34.clone.wx_ref) | copy-start | bytes 786436
  218.7 32.8 %copy-start.8 = (f32[2,8,2048]{2,1,0:T(8,128)S(1)}, f32[2,8,2048]{2,1,0:T(8,128)}, u32[]{:S(2)}) copy-start(f32[2,8,2048]{2,1,0:T(8,128)} %get-tuple-element.13.b_ref) | copy-start | bytes 393220
  255.8 74.7 %copy-start = (f32[3,128,2048]{2,1,0:T(8,128)S(1)}, f32[3,128,2048]{2,1,0:T(8,128)}, u32[]{:S(2)}) copy-start(f32[3,128,2048]{2,1,0:T(8,128)} %v_ref.2) | copy-start | bytes 9437188

commit v5 on v4

--- a/solution.py
+++ b/solution.py
@@ -295,22 +295,22 @@
         emit(t, table_data(w_0 if t == 0 else w_y, z[t]))
 
 
+def y_load(z, here, turn, groups, lanes):
+    zs = [(z[0, here, :lanes] * 2.0, None)]
+    for t in range(1, groups // 2):
+        re, im = z[t, here, :lanes], z[t, here, lanes:]
+        c, s = turn[t, 0:1, :], turn[t, 1:2, :]
+        zs.append((re * c + im * s, im * c - re * s))
+    zs.append((z[0, here, lanes:] * 2.0, None))
+    return zs
+
+
 def y_inverse(fetch, write, z, w_y, w_0, turn, groups, rows, lanes):
     for t in range(groups // 2):
         z[t] = data_table(fetch(t).T, w_0 if t == 0 else w_y)
-
-    def chunk(i, carry):
-        here = pl.ds(pl.multiple_of(i * SUB, SUB), SUB)
-        zs = [(z[0, here, :lanes] * 2.0, None)]
-        for t in range(1, groups // 2):
-            re, im = z[t, here, :lanes], z[t, here, lanes:]
-            c, s = turn[t, 0:1, :], turn[t, 1:2, :]
-            zs.append((re * c + im * s, im * c - re * s))
-        zs.append((z[0, here, lanes:] * 2.0, None))
-        write(i, here, c2r(zs))
-        return carry
-
-    lax.fori_loop(0, rows // SUB, chunk, 0)
+    for i in range(rows // SUB):
+        here = slice(i * SUB, (i + 1) * SUB)
+        write(here, c2r(y_load(z, here, turn, groups, lanes)))
 
 
 def x_radix(tile, z, base, turn, lanes, step):
@@ -398,9 +398,9 @@
                 grid=(1,),
                 in_specs=[whole(kept, rows),
                           pl.BlockSpec((1, 1, rows, length), lambda i, where, d=d: (where[0], d, 0, 0))],
-                out_specs=whole(kept, length),
+                out_specs=near,
             ),
-            out_shape=jax.ShapeDtypeStruct((kept, length), f32),
+            out_shape=pltpu.VMEM((kept, length), f32),
             name="pick",
         )(part.astype(jnp.int32).reshape(1), sel_send, psf_spectra)
         sends.append(send)
@@ -507,33 +507,53 @@
     arrived = swap(outgoing)
 
     block = groups * pair
-    x_scratch = lambda n: pltpu.VMEM((n * block, 2 * lanes), f32)
 
     small = groups * SUB
     lead = lambda: lax.broadcasted_iota(jnp.int32, (SUB, lanes), 0)
 
-    def project_kernel(wx_ref, wxi_ref, turn_ref, s_ref, a_ref, b_ref, o_ref, z, t_s, zc):
-        for d in range(depth):
-            for h in range(2):
-                j = pl.program_id(0) * 2 + h
-                tile = [(s_ref[s, d, j, 0], s_ref[s, d, j, 1]) for s in range(groups)]
-                x_radix(tile, z, d * block + h * SUB, turn_ref, lanes, pair)
-            zc[d * block:(d + 1) * block, :] = data_table(z[d * block:(d + 1) * block, :], wx_ref)
-        for t in range(groups):
-            here = slice(t * pair, (t + 1) * pair)
-            cols = slice(t * lanes, (t + 1) * lanes)
-            re = im = None
+    steps = tiles // 2
+
+    def per_step(n, count):
+        return pltpu.VMEM((count, n * block, 2 * lanes), f32)
+
+    def project_kernel(wx_any, wxi_any, turn_ref, s_ref, a_any, b_any, o_ref,
+                       wx_ref, wxi_ref, a_s, b_ref, z_s, t_all, zc_s, sems):
+        loads = [pltpu.make_async_copy(wx_any, wx_ref, sems.at[0])]
+        for step in range(steps):
+            mine_rows = pl.ds(step * pair, pair)
+            loads.append(pltpu.make_async_copy(a_any.at[:, :, mine_rows, :], a_s.at[step], sems.at[step + 1]))
+        loads.append(pltpu.make_async_copy(b_any, b_ref, sems.at[steps + 1]))
+        loads.append(pltpu.make_async_copy(wxi_any, wxi_ref, sems.at[steps + 2]))
+        for n in (0, 1, steps + 1, steps + 2, *range(2, steps + 1)):
+            loads[n].start()
+
+        def forward(step):
+            z, zc, t_s = z_s.at[step], zc_s.at[step], t_all.at[step]
             for d in range(depth):
-                at = slice(d * block + t * pair, d * block + (t + 1) * pair)
-                zr, zi = zc[at, :lanes], zc[at, lanes:]
-                kr, ki = a_ref[0, d, :, cols], a_ref[1, d, :, cols]
-                re = plus(re, zr * kr - zi * ki)
-                im = plus(im, zr * ki + zi * kr)
-            t_s[here, :lanes] = re
-            t_s[here, lanes:] = im
-
-        @pl.when(pl.program_id(0) == 0)
-        def _():
+                for h in range(2):
+                    j = step * 2 + h
+                    tile = [(s_ref[s, d, j, 0], s_ref[s, d, j, 1]) for s in range(groups)]
+                    x_radix(tile, z, d * block + h * SUB, turn_ref, lanes, pair)
+                if step == 0 and d == 0:
+                    loads[0].wait()
+                zc[d * block:(d + 1) * block, :] = data_table(z[d * block:(d + 1) * block, :], wx_ref)
+            loads[step + 1].wait()
+            for t in range(groups):
+                here = slice(t * pair, (t + 1) * pair)
+                cols = slice(t * lanes, (t + 1) * lanes)
+                re = im = None
+                for d in range(depth):
+                    at = slice(d * block + t * pair, d * block + (t + 1) * pair)
+                    zr, zi = zc[at, :lanes], zc[at, lanes:]
+                    kr, ki = a_s[step, 0, d, :, cols], a_s[step, 1, d, :, cols]
+                    re = plus(re, zr * kr - zi * ki)
+                    im = plus(im, zr * ki + zi * kr)
+                t_s[here, :lanes] = re
+                t_s[here, lanes:] = im
+
+        def packed():
+            z, zc, t_s = z_s.at[steps], zc_s.at[steps], t_all.at[0]
+
             def row(s, c):
                 out = s_ref[s, 0, 0, c, 0:1, :]
                 for d in range(1, depth):
@@ -542,6 +562,7 @@
 
             x_radix([(row(s, 0), -row(s, 1)) for s in range(groups)], z, 0, turn_ref, lanes, SUB)
             zc[:small, :] = data_table(z[:small, :], wx_ref)
+            loads[steps + 1].wait()
             for t in range(groups):
                 at = slice(t * SUB, (t + 1) * SUB)
                 cols = slice(t * lanes, (t + 1) * lanes)
@@ -551,32 +572,41 @@
                 t_s[top, :lanes] += jnp.sum(zr * kr - zi * ki, axis=0, keepdims=True)
                 t_s[top, lanes:] += jnp.sum(zr * ki + zi * kr, axis=0, keepdims=True)
 
-        zc[:block, :] = data_table(t_s[...], wxi_ref)
-
-        for h in range(2):
-            j = pl.program_id(0) * 2 + h
-            for s, (re, im) in enumerate(x_unradix(zc, h * SUB, turn_ref, groups, lanes, pair)):
-                o_ref[s, j, 0] = re
-                o_ref[s, j, 1] = im
-
-    k_specs = [pl.BlockSpec((2, depth, pair, length), lambda j: (0, 0, j, 0)), whole(2, SUB, length)]
+        def back(step):
+            zc = z_s.at[step]
+            zc[:block, :] = data_table(t_all[step], wxi_ref)
+            for h in range(2):
+                for s, (re, im) in enumerate(x_unradix(zc, h * SUB, turn_ref, groups, lanes, pair)):
+                    o_ref[s, step * 2 + h, 0] = re
+                    o_ref[s, step * 2 + h, 1] = im
+
+        for step in range(steps):
+            forward(step)
+            if step == 0:
+                packed()
+                loads[steps + 2].wait()
+            back(step)
+
+    hbm = pl.BlockSpec(memory_space=pl.ANY)
     outgoing = pl.pallas_call(
         project_kernel,
-        grid=(tiles // 2,),
-        in_specs=x_specs + [near] + k_specs,
+        in_specs=[hbm, hbm, whole(*turn.shape), near, hbm, hbm],
         out_specs=near,
         out_shape=pltpu.VMEM(send_shape, f32),
-        scratch_shapes=[x_scratch(depth), x_scratch(1), x_scratch(depth)],
-        compiler_params=pltpu.CompilerParams(vmem_limit_bytes=24 << 20),
+        scratch_shapes=[pltpu.VMEM(w_x.shape, bf), pltpu.VMEM(w_xi.shape, bf),
+                        pltpu.VMEM((steps, 2, depth, pair, length), f32), pltpu.VMEM((2, SUB, length), f32),
+                        per_step(depth, steps + 1), per_step(1, steps), per_step(depth, steps + 1),
+                        pltpu.SemaphoreType.DMA((steps + 3,))],
+        compiler_params=pltpu.CompilerParams(vmem_limit_bytes=36 << 20),
         name="project_x",
-    )(*(far(t) for t in x_tables), keep(arrived), far(a_all), far(b_all))
+    )(far(w_x), far(w_xi), turn, keep(arrived), far(a_all), far(b_all))
     arrived = swap(outgoing)
 
     def ratio_kernel(wy_ref, w0_ref, turn_ref, g_ref, bg_ref, me_ref, p_ref, o_ref, z):
         def fetch(t):
             return g_ref[:, t].reshape(groups * 2 * SUB, rows)
 
-        def write(i, here, outs):
+        def write(here, outs):
             ratio = []
             for a, value in enumerate(outs):
                 cols = slice(a * lanes, (a + 1) * lanes)
@@ -600,26 +630,27 @@
     )(*y_near, keep(arrived), keep(background), keep(measured))
     arrived = swap(outgoing)
 
-    def correct_kernel(wx_ref, wxi_ref, turn_ref, s_ref, a_ref, b_ref, o_ref, z, zq, zc, c_s):
-        mine_rows = pl.ds(pl.multiple_of(pl.program_id(0) * pair, pair), pair)
-
-        for h in range(2):
-            j = pl.program_id(0) * 2 + h
-            tile = [(s_ref[s, j, 0], s_ref[s, j, 1]) for s in range(groups)]
-            x_radix(tile, z, h * SUB, turn_ref, lanes, pair)
-        zq[...] = data_table(z[...], wx_ref)
-        for t in range(groups):
-            here = slice(t * pair, (t + 1) * pair)
-            cols = slice(t * lanes, (t + 1) * lanes)
-            zr, zi = zq[here, :lanes], zq[here, lanes:]
-            for d in range(depth):
-                at = slice(d * block + t * pair, d * block + (t + 1) * pair)
-                kr, ki = a_ref[0, d, mine_rows, cols], a_ref[1, d, mine_rows, cols]
-                c_s[at, :lanes] = zr * kr + zi * ki
-                c_s[at, lanes:] = zi * kr - zr * ki
-
-        @pl.when(pl.program_id(0) == 0)
-        def _():
+    def correct_kernel(wx_ref, wxi_ref, turn_ref, s_ref, a_ref, b_ref, o_ref, z_s, zq_s, zc_s, cs_s):
+        def forward(step):
+            z, zq, c_s = z_s.at[step], zq_s.at[step], cs_s.at[step]
+            for h in range(2):
+                j = step * 2 + h
+                tile = [(s_ref[s, j, 0], s_ref[s, j, 1]) for s in range(groups)]
+                x_radix(tile, z, h * SUB, turn_ref, lanes, pair)
+            zq[...] = data_table(z[...], wx_ref)
+            mine_rows = slice(step * pair, (step + 1) * pair)
+            for t in range(groups):
+                here = slice(t * pair, (t + 1) * pair)
+                cols = slice(t * lanes, (t + 1) * lanes)
+                zr, zi = zq[here, :lanes], zq[here, lanes:]
+                for d in range(depth):
+                    at = slice(d * block + t * pair, d * block + (t + 1) * pair)
+                    kr, ki = a_ref[0, d, mine_rows, cols], a_ref[1, d, mine_rows, cols]
+                    c_s[at, :lanes] = zr * kr + zi * ki
+                    c_s[at, lanes:] = zi * kr - zr * ki
+
+        def packed():
+            z, zq, c_s = z_s.at[steps], zq_s.at[steps], cs_s.at[0]
             tile = [(s_ref[s, 0, 0], -s_ref[s, 0, 1]) for s in range(groups)]
             x_radix(tile, z, 0, turn_ref, lanes, SUB)
             zq[:small, :] = data_table(z[:small, :], wx_ref)
@@ -634,45 +665,64 @@
                     c_s[top, :lanes] += re[d:d + 1, :]
                     c_s[top, lanes:] += im[d:d + 1, :]
 
-        for d in range(depth):
-            zc[d * block:(d + 1) * block, :] = data_table(c_s[d * block:(d + 1) * block, :], wxi_ref)
-            for h in range(2):
-                j = pl.program_id(0) * 2 + h
-                out = x_unradix(zc, d * block + h * SUB, turn_ref, groups, lanes, pair)
-                for s, (re, im) in enumerate(out):
-                    o_ref[s, d, j, 0] = re
-                    o_ref[s, d, j, 1] = im
+        def back(step):
+            zc, c_s = zc_s.at[step], cs_s.at[step]
+            for d in range(depth):
+                zc[d * block:(d + 1) * block, :] = data_table(c_s[d * block:(d + 1) * block, :], wxi_ref)
+                for h in range(2):
+                    out = x_unradix(zc, d * block + h * SUB, turn_ref, groups, lanes, pair)
+                    for s, (re, im) in enumerate(out):
+                        o_ref[s, d, step * 2 + h, 0] = re
+                        o_ref[s, d, step * 2 + h, 1] = im
+
+        for step in range(steps):
+            forward(step)
+            if step == 0:
+                packed()
+            back(step)
 
     outgoing = pl.pallas_call(
         correct_kernel,
-        grid=(tiles // 2,),
         in_specs=[near] * 6,
         out_specs=near,
         out_shape=pltpu.VMEM(many(depth), f32),
-        scratch_shapes=[x_scratch(1), x_scratch(1), x_scratch(depth), x_scratch(depth)],
-        compiler_params=pltpu.CompilerParams(vmem_limit_bytes=24 << 20),
+        scratch_shapes=[per_step(1, steps + 1), per_step(1, steps + 1), per_step(depth, steps), per_step(depth, steps)],
+        compiler_params=pltpu.CompilerParams(vmem_limit_bytes=32 << 20),
         name="correct_x",
     )(*x_near, keep(arrived), keep(a_all), keep(b_all))
     arrived = swap(outgoing)
 
-    def final_kernel(wy_ref, w0_ref, turn_ref, g_ref, v_ref, o_ref, z):
-        def fetch(t):
-            return g_ref[:, pl.program_id(0), t].reshape(groups * 2 * SUB, rows)
-
-        def write(i, here, outs):
-            for a, value in enumerate(outs):
-                cols = slice(a * lanes, (a + 1) * lanes)
-                o_ref[0, here, cols] = v_ref[pl.program_id(0), here, cols] * value
-
-        y_inverse(fetch, write, z, wy_ref, w0_ref, turn_ref, groups, rows, lanes)
+    def final_kernel(wy_ref, w0_ref, turn_ref, g_ref, v_ref, o_ref, z, out_s, sems):
+        def products(d):
+            for t in range(tiles):
+                spectrum = g_ref[:, d, t].reshape(groups * 2 * SUB, rows)
+                z[d % 2, t] = data_table(spectrum.T, w0_ref if t == 0 else wy_ref)
+
+        def lines(d, first, last):
+            for i in range(first, last):
+                here = slice(i * SUB, (i + 1) * SUB)
+                for a, value in enumerate(c2r(y_load(z.at[d % 2], here, turn_ref, groups, lanes))):
+                    cols = slice(a * lanes, (a + 1) * lanes)
+                    out_s[d, here, cols] = v_ref[d, here, cols] * value
+
+        copies = []
+        products(0)
+        for d in range(depth):
+            if d + 1 < depth:
+                products(d + 1)
+            lines(d, 0, rows // SUB)
+            copies.append(pltpu.make_async_copy(out_s.at[d], o_ref.at[d], sems.at[d]))
+            copies[d].start()
+        for copy in copies:
+            copy.wait()
 
     new_volume = pl.pallas_call(
         final_kernel,
-        grid=(depth,),
-        in_specs=[near] * 3 + [near, near],
-        out_specs=pl.BlockSpec((1, rows, length), lambda d: (d, 0, 0)),
-        out_shape=jax.ShapeDtypeStruct((depth, rows, length), f32),
-        scratch_shapes=[y_scratch],
+        in_specs=[near] * 5,
+        out_specs=pl.BlockSpec(memory_space=pl.ANY),
+        out_shape=pltpu.HBM((depth, rows, length), f32),
+        scratch_shapes=[pltpu.VMEM((2, tiles, rows, 2 * lanes), f32),
+                        pltpu.VMEM((depth, rows, length), f32), pltpu.SemaphoreType.DMA((depth,))],
         compiler_params=pltpu.CompilerParams(vmem_limit_bytes=16 << 20),
         name="final_y",
     )(*y_near, keep(arrived), keep(volume))

time: 337 us -> 332 us (0.985)
  Pallas kernels: 46.3 us -> 41.3 us
where the time goes in v5:
time: 332 us; the launch traced here: 330 us
  waiting for transfers between devices  140 us (42%)
  blocking collectives  134 us (40%)
  Pallas kernels  41.3 us (12%)
  starting transfers between devices  11.9 us (4%)
    all_to_all x3, blocking collectives, swap(): return lax.all_to_all(field, 'row', split_axis=0, concat_axis=0, tiled=True)  134 us
    ppermute x3, waiting for transfers between devices, fast_shards(): mine.append(lax.ppermute(send, 'row', flip))  129 us
    pallas_call x1, Pallas kernels, fast_shards(): pl.pallas_call(mix_kernel, grid=(groups // many_t,), in_specs=[smem, whol...  15.8 us
    pallas_call x1, Pallas kernels, fast_shards(): pl.pallas_call(project_kernel, in_specs=[hbm, hbm, whole(*turn.shape), ne...  6.84 us
    pallas_call x1, Pallas kernels, fast_shards(): pl.pallas_call(forward_kernel, grid=(depth,), in_specs=y_specs + [pl.Bloc...  6.65 us
  transfers between devices with their start and end apart: 8, of which 5 were waited for; matrix products, arithmetic and copies ran while one was open for 1% of the time, Pallas kernels for 8%

profile of v5, /device:TPU:15, one launch (start us, length us, event | category | flops | bytes accessed | tf_op | source)
XLA Modules:
  0.0 330.4 jit_solution(10488394863603071046)
XLA Ops:
  0.6 1.3 pick.4
  1.9 1.9 collective-permute-start
  3.8 1.3 pick.3
  5.1 6.7 %forward_y.1 = f32[16,3,8,2,8,128]{5,4,3,2,1,0:T(8,128)} custom-call(bf16[2,256,256]{2,1,0:T(8,128)(2,1)} %constant.32.clone.wy_ref, bf16[2,256,256]{2,1,0:T(8,128)(2,1)} %constant.33.clone.w0_ref, f32[16,2,128]{2,1,0:T(2,128)} %constant.36.clone.turn_ref, f32[3,128,2048]{2,1,0:T(8,128)} %v_ref.2), custom_call_target="tpu_custom_call" | custom-call | tf_op jit(solution)/shard_map/forward_y/pallas_call | solution.py:493
  11.7 16.9 %collective-permute-done.rest_0_ = f32[64,2048]{1,0:T(8,128)S(1)} collective-permute-done((f32[64,2048]{1,0:T(8,128)S(1)}, f32[64,2048]{1,0:T(8,128)S(1)}, u32[]{:S(2)}, u32[]{:S(2)}) %collective-permute-start) | collective-permute-done | bytes 524320 | tf_op jit(solution)/shard_map/ppermute | solution.py:407
  28.6 5.2 %all-to-all-start = ((f32[16,3,8,2,8,128]{5,4,3,2,1,0:T(8,128)}), f32[16,3,8,2,8,128]{5,4,3,2,1,0:T(8,128)}, u32[]{:S(2)}, u32[]{:S(2)}) async-start(f32[16,3,8,2,8,128]{5,4,3,2,1,0:T(8,128)} %forward_y.1), calls=%async_computation | async-start | bytes 6291456 | tf_op jit(solution)/shard_map/all_to_all | solution.py:504
  33.8 1.3 pick.5
  35.1 1.5 collective-permute-start.2
  36.6 1.2 collective-permute-start.3
  37.8 0.0 copy-done.10
  37.8 0.3 collective-permute-start.4
  38.1 101.6 %collective-permute-done.2.rest_1_ = f32[64,2048]{1,0:T(8,128)S(1)} collective-permute-done((f32[64,2048]{1,0:T(8,128)S(1)}, f32[64,2048]{1,0:T(8,128)S(1)}, u32[]{:S(2)}, u32[]{:S(2)}) %collective-permute-start.2) | collective-permute-done | bytes 524320 | tf_op jit(solution)/shard_map/ppermute | solution.py:407
  139.7 0.3 collective-permute-start.5
  140.0 10.1 %collective-permute-done.3.rest_2_ = f32[64,2048]{1,0:T(8,128)S(1)} collective-permute-done((f32[64,2048]{1,0:T(8,128)S(1)}, f32[64,2048]{1,0:T(8,128)S(1)}, u32[]{:S(2)}, u32[]{:S(2)}) %collective-permute-start.3) | collective-permute-done | bytes 524320 | tf_op jit(solution)/shard_map/ppermute | solution.py:407
  150.1 0.3 collective-permute-start.6
  150.3 1.1 slice_reduce_fusion
  151.4 1.3 collective-permute-start.1
  152.7 0.6 pad_add_fusion.where_ref
  153.4 4.7 %collective-permute-done.1.edge_ref = f32[16,2048]{1,0:T(8,128)S(1)} collective-permute-done((f32[16,2048]{1,0:T(8,128)S(1)}, f32[16,2048]{1,0:T(8,128)S(1)}, u32[]{:S(2)}, u32[]{:S(2)}) %collective-permute-start.1) | collective-permute-done | bytes 131104 | tf_op jit(solution)/shard_map/ppermute | solution.py:412
  158.1 0.0 collective-permute-done.4.rest_3_
  158.1 0.0 collective-permute-done.5.rest_4_
  158.1 0.0 copy-start.14
  158.1 6.6 %collective-permute-done.6.rest_5_ = f32[64,2048]{1,0:T(8,128)} collective-permute-done((f32[64,2048]{1,0:T(8,128)S(1)}, f32[64,2048]{1,0:T(8,128)}, u32[]{:S(2)}, u32[]{:S(2)}) %collective-permute-start.6) | collective-permute-done | bytes 524320 | tf_op jit(solution)/shard_map/ppermute | solution.py:414
  164.7 0.0 copy-done.11
  164.7 0.0 copy-done.12
  164.7 0.0 copy-done.15
  164.7 0.0 copy-done.13
  164.7 0.0 copy-done.14
  164.7 15.8 %mix.1 = (f32[2,3,64,2048]{3,2,1,0:T(8,128)}, f32[2,8,2048]{2,1,0:T(8,128)}) custom-call(s32[3]{0:T(128)} %pad_add_fusion.where_ref, f32[64,128]{1,0:T(8,128)} %constant.38.clone.own_l_ref, f32[64,128]{1,0:T(8,128)} %constant.39.clone.own_h_ref, bf16[2,3,128,2048]{3,2,1,0:T(8,128)(2,1)} %psf_ref.7, f32[16,2048]{1,0:T(8,128)} %copy-done.15, ...), custom_call_target="tpu_custom_call" | custom-call | tf_op jit(solution)/shard_map/mix/pallas_call | solution.py:470
  180.5 0.0 all-to-all-done.s_ref
  180.5 0.0 copy-done.9
  180.5 0.0 copy-start.2
  180.5 0.0 copy-start.3
  180.5 0.0 copy-start.4
  180.5 0.0 copy-start.5
  180.5 6.8 %project_x.1 = f32[16,8,2,8,128]{4,3,2,1,0:T(8,128)S(1)} custom-call(bf16[2,256,256]{2,1,0:T(8,128)(2,1)} %constant.34.clone.wx_any.wx_ref, bf16[2,256,256]{2,1,0:T(8,128)(2,1)} %constant.35.clone.wxi_any.wxi_ref, f32[16,2,128]{2,1,0:T(2,128)S(1)} %copy-done.9, f32[16,3,8,2,8,128]{5,4,3,2,1,0:T(8,128)} %all-to-all-done.s_ref, ...), custom_call_target="tpu_custom_call" | custom-call | tf_op jit(solution)/shard_map/project_x/pallas_call | solution.py:591
  187.4 30.2 %all_to_all.20.g_ref = f32[16,8,2,8,128]{4,3,2,1,0:T(8,128)S(1)} all-to-all(f32[16,8,2,8,128]{4,3,2,1,0:T(8,128)S(1)} %project_x.1), channel_id=1, replica_groups=mesh['vol'=2,'row'=16] {'row'}, dimensions={0} | all-to-all | bytes 2097152 | tf_op jit(solution)/shard_map/all_to_all | solution.py:504
  217.6 0.0 copy-done.2
  217.6 0.0 copy-done.3
  217.6 0.0 copy-start.6
  217.6 0.0 copy-start.7
  217.7 2.1 ratio.1
  219.7 29.5 %all_to_all.21.s_ref = f32[16,8,2,8,128]{4,3,2,1,0:T(8,128)S(1)} all-to-all(f32[16,8,2,8,128]{4,3,2,1,0:T(8,128)S(1)} %get-tuple-element.14), channel_id=1, replica_groups=mesh['vol'=2,'row'=16] {'row'}, dimensions={0} | all-to-all | bytes 2097152 | tf_op jit(solution)/shard_map/all_to_all | solution.py:504
  249.3 0.0 copy-done.6
  249.3 3.1 correct_x.1
  252.4 0.0 copy-start
  252.4 74.7 %all_to_all.22.g_ref = f32[16,3,8,2,8,128]{5,4,3,2,1,0:T(8,128)S(1)} all-to-all(f32[16,3,8,2,8,128]{5,4,3,2,1,0:T(8,128)S(1)} %correct_x.1), channel_id=1, replica_groups=mesh['vol'=2,'row'=16] {'row'}, dimensions={0} | all-to-all | bytes 6291456 | tf_op jit(solution)/shard_map/all_to_all | solution.py:504
  327.1 3.1 final_y.1
  (16 shorter events, 0.1 us)
Async XLA Ops:
  1.9 26.7 %collective-permute-start = (f32[64,2048]{1,0:T(8,128)S(1)}, f32[64,2048]{1,0:T(8,128)S(1)}, u32[]{:S(2)}, u32[]{:S(2)}) collective-permute-start(f32[64,2048]{1,0:T(8,128)S(1)} %pick.4), channel_id=1, source_target_pairs={{0,15},{1,14},{2,13},{3,12},{4,11},{5,10},{6,9},{7,8},{8,7},{9,6},... | collective-permute-start | bytes 1572872 | tf_op jit(solution)/shard_map/ppermute | solution.py:407
  28.6 9.2 %copy-start.10 = (f32[64,2048]{1,0:T(8,128)}, f32[64,2048]{1,0:T(8,128)S(1)}, u32[]{:S(2)}) copy-start(f32[64,2048]{1,0:T(8,128)S(1)} %collective-permute-done.rest_0_) | copy-start | bytes 1572868
  28.6 151.9 %all-to-all-start = ((f32[16,3,8,2,8,128]{5,4,3,2,1,0:T(8,128)}), f32[16,3,8,2,8,128]{5,4,3,2,1,0:T(8,128)}, u32[]{:S(2)}, u32[]{:S(2)}) async-start(f32[16,3,8,2,8,128]{5,4,3,2,1,0:T(8,128)} %forward_y.1), calls=%async_computation | async-start | bytes 6291456 | tf_op jit(solution)/shard_map/all_to_all | solution.py:504
  35.1 104.6 %collective-permute-start.2 = (f32[64,2048]{1,0:T(8,128)S(1)}, f32[64,2048]{1,0:T(8,128)S(1)}, u32[]{:S(2)}, u32[]{:S(2)}) collective-permute-start(f32[64,2048]{1,0:T(8,128)S(1)} %pick.5), channel_id=1, source_target_pairs={{0,15},{1,14},{2,13},{3,12},{4,11},{5,10},{6,9},{7,8},{8,7},{9,6},... | collective-permute-start | bytes 1572872 | tf_op jit(solution)/shard_map/ppermute | solution.py:407
  36.6 113.4 %collective-permute-start.3 = (f32[64,2048]{1,0:T(8,128)S(1)}, f32[64,2048]{1,0:T(8,128)S(1)}, u32[]{:S(2)}, u32[]{:S(2)}) collective-permute-start(f32[64,2048]{1,0:T(8,128)S(1)} %pick.3), channel_id=1, source_target_pairs={{0,15},{1,14},{2,13},{3,12},{4,11},{5,10},{6,9},{7,8},{8,7},{9,6},... | collective-permute-start | bytes 1572872 | tf_op jit(solution)/shard_map/ppermute | solution.py:407
  37.8 120.2 %collective-permute-start.4 = (f32[64,2048]{1,0:T(8,128)S(1)}, f32[64,2048]{1,0:T(8,128)S(1)}, u32[]{:S(2)}, u32[]{:S(2)}) collective-permute-start(f32[64,2048]{1,0:T(8,128)S(1)} %collective-permute-done.rest_0_), channel_id=1, source_target_pairs={{0,16},{16,0},{1,17},{17,1},{2,18},{18,2},{3,19},{19,3},{4,20},{20... | collective-permute-start | bytes 1572872 | tf_op jit(solution)/shard_map/ppermute | solution.py:414
  139.7 25.0 %copy-start.11 = (f32[64,2048]{1,0:T(8,128)}, f32[64,2048]{1,0:T(8,128)S(1)}, u32[]{:S(2)}) copy-start(f32[64,2048]{1,0:T(8,128)S(1)} %collective-permute-done.2.rest_1_) | copy-start | bytes 1572868
  139.7 18.4 %collective-permute-start.5 = (f32[64,2048]{1,0:T(8,128)S(1)}, f32[64,2048]{1,0:T(8,128)S(1)}, u32[]{:S(2)}, u32[]{:S(2)}) collective-permute-start(f32[64,2048]{1,0:T(8,128)S(1)} %collective-permute-done.2.rest_1_), channel_id=1, source_target_pairs={{0,16},{16,0},{1,17},{17,1},{2,18},{18,2},{3,19},{19,3},{4,20},{20... | collective-permute-start | bytes 1572872 | tf_op jit(solution)/shard_map/ppermute | solution.py:414
  150.1 14.6 %copy-start.12 = (f32[64,2048]{1,0:T(8,128)}, f32[64,2048]{1,0:T(8,128)S(1)}, u32[]{:S(2)}) copy-start(f32[64,2048]{1,0:T(8,128)S(1)} %collective-permute-done.3.rest_2_) | copy-start | bytes 1572868
  150.1 14.6 %collective-permute-start.6 = (f32[64,2048]{1,0:T(8,128)S(1)}, f32[64,2048]{1,0:T(8,128)}, u32[]{:S(2)}, u32[]{:S(2)}) collective-permute-start(f32[64,2048]{1,0:T(8,128)S(1)} %collective-permute-done.3.rest_2_), channel_id=1, source_target_pairs={{0,16},{16,0},{1,17},{17,1},{2,18},{18,2},{3,19},{19,3},{4,20},{20... | collective-permute-start | bytes 1572872 | tf_op jit(solution)/shard_map/ppermute | solution.py:414
  151.4 6.6 %collective-permute-start.1 = (f32[16,2048]{1,0:T(8,128)S(1)}, f32[16,2048]{1,0:T(8,128)S(1)}, u32[]{:S(2)}, u32[]{:S(2)}) collective-permute-start(f32[16,2048]{1,0:T(8,128)S(1)} %pad_convert_fusion), channel_id=1, source_target_pairs={{15,1},{14,2},{13,3},{12,4},{11,5},{10,6},{9,7},{8,0},{31,17},{30,... | collective-permute-start | bytes 393224 | tf_op jit(solution)/shard_map/ppermute | solution.py:412
  153.4 27.1 %copy-start.9 = (f32[16,2,128]{2,1,0:T(2,128)S(1)}, f32[16,2,128]{2,1,0:T(2,128)}, u32[]{:S(2)}) copy-start(f32[16,2,128]{2,1,0:T(2,128)} %constant.36.clone.turn_ref) | copy-start | bytes 49156
  158.1 6.6 %copy-start.15 = (f32[16,2048]{1,0:T(8,128)}, f32[16,2048]{1,0:T(8,128)S(1)}, u32[]{:S(2)}) copy-start(f32[16,2048]{1,0:T(8,128)S(1)} %collective-permute-done.1.edge_ref) | copy-start | bytes 393220
  158.1 6.6 %copy-start.13 = (f32[64,2048]{1,0:T(8,128)}, f32[64,2048]{1,0:T(8,128)S(1)}, u32[]{:S(2)}) copy-start(f32[64,2048]{1,0:T(8,128)S(1)} %collective-permute-done.4.rest_3_) | copy-start | bytes 1572868
  158.1 6.6 %copy-start.14 = (f32[64,2048]{1,0:T(8,128)}, f32[64,2048]{1,0:T(8,128)S(1)}, u32[]{:S(2)}) copy-start(f32[64,2048]{1,0:T(8,128)S(1)} %collective-permute-done.5.rest_4_) | copy-start | bytes 1572868
  180.5 37.1 %copy-start.2 = (bf16[2,256,256]{2,1,0:T(8,128)(2,1)S(1)}, bf16[2,256,256]{2,1,0:T(8,128)(2,1)}, u32[]{:S(2)}) copy-start(bf16[2,256,256]{2,1,0:T(8,128)(2,1)} %constant.33.clone.w0_ref) | copy-start | bytes 786436
  180.5 37.1 %copy-start.3 = (bf16[2,256,256]{2,1,0:T(8,128)(2,1)S(1)}, bf16[2,256,256]{2,1,0:T(8,128)(2,1)}, u32[]{:S(2)}) copy-start(bf16[2,256,256]{2,1,0:T(8,128)(2,1)} %constant.32.clone.wy_ref) | copy-start | bytes 786436
  180.5 37.1 %copy-start.4 = (f32[128,2048]{1,0:T(8,128)S(1)}, f32[128,2048]{1,0:T(8,128)}, u32[]{:S(2)}) copy-start(f32[128,2048]{1,0:T(8,128)} %bg_ref.1) | copy-start | bytes 3145732
  180.5 37.1 %copy-start.5 = (f32[128,2048]{1,0:T(8,128)S(1)}, f32[128,2048]{1,0:T(8,128)}, u32[]{:S(2)}) copy-start(f32[128,2048]{1,0:T(8,128)} %me_ref.1) | copy-start | bytes 3145732
  217.6 31.6 %copy-start.1 = (f32[2,3,64,2048]{3,2,1,0:T(8,128)S(1)}, f32[2,3,64,2048]{3,2,1,0:T(8,128)}, u32[]{:S(2)}) copy-start(f32[2,3,64,2048]{3,2,1,0:T(8,128)} %get-tuple-element.12.a_any.a_ref) | copy-start | bytes 9437188
  217.6 31.6 %copy-start.6 = (bf16[2,256,256]{2,1,0:T(8,128)(2,1)S(1)}, bf16[2,256,256]{2,1,0:T(8,128)(2,1)}, u32[]{:S(2)}) copy-start(bf16[2,256,256]{2,1,0:T(8,128)(2,1)} %constant.35.clone.wxi_any.wxi_ref) | copy-start | bytes 786436
  217.6 31.6 %copy-start.7 = (bf16[2,256,256]{2,1,0:T(8,128)(2,1)S(1)}, bf16[2,256,256]{2,1,0:T(8,128)(2,1)}, u32[]{:S(2)}) copy-start(bf16[2,256,256]{2,1,0:T(8,128)(2,1)} %constant.34.clone.wx_any.wx_ref) | copy-start | bytes 786436
  217.7 31.6 %copy-start.8 = (f32[2,8,2048]{2,1,0:T(8,128)S(1)}, f32[2,8,2048]{2,1,0:T(8,128)}, u32[]{:S(2)}) copy-start(f32[2,8,2048]{2,1,0:T(8,128)} %get-tuple-element.13.b_any.b_ref) | copy-start | bytes 393220
  252.4 74.7 %copy-start = (f32[3,128,2048]{2,1,0:T(8,128)S(1)}, f32[3,128,2048]{2,1,0:T(8,128)}, u32[]{:S(2)}) copy-start(f32[3,128,2048]{2,1,0:T(8,128)} %v_ref.2) | copy-start | bytes 9437188

commit v6 on v5

--- a/solution.py
+++ b/solution.py
@@ -580,11 +580,12 @@
                     o_ref[s, step * 2 + h, 0] = re
                     o_ref[s, step * 2 + h, 1] = im
 
+        forward(0)
+        packed()
+        loads[steps + 2].wait()
         for step in range(steps):
-            forward(step)
-            if step == 0:
-                packed()
-                loads[steps + 2].wait()
+            if step + 1 < steps:
+                forward(step + 1)
             back(step)
 
     hbm = pl.BlockSpec(memory_space=pl.ANY)
@@ -675,10 +676,11 @@
                         o_ref[s, d, step * 2 + h, 0] = re
                         o_ref[s, d, step * 2 + h, 1] = im
 
+        forward(0)
+        packed()
         for step in range(steps):
-            forward(step)
-            if step == 0:
-                packed()
+            if step + 1 < steps:
+                forward(step + 1)
             back(step)
 
     outgoing = pl.pallas_call(
@@ -693,10 +695,9 @@
     arrived = swap(outgoing)
 
     def final_kernel(wy_ref, w0_ref, turn_ref, g_ref, v_ref, o_ref, z, out_s, sems):
-        def products(d):
-            for t in range(tiles):
-                spectrum = g_ref[:, d, t].reshape(groups * 2 * SUB, rows)
-                z[d % 2, t] = data_table(spectrum.T, w0_ref if t == 0 else wy_ref)
+        def product(d, t):
+            spectrum = g_ref[:, d, t].reshape(groups * 2 * SUB, rows)
+            z[d % 2, t] = data_table(spectrum.T, w0_ref if t == 0 else wy_ref)
 
         def lines(d, first, last):
             for i in range(first, last):
@@ -706,11 +707,14 @@
                     out_s[d, here, cols] = v_ref[d, here, cols] * value
 
         copies = []
-        products(0)
+        share = rows // SUB // tiles
+        for t in range(tiles):
+            product(0, t)
         for d in range(depth):
-            if d + 1 < depth:
-                products(d + 1)
-            lines(d, 0, rows // SUB)
+            for t in range(tiles):
+                if d + 1 < depth:
+                    product(d + 1, t)
+                lines(d, t * share, (t + 1) * share)
             copies.append(pltpu.make_async_copy(out_s.at[d], o_ref.at[d], sems.at[d]))
             copies[d].start()
         for copy in copies:

time: 332 us -> 332 us (level)
  no operation moved by 1% of the time
where the time goes in v6:
time: 332 us; the launch traced here: 330 us
  waiting for transfers between devices  140 us (42%)
  blocking collectives  134 us (40%)
  Pallas kernels  40.9 us (12%)
  starting transfers between devices  11.9 us (4%)
    all_to_all x3, blocking collectives, swap(): return lax.all_to_all(field, 'row', split_axis=0, concat_axis=0, tiled=True)  134 us
    ppermute x3, waiting for transfers between devices, fast_shards(): mine.append(lax.ppermute(send, 'row', flip))  129 us
    pallas_call x1, Pallas kernels, fast_shards(): pl.pallas_call(mix_kernel, grid=(groups // many_t,), in_specs=[smem, whol...  15.8 us
    pallas_call x1, Pallas kernels, fast_shards(): pl.pallas_call(project_kernel, in_specs=[hbm, hbm, whole(*turn.shape), ne...  6.82 us
    pallas_call x1, Pallas kernels, fast_shards(): pl.pallas_call(forward_kernel, grid=(depth,), in_specs=y_specs + [pl.Bloc...  6.65 us
  transfers between devices with their start and end apart: 8, of which 5 were waited for; matrix products, arithmetic and copies ran while one was open for 1% of the time, Pallas kernels for 8%

profile of v6, /device:TPU:15, one launch (start us, length us, event | category | flops | bytes accessed | tf_op | source)
XLA Modules:
  0.0 329.9 jit_solution(1815946074545424378)
XLA Ops:
  0.6 1.3 pick.4
  1.9 1.9 collective-permute-start
  3.8 1.3 pick.3
  5.1 6.7 %forward_y.1 = f32[16,3,8,2,8,128]{5,4,3,2,1,0:T(8,128)} custom-call(bf16[2,256,256]{2,1,0:T(8,128)(2,1)} %constant.32.clone.wy_ref, bf16[2,256,256]{2,1,0:T(8,128)(2,1)} %constant.33.clone.w0_ref, f32[16,2,128]{2,1,0:T(2,128)} %constant.36.clone.turn_ref, f32[3,128,2048]{2,1,0:T(8,128)} %v_ref.2), custom_call_target="tpu_custom_call" | custom-call | tf_op jit(solution)/shard_map/forward_y/pallas_call | solution.py:493
  11.7 16.9 %collective-permute-done.rest_0_ = f32[64,2048]{1,0:T(8,128)S(1)} collective-permute-done((f32[64,2048]{1,0:T(8,128)S(1)}, f32[64,2048]{1,0:T(8,128)S(1)}, u32[]{:S(2)}, u32[]{:S(2)}) %collective-permute-start) | collective-permute-done | bytes 524320 | tf_op jit(solution)/shard_map/ppermute | solution.py:407
  28.6 5.2 %all-to-all-start = ((f32[16,3,8,2,8,128]{5,4,3,2,1,0:T(8,128)}), f32[16,3,8,2,8,128]{5,4,3,2,1,0:T(8,128)}, u32[]{:S(2)}, u32[]{:S(2)}) async-start(f32[16,3,8,2,8,128]{5,4,3,2,1,0:T(8,128)} %forward_y.1), calls=%async_computation | async-start | bytes 6291456 | tf_op jit(solution)/shard_map/all_to_all | solution.py:504
  33.8 1.3 pick.5
  35.1 1.5 collective-permute-start.2
  36.6 1.2 collective-permute-start.3
  37.8 0.0 copy-done.10
  37.8 0.3 collective-permute-start.4
  38.1 101.6 %collective-permute-done.2.rest_1_ = f32[64,2048]{1,0:T(8,128)S(1)} collective-permute-done((f32[64,2048]{1,0:T(8,128)S(1)}, f32[64,2048]{1,0:T(8,128)S(1)}, u32[]{:S(2)}, u32[]{:S(2)}) %collective-permute-start.2) | collective-permute-done | bytes 524320 | tf_op jit(solution)/shard_map/ppermute | solution.py:407
  139.7 0.3 collective-permute-start.5
  140.0 10.1 %collective-permute-done.3.rest_2_ = f32[64,2048]{1,0:T(8,128)S(1)} collective-permute-done((f32[64,2048]{1,0:T(8,128)S(1)}, f32[64,2048]{1,0:T(8,128)S(1)}, u32[]{:S(2)}, u32[]{:S(2)}) %collective-permute-start.3) | collective-permute-done | bytes 524320 | tf_op jit(solution)/shard_map/ppermute | solution.py:407
  150.1 0.3 collective-permute-start.6
  150.3 1.1 slice_reduce_fusion
  151.4 1.3 collective-permute-start.1
  152.7 0.6 pad_add_fusion.where_ref
  153.4 4.7 %collective-permute-done.1.edge_ref = f32[16,2048]{1,0:T(8,128)S(1)} collective-permute-done((f32[16,2048]{1,0:T(8,128)S(1)}, f32[16,2048]{1,0:T(8,128)S(1)}, u32[]{:S(2)}, u32[]{:S(2)}) %collective-permute-start.1) | collective-permute-done | bytes 131104 | tf_op jit(solution)/shard_map/ppermute | solution.py:412
  158.1 0.0 collective-permute-done.4.rest_3_
  158.1 0.0 collective-permute-done.5.rest_4_
  158.1 0.0 copy-start.14
  158.1 6.6 %collective-permute-done.6.rest_5_ = f32[64,2048]{1,0:T(8,128)} collective-permute-done((f32[64,2048]{1,0:T(8,128)S(1)}, f32[64,2048]{1,0:T(8,128)}, u32[]{:S(2)}, u32[]{:S(2)}) %collective-permute-start.6) | collective-permute-done | bytes 524320 | tf_op jit(solution)/shard_map/ppermute | solution.py:414
  164.7 0.0 copy-done.11
  164.7 0.0 copy-done.12
  164.7 0.0 copy-done.15
  164.7 0.0 copy-done.13
  164.7 0.0 copy-done.14
  164.7 15.8 %mix.1 = (f32[2,3,64,2048]{3,2,1,0:T(8,128)}, f32[2,8,2048]{2,1,0:T(8,128)}) custom-call(s32[3]{0:T(128)} %pad_add_fusion.where_ref, f32[64,128]{1,0:T(8,128)} %constant.38.clone.own_l_ref, f32[64,128]{1,0:T(8,128)} %constant.39.clone.own_h_ref, bf16[2,3,128,2048]{3,2,1,0:T(8,128)(2,1)} %psf_ref.7, f32[16,2048]{1,0:T(8,128)} %copy-done.15, ...), custom_call_target="tpu_custom_call" | custom-call | tf_op jit(solution)/shard_map/mix/pallas_call | solution.py:470
  180.5 0.0 all-to-all-done.s_ref
  180.5 0.0 copy-start.2
  180.5 0.0 copy-start.3
  180.5 0.0 copy-start.4
  180.5 0.0 copy-start.5
  180.5 6.8 %project_x.1 = f32[16,8,2,8,128]{4,3,2,1,0:T(8,128)S(1)} custom-call(bf16[2,256,256]{2,1,0:T(8,128)(2,1)} %constant.34.clone.wx_any.wx_ref, bf16[2,256,256]{2,1,0:T(8,128)(2,1)} %constant.35.clone.wxi_any.wxi_ref, f32[16,2,128]{2,1,0:T(2,128)S(1)} %copy-done.9, f32[16,3,8,2,8,128]{5,4,3,2,1,0:T(8,128)} %all-to-all-done.s_ref, ...), custom_call_target="tpu_custom_call" | custom-call | tf_op jit(solution)/shard_map/project_x/pallas_call | solution.py:592
  187.4 30.2 %all_to_all.20.g_ref = f32[16,8,2,8,128]{4,3,2,1,0:T(8,128)S(1)} all-to-all(f32[16,8,2,8,128]{4,3,2,1,0:T(8,128)S(1)} %project_x.1), channel_id=1, replica_groups=mesh['vol'=2,'row'=16] {'row'}, dimensions={0} | all-to-all | bytes 2097152 | tf_op jit(solution)/shard_map/all_to_all | solution.py:504
  217.6 0.0 copy-done.2
  217.6 0.0 copy-done.4
  217.6 0.0 copy-start.6
  217.6 0.0 copy-start.7
  217.6 2.1 ratio.1
  219.7 29.5 %all_to_all.21.s_ref = f32[16,8,2,8,128]{4,3,2,1,0:T(8,128)S(1)} all-to-all(f32[16,8,2,8,128]{4,3,2,1,0:T(8,128)S(1)} %get-tuple-element.14), channel_id=1, replica_groups=mesh['vol'=2,'row'=16] {'row'}, dimensions={0} | all-to-all | bytes 2097152 | tf_op jit(solution)/shard_map/all_to_all | solution.py:504
  249.2 0.0 copy-done.6
  249.3 2.7 correct_x.1
  252.0 0.0 copy-start
  252.0 74.7 %all_to_all.22.g_ref = f32[16,3,8,2,8,128]{5,4,3,2,1,0:T(8,128)S(1)} all-to-all(f32[16,3,8,2,8,128]{5,4,3,2,1,0:T(8,128)S(1)} %correct_x.1), channel_id=1, replica_groups=mesh['vol'=2,'row'=16] {'row'}, dimensions={0} | all-to-all | bytes 6291456 | tf_op jit(solution)/shard_map/all_to_all | solution.py:504
  326.7 0.0 copy-done
  326.7 3.1 final_y.1
  (16 shorter events, 0.1 us)
Async XLA Ops:
  1.9 26.7 %collective-permute-start = (f32[64,2048]{1,0:T(8,128)S(1)}, f32[64,2048]{1,0:T(8,128)S(1)}, u32[]{:S(2)}, u32[]{:S(2)}) collective-permute-start(f32[64,2048]{1,0:T(8,128)S(1)} %pick.4), channel_id=1, source_target_pairs={{0,15},{1,14},{2,13},{3,12},{4,11},{5,10},{6,9},{7,8},{8,7},{9,6},... | collective-permute-start | bytes 1572872 | tf_op jit(solution)/shard_map/ppermute | solution.py:407
  28.6 9.2 %copy-start.10 = (f32[64,2048]{1,0:T(8,128)}, f32[64,2048]{1,0:T(8,128)S(1)}, u32[]{:S(2)}) copy-start(f32[64,2048]{1,0:T(8,128)S(1)} %collective-permute-done.rest_0_) | copy-start | bytes 1572868
  28.6 151.9 %all-to-all-start = ((f32[16,3,8,2,8,128]{5,4,3,2,1,0:T(8,128)}), f32[16,3,8,2,8,128]{5,4,3,2,1,0:T(8,128)}, u32[]{:S(2)}, u32[]{:S(2)}) async-start(f32[16,3,8,2,8,128]{5,4,3,2,1,0:T(8,128)} %forward_y.1), calls=%async_computation | async-start | bytes 6291456 | tf_op jit(solution)/shard_map/all_to_all | solution.py:504
  35.1 104.6 %collective-permute-start.2 = (f32[64,2048]{1,0:T(8,128)S(1)}, f32[64,2048]{1,0:T(8,128)S(1)}, u32[]{:S(2)}, u32[]{:S(2)}) collective-permute-start(f32[64,2048]{1,0:T(8,128)S(1)} %pick.5), channel_id=1, source_target_pairs={{0,15},{1,14},{2,13},{3,12},{4,11},{5,10},{6,9},{7,8},{8,7},{9,6},... | collective-permute-start | bytes 1572872 | tf_op jit(solution)/shard_map/ppermute | solution.py:407
  36.6 113.4 %collective-permute-start.3 = (f32[64,2048]{1,0:T(8,128)S(1)}, f32[64,2048]{1,0:T(8,128)S(1)}, u32[]{:S(2)}, u32[]{:S(2)}) collective-permute-start(f32[64,2048]{1,0:T(8,128)S(1)} %pick.3), channel_id=1, source_target_pairs={{0,15},{1,14},{2,13},{3,12},{4,11},{5,10},{6,9},{7,8},{8,7},{9,6},... | collective-permute-start | bytes 1572872 | tf_op jit(solution)/shard_map/ppermute | solution.py:407
  37.8 120.2 %collective-permute-start.4 = (f32[64,2048]{1,0:T(8,128)S(1)}, f32[64,2048]{1,0:T(8,128)S(1)}, u32[]{:S(2)}, u32[]{:S(2)}) collective-permute-start(f32[64,2048]{1,0:T(8,128)S(1)} %collective-permute-done.rest_0_), channel_id=1, source_target_pairs={{0,16},{16,0},{1,17},{17,1},{2,18},{18,2},{3,19},{19,3},{4,20},{20... | collective-permute-start | bytes 1572872 | tf_op jit(solution)/shard_map/ppermute | solution.py:414
  139.7 25.0 %copy-start.11 = (f32[64,2048]{1,0:T(8,128)}, f32[64,2048]{1,0:T(8,128)S(1)}, u32[]{:S(2)}) copy-start(f32[64,2048]{1,0:T(8,128)S(1)} %collective-permute-done.2.rest_1_) | copy-start | bytes 1572868
  139.7 18.4 %collective-permute-start.5 = (f32[64,2048]{1,0:T(8,128)S(1)}, f32[64,2048]{1,0:T(8,128)S(1)}, u32[]{:S(2)}, u32[]{:S(2)}) collective-permute-start(f32[64,2048]{1,0:T(8,128)S(1)} %collective-permute-done.2.rest_1_), channel_id=1, source_target_pairs={{0,16},{16,0},{1,17},{17,1},{2,18},{18,2},{3,19},{19,3},{4,20},{20... | collective-permute-start | bytes 1572872 | tf_op jit(solution)/shard_map/ppermute | solution.py:414
  150.1 14.6 %copy-start.12 = (f32[64,2048]{1,0:T(8,128)}, f32[64,2048]{1,0:T(8,128)S(1)}, u32[]{:S(2)}) copy-start(f32[64,2048]{1,0:T(8,128)S(1)} %collective-permute-done.3.rest_2_) | copy-start | bytes 1572868
  150.1 14.6 %collective-permute-start.6 = (f32[64,2048]{1,0:T(8,128)S(1)}, f32[64,2048]{1,0:T(8,128)}, u32[]{:S(2)}, u32[]{:S(2)}) collective-permute-start(f32[64,2048]{1,0:T(8,128)S(1)} %collective-permute-done.3.rest_2_), channel_id=1, source_target_pairs={{0,16},{16,0},{1,17},{17,1},{2,18},{18,2},{3,19},{19,3},{4,20},{20... | collective-permute-start | bytes 1572872 | tf_op jit(solution)/shard_map/ppermute | solution.py:414
  151.4 6.6 %collective-permute-start.1 = (f32[16,2048]{1,0:T(8,128)S(1)}, f32[16,2048]{1,0:T(8,128)S(1)}, u32[]{:S(2)}, u32[]{:S(2)}) collective-permute-start(f32[16,2048]{1,0:T(8,128)S(1)} %pad_convert_fusion), channel_id=1, source_target_pairs={{15,1},{14,2},{13,3},{12,4},{11,5},{10,6},{9,7},{8,0},{31,17},{30,... | collective-permute-start | bytes 393224 | tf_op jit(solution)/shard_map/ppermute | solution.py:412
  153.4 27.1 %copy-start.9 = (f32[16,2,128]{2,1,0:T(2,128)S(1)}, f32[16,2,128]{2,1,0:T(2,128)}, u32[]{:S(2)}) copy-start(f32[16,2,128]{2,1,0:T(2,128)} %constant.36.clone.turn_ref) | copy-start | bytes 49156
  158.1 6.6 %copy-start.15 = (f32[16,2048]{1,0:T(8,128)}, f32[16,2048]{1,0:T(8,128)S(1)}, u32[]{:S(2)}) copy-start(f32[16,2048]{1,0:T(8,128)S(1)} %collective-permute-done.1.edge_ref) | copy-start | bytes 393220
  158.1 6.6 %copy-start.13 = (f32[64,2048]{1,0:T(8,128)}, f32[64,2048]{1,0:T(8,128)S(1)}, u32[]{:S(2)}) copy-start(f32[64,2048]{1,0:T(8,128)S(1)} %collective-permute-done.4.rest_3_) | copy-start | bytes 1572868
  158.1 6.6 %copy-start.14 = (f32[64,2048]{1,0:T(8,128)}, f32[64,2048]{1,0:T(8,128)S(1)}, u32[]{:S(2)}) copy-start(f32[64,2048]{1,0:T(8,128)S(1)} %collective-permute-done.5.rest_4_) | copy-start | bytes 1572868
  180.5 37.1 %copy-start.2 = (bf16[2,256,256]{2,1,0:T(8,128)(2,1)S(1)}, bf16[2,256,256]{2,1,0:T(8,128)(2,1)}, u32[]{:S(2)}) copy-start(bf16[2,256,256]{2,1,0:T(8,128)(2,1)} %constant.33.clone.w0_ref) | copy-start | bytes 786436
  180.5 37.1 %copy-start.3 = (bf16[2,256,256]{2,1,0:T(8,128)(2,1)S(1)}, bf16[2,256,256]{2,1,0:T(8,128)(2,1)}, u32[]{:S(2)}) copy-start(bf16[2,256,256]{2,1,0:T(8,128)(2,1)} %constant.32.clone.wy_ref) | copy-start | bytes 786436
  180.5 37.1 %copy-start.4 = (f32[128,2048]{1,0:T(8,128)S(1)}, f32[128,2048]{1,0:T(8,128)}, u32[]{:S(2)}) copy-start(f32[128,2048]{1,0:T(8,128)} %bg_ref.1) | copy-start | bytes 3145732
  180.5 37.1 %copy-start.5 = (f32[128,2048]{1,0:T(8,128)S(1)}, f32[128,2048]{1,0:T(8,128)}, u32[]{:S(2)}) copy-start(f32[128,2048]{1,0:T(8,128)} %me_ref.1) | copy-start | bytes 3145732
  217.6 31.6 %copy-start.1 = (f32[2,3,64,2048]{3,2,1,0:T(8,128)S(1)}, f32[2,3,64,2048]{3,2,1,0:T(8,128)}, u32[]{:S(2)}) copy-start(f32[2,3,64,2048]{3,2,1,0:T(8,128)} %get-tuple-element.12.a_any.a_ref) | copy-start | bytes 9437188
  217.6 31.6 %copy-start.6 = (bf16[2,256,256]{2,1,0:T(8,128)(2,1)S(1)}, bf16[2,256,256]{2,1,0:T(8,128)(2,1)}, u32[]{:S(2)}) copy-start(bf16[2,256,256]{2,1,0:T(8,128)(2,1)} %constant.35.clone.wxi_any.wxi_ref) | copy-start | bytes 786436
  217.6 31.6 %copy-start.7 = (bf16[2,256,256]{2,1,0:T(8,128)(2,1)S(1)}, bf16[2,256,256]{2,1,0:T(8,128)(2,1)}, u32[]{:S(2)}) copy-start(bf16[2,256,256]{2,1,0:T(8,128)(2,1)} %constant.34.clone.wx_any.wx_ref) | copy-start | bytes 786436
  217.6 31.6 %copy-start.8 = (f32[2,8,2048]{2,1,0:T(8,128)S(1)}, f32[2,8,2048]{2,1,0:T(8,128)}, u32[]{:S(2)}) copy-start(f32[2,8,2048]{2,1,0:T(8,128)} %get-tuple-element.13.b_any.b_ref) | copy-start | bytes 393220
  252.0 74.7 %copy-start = (f32[3,128,2048]{2,1,0:T(8,128)S(1)}, f32[3,128,2048]{2,1,0:T(8,128)}, u32[]{:S(2)}) copy-start(f32[3,128,2048]{2,1,0:T(8,128)} %v_ref.2) | copy-start | bytes 9437188
